TPU v7x, 128 devices: a whole 4x4x4 slice. The times are simulated.
128 devices in a mesh: row: 8 (over y, core), col: 16 (over z, x).
Axes of the slice: x: 4, y: 4, z: 4, core: 2. Of those that a mesh axis runs over, the one named last changes fastest.
Arguments:
- positions: float32 [3, 16384], P(None, 'col'), may hold values from 0 to 4
- modulus: float32 [16384], P('col'), may hold values from 0.5 to 2
- self_weight: float32 [128, 768], P('col'), may hold values from 1 to 4
- omega: float32 [128, 768, 256], P('col'), may hold values from -6 to 6
- psi: float32 [128, 768, 256], P('row'), may hold values from -6 to 6
- blocks: int32 [8, 16, 2, 2], P('row', 'col'), may hold values from -1 to 15, as said below
Outputs:
- row_basis: float32 [128, 768, 256], P('row', 'col')
- col_basis: float32 [128, 768, 256], P('col', 'row')
Inputs may be any that keep to these rules, and one draw needn't show every extreme that they name: `blocks`: on every device the valid slots come first and the rest hold -1 in both entries; valid pairs are distinct, a row entry below 16, a column entry below 8, and never a cluster paired with itself; each device has at least one valid slot and some device has all 2 slots valid.
All inputs are finite; a program needn't handle non-finite values.
Results may differ from a plain program's by a relative error of at most 0.0003.
Values sent between devices are 32-bit elements; how exact they have to be, the bound alone decides.
No kernel may reach another device: no remote copies, remote signals or barrier semaphores. Data moves between devices by JAX's collectives and lax.ppermute only.
A program may use at most 192 MiB of HBM per device.

v0:
```python
import jax
import jax.numpy as jnp
from jax import lax
from jax.sharding import PartitionSpec as P

COUPLE = 0.25
ROOT_TWO = 1.4142135623730951
HIGH = lax.Precision.HIGHEST
GROUP_SIZE = 2


def gather_turned(arrays, axis, dims):
    turned = [jnp.moveaxis(a, dim, 0) for a, dim in zip(arrays, dims)]
    widths = [t[0].size for t in turned]
    both = jnp.concatenate([t.reshape(-1, w) for t, w in zip(turned, widths)], axis=1)
    filled = lax.all_gather(both, axis, axis=0, tiled=True)
    pieces = jnp.split(filled, [sum(widths[:k]) for k in range(1, len(widths))], axis=1)
    return tuple(
        (
            jnp.moveaxis(b.reshape(-1, *t.shape[1:]), 0, dim)
            for b, t, dim in zip(pieces, turned, dims)
        )
    )


def cut_along(shard, dim, size):
    before, after = (shard.shape[:dim], shard.shape[dim + 1 :])
    return jnp.moveaxis(shard.reshape(*before, size, -1, *after), dim, 0)


def summed_on_arrival(shard, axis, dim):
    pieces = cut_along(shard, dim, lax.axis_size(axis))
    arrived = lax.all_to_all(pieces, axis, split_axis=0, concat_axis=0, tiled=True)
    return arrived.sum(axis=0)


def make_tiles(row_points, row_scale, col_points, col_scale):
    offsets = row_points[:, :, :, None] - col_points[:, :, None, :]
    spread = jnp.sum(offsets * offsets, axis=1) + 1.0
    inverse = lax.rsqrt(spread)
    normal = offsets * inverse[:, None]
    weight_ab = COUPLE * inverse * inverse * inverse * row_scale[:, :, None] * col_scale[:, None, :]
    comp_x = normal[:, 0]
    comp_y = normal[:, 1]
    comp_z = normal[:, 2]
    voigt = jnp.stack(
        [
            comp_x * comp_x,
            comp_y * comp_y,
            comp_z * comp_z,
            ROOT_TWO * comp_y * comp_z,
            ROOT_TWO * comp_x * comp_z,
            ROOT_TWO * comp_x * comp_y,
        ],
        axis=1,
    )
    trace_vec = jnp.array([1.0, 1.0, 1.0, 0.0, 0.0, 0.0], dtype=voigt.dtype)
    identity = jnp.eye(6, dtype=voigt.dtype)
    voigt_row = voigt[:, :, :, None, :]
    voigt_col = jnp.transpose(voigt, (0, 2, 1, 3))[:, None]
    angular = (
        identity[None, :, None, :, None]
        + voigt_row * trace_vec[None, None, None, :, None]
        + trace_vec[None, :, None, None, None] * voigt_col
        - 5.0 * voigt_row * voigt_col
    )
    result = angular * weight_ab[:, None, :, None, :]
    zones_per = row_points.shape[2]
    return result.reshape(result.shape[0], 6 * zones_per, 6 * zones_per)


def gram_of(sketch):
    return jnp.einsum("kxs,kxt->kst", sketch, sketch, precision=HIGH)


def apply_factor(gram, sketch):
    factor = jnp.linalg.cholesky(gram)
    return lax.linalg.triangular_solve(
        factor, sketch, left_side=False, lower=True, transpose_a=True
    )


def per_device(positions, modulus, self_weight, omega, psi, blocks):
    col_clusters = omega.shape[0]
    row_clusters = psi.shape[0]
    zones_per = positions.shape[1] // col_clusters
    height = omega.shape[1]
    width = omega.shape[2]
    all_points, all_scales = gather_turned((positions, modulus), "col", (1, 0))
    row_index = lax.axis_index("row")
    col_index = lax.axis_index("col")
    row_points = lax.dynamic_slice_in_dim(
        all_points, row_index * row_clusters * zones_per, row_clusters * zones_per, 1
    ).reshape(3, row_clusters, zones_per)
    row_scales = lax.dynamic_slice_in_dim(
        all_scales, row_index * row_clusters * zones_per, row_clusters * zones_per, 0
    ).reshape(row_clusters, zones_per)
    col_points = positions.reshape(3, col_clusters, zones_per)
    col_scales = modulus.reshape(col_clusters, zones_per)
    on_diagonal = col_index * col_clusters // row_clusters == row_index
    offset_rows = jnp.clip(
        col_index * col_clusters - row_index * row_clusters, 0, row_clusters - col_clusters
    )
    own_rows = jnp.where(on_diagonal, self_weight[:, :, None] * omega, 0.0)
    row_sketch = lax.dynamic_update_slice_in_dim(
        jnp.zeros((row_clusters, height, width), jnp.float32), own_rows, offset_rows, 0
    )
    psi_local = lax.dynamic_slice_in_dim(psi, offset_rows, col_clusters, 0)
    col_sketch = jnp.where(on_diagonal, self_weight[:, :, None] * psi_local, 0.0)
    pair_list = blocks.reshape(-1, 2)
    slot_total = pair_list.shape[0]
    padded_count = (slot_total + GROUP_SIZE - 1) // GROUP_SIZE * GROUP_SIZE
    pair_list = jnp.concatenate(
        [pair_list, jnp.full((padded_count - slot_total, 2), -1, jnp.int32)], axis=0
    )
    live_count = jnp.sum((pair_list[:, 0] >= 0).astype(jnp.int32))
    group_count = (live_count + GROUP_SIZE - 1) // GROUP_SIZE

    def step(group_index, state):
        sketch_rows, sketch_cols = state
        live = (pair_list[:, 0] >= 0).astype(jnp.float32)
        row_ids = jnp.maximum(pair_list[:, 0], 0)
        col_ids = jnp.maximum(pair_list[:, 1], 0)
        left_points = jnp.transpose(row_points[:, row_ids], (1, 0, 2))
        right_points = jnp.transpose(col_points[:, col_ids], (1, 0, 2))
        blocks_now = (
            make_tiles(left_points, row_scales[row_ids], right_points, col_scales[col_ids])
            * live[:, None, None]
        )
        row_terms = jnp.einsum("kxy,kys->kxs", blocks_now, omega[col_ids], precision=HIGH)
        col_terms = jnp.einsum("kxy,kxs->kys", blocks_now, psi[row_ids], precision=HIGH)
        for member in range(GROUP_SIZE):
            sketch_rows = sketch_rows.at[row_ids[member]].add(row_terms[member])
            sketch_cols = sketch_cols.at[col_ids[member]].add(col_terms[member])
        return (sketch_rows, sketch_cols)

    row_sketch, col_sketch = lax.fori_loop(0, group_count, step, (row_sketch, col_sketch))
    owned_rows = lax.psum_scatter(row_sketch, "col", scatter_dimension=0, tiled=True)
    owned_cols = summed_on_arrival(col_sketch, "row", 0)
    finished_rows = apply_factor(gram_of(owned_rows), owned_rows)
    finished_cols = apply_factor(gram_of(owned_cols), owned_cols)
    row_basis = lax.all_to_all(finished_rows, "col", split_axis=1, concat_axis=0, tiled=True)
    col_basis = lax.all_to_all(finished_cols, "row", split_axis=1, concat_axis=0, tiled=True)
    return (row_basis, col_basis)


def solution(mesh):
    placed = (
        P(None, "col"),
        P("col"),
        P("col", None),
        P("col", None, None),
        P("row", None, None),
        P("row", "col", None, None),
    )
    return jax.shard_map(
        per_device,
        mesh=mesh,
        in_specs=placed,
        out_specs=(P("row", "col", None), P("col", "row", None)),
        check_vma=False,
    )
```

profile of v0, /device:TPU:0, one launch (start us, length us, event | category | flops | bytes accessed | tf_op | source)
XLA Modules:
  0.0 429.5 jit_solution(9127594609795652947)
XLA Ops:
  7.2 1.5 fusion.25
  16.8 25.2 %all_gather.3 = f32[16384,4]{0,1:T(4,128)S(1)} all-gather(f32[1024,4]{0,1:T(4,128)S(1)} %pad_maximum_fusion.2), channel_id=1, replica_groups=mesh['row'=8,'col'=16] {'col'}, dimensions={0}, use_global_device_ids=true | all-gather | bytes 278528 | tf_op jit(solution)/shard_map/all_gather | solution.py:16
  43.2 1.3 gather_fusion.1
  46.9 3.2 mul.274
  50.1 6.9 %mul.275 = f32[2,768,768]{2,1,0:T(8,128)} reshape(f32[2,6,128,6,128]{4,3,2,1,0:T(8,128)} %mul.274) | data formatting | bytes 9437184 | tf_op jit(solution)/shard_map/while/body/mul | solution.py:64
  57.0 3.1 mul.278
  60.1 6.9 %mul.279 = f32[2,768,768]{2,1,0:T(8,128)} reshape(f32[2,6,128,6,128]{4,3,2,1,0:T(8,128)} %mul.278) | data formatting | bytes 9437184 | tf_op jit(solution)/shard_map/while/body/mul | solution.py:65
  67.0 3.1 mul.267
  70.1 6.9 %mul.268 = f32[2,768,768]{2,1,0:T(8,128)} reshape(f32[2,6,128,6,128]{4,3,2,1,0:T(8,128)} %mul.267) | data formatting | bytes 9437184 | tf_op jit(solution)/shard_map/while/body/mul | solution.py:63
  77.0 3.2 mul.288
  80.2 6.9 %mul.289 = f32[2,768,768]{2,1,0:T(8,128)} reshape(f32[2,6,128,6,128]{4,3,2,1,0:T(8,128)} %mul.288) | data formatting | bytes 9437184 | tf_op jit(solution)/shard_map/while/body/mul | solution.py:67
  88.0 6.4 %gather_fusion.5 = f32[2,768,256]{2,1,0:T(8,128)} fusion(f32[16,768,256]{2,1,0:T(8,128)} %param.24, s32[1024]{0:T(1024)S(1)} %get-tuple-element.310), kind=kCustom, calls=%fused_computation.5 | custom fusion | bytes 3145736 | tf_op jit(solution)/shard_map/while/body/gather | solution.py:131
  94.4 4.6 %gather_fusion.4 = f32[2,768,256]{2,1,0:T(8,128)} fusion(f32[8,768,256]{2,1,0:T(8,128)} %param.23, s32[1024]{0:T(1024)S(1)} %get-tuple-element.309), kind=kCustom, calls=%fused_computation.4 | custom fusion | bytes 3145736 | tf_op jit(solution)/shard_map/while/body/gather | solution.py:130
  99.0 7.6 %multiply_multiply_fusion = f32[2,768,768]{2,1,0:T(8,128)S(1)} fusion(f32[2,768,768]{2,1,0:T(8,128)} %mul.289, f32[2,768,768]{2,1,0:T(8,128)} %mul.279, f32[2,768,768]{2,1,0:T(8,128)} %mul.275, f32[2,768,768]{2,1,0:T(8,128)} %mul.268, f32[2]{0:T(128)S(1)} %convert_reduce_fusion, f32[768]{0:T(1024)S(1)} %broadcast_bitcast_fusion, f32[768,768]{1,0:T(8,128)S(1)} %bitcast.185), kind=kLoop, calls=%fused_computation.22 | loop fusion | flops 9437184 | bytes 25955336 | tf_op jit(solution)/shard_map/while/body/mul | solution.py:127
  106.7 7.8 %fusion.34 = f32[2,768,256]{2,1,0:T(8,128)S(1)} fusion(f32[2,768,768]{2,1,0:T(8,128)S(1)} %multiply_multiply_fusion, f32[2,768,256]{2,1,0:T(8,128)S(1)} %copy-done.1), kind=kOutput, calls=%fused_computation.131 | convolution fusion | flops 3623878656 | bytes 7864320 | tf_op jit(solution)/shard_map/while/body/kxy,kxs->kys/dot_general | solution.py:131
  114.4 4.2 fusion.33
  122.3 7.5 %multiply_select_fusion = (f32[8,768,256]{2,1,0:T(8,128)}, f32[16,768,256]{2,1,0:T(8,128)S(1)}) fusion(f32[16,768,256]{2,1,0:T(8,128)} %param.24, s32[]{:T(128)S(6)} %min.4, f32[8,768]{1,0:T(8,128)S(1)} %copy-done.4, pred[]{:T(512)S(6)} %eq.12, f32[16,768,256]{2,1,0:T(8,128)S(1)} %broadcast_in_dim.7, f32[8,768,256]{2,1,0:T(8,128)} %param.23), kind=kLoop, calls=%fused_computation.20 | loop fusion | flops 6291456 | bytes 25190404 | tf_op jit(solution)/shard_map/jit(_where)/select_n | solution.py:109
  130.9 3.5 copy-done
  134.4 18.0 %while.22 = (s32[]{:T(128)}, f32[16,768,256]{2,1,0:T(8,128)}, f32[8,768,256]{2,1,0:T(8,128)}, s32[]{:T(128)}, pred[]{:T(512)}, /*index=5*/s32[2,2]{1,0:T(2,128)S...) while((s32[]{:T(128)}, f32[16,768,256]{2,1,0:T(8,128)}, ...), condition=%wide.region_7.8_spmd, body=%wide.region_6.7_spmd.sunk | while | flops 1572882 | bytes 9439589 | solution.py:137
  139.3 4.0 fusion.59
  145.0 2.8 fusion.60
  149.6 2.7 fusion.61
  152.4 5.2 %all-to-all-start.1 = ((f32[8,1,768,256]{3,2,1,0:T(8,128)}), f32[8,1,768,256]{3,2,1,0:T(8,128)}, u32[]{:S(2)}, u32[]{:S(2)}) async-start(f32[8,1,768,256]{3,2,1,0:T(8,128)} %bitcast.181), calls=%async_computation.1 | async-start | bytes 12582912 | tf_op jit(solution)/shard_map/all_to_all | solution.py:33
  158.2 71.1 %all-to-all-done.1 = f32[8,1,768,256]{3,2,1,0:T(8,128)} async-done(((f32[8,1,768,256]{3,2,1,0:T(8,128)}), f32[8,1,768,256]{3,2,1,0:T(8,128)}, u32[]{:S(2)}, u32[]{:S(2)}) %all-to-all-start.1) | async-done | bytes 6291488 | tf_op jit(solution)/shard_map/all_to_all | solution.py:33
  229.3 3.4 reduce_sum.33
  232.7 1.4 fusion.35
  234.3 11.7 %custom-call.21 = f32[1,128,128]{2,1,0:T(8,128)S(1)} custom-call(f32[1,128,128]{2,1,0:T(8,128)S(1)} %cholesky.194), custom_call_target="Cholesky" | custom-call | tf_op jit(solution)/shard_map/jit(cholesky)/cholesky | solution.py:77
  246.1 9.8 %custom-call.22 = f32[1,1,128,128]{2,3,1,0:T(8,128)S(1)} custom-call(f32[1,1,128,128]{3,2,1,0:T(8,128)S(1)} %get-tuple-element.290), custom_call_target="InvertDiagBlocksLowerTriangular" | custom-call | tf_op jit(solution)/shard_map/jit(cholesky)/cholesky | solution.py:77
  256.4 11.9 %custom-call.23 = f32[1,128,128]{2,1,0:T(8,128)S(1)} custom-call(f32[1,128,128]{2,1,0:T(8,128)S(1)} %fusion.9), custom_call_target="Cholesky" | custom-call | tf_op jit(solution)/shard_map/jit(cholesky)/cholesky | solution.py:77
  270.8 3.8 while.24
  273.4 1.3 bitcast_dynamic-update-slice_fusion.7
  274.7 19.7 %custom-call.24 = f32[1,2,128,128]{2,3,1,0:T(8,128)S(1)} custom-call(f32[1,2,128,128]{3,2,1,0:T(8,128)S(1)} %bitcast.198), custom_call_target="InvertDiagBlocksLowerTriangular" | custom-call | tf_op jit(solution)/shard_map/triangular_solve/custom-call.0 | solution.py:78
  296.3 1.7 copy.35
  298.0 3.6 all-to-all-start.2
  301.6 29.6 %all-reduce.4.cloned.1.call-done = f32[16,768,256]{2,1,0:T(8,128)} async-done(((f32[16,768,256]{2,1,0:T(8,128)}), f32[16,768,256]{2,1,0:T(8,128)}) %all-reduce.4.cloned.1.call-update) | async-done | bytes 12582928
  331.1 3.4 fusion.10
  334.8 11.7 %custom-call.17 = f32[1,128,128]{2,1,0:T(8,128)S(1)} custom-call(f32[1,128,128]{2,1,0:T(8,128)S(1)} %cholesky.191), custom_call_target="Cholesky" | custom-call | tf_op jit(solution)/shard_map/jit(cholesky)/cholesky | solution.py:77
  346.5 9.8 %custom-call.18 = f32[1,1,128,128]{2,3,1,0:T(8,128)S(1)} custom-call(f32[1,1,128,128]{3,2,1,0:T(8,128)S(1)} %get-tuple-element.294), custom_call_target="InvertDiagBlocksLowerTriangular" | custom-call | tf_op jit(solution)/shard_map/jit(cholesky)/cholesky | solution.py:77
  356.8 11.7 %custom-call.19 = f32[1,128,128]{2,1,0:T(8,128)S(1)} custom-call(f32[1,128,128]{2,1,0:T(8,128)S(1)} %fusion.8), custom_call_target="Cholesky" | custom-call | tf_op jit(solution)/shard_map/jit(cholesky)/cholesky | solution.py:77
  371.3 4.0 while.23
  371.9 1.4 bitcast_dynamic-update-slice_fusion.6
  373.9 1.4 bitcast_dynamic-update-slice_fusion.6
  375.3 19.9 %custom-call.20 = f32[1,2,128,128]{2,3,1,0:T(8,128)S(1)} custom-call(f32[1,2,128,128]{3,2,1,0:T(8,128)S(1)} %bitcast.197), custom_call_target="InvertDiagBlocksLowerTriangular" | custom-call | tf_op jit(solution)/shard_map/triangular_solve/custom-call.0 | solution.py:78
  395.2 2.1 fusion.13
  397.4 2.4 fusion.5
  400.4 1.7 copy.32
  402.1 5.2 %all-to-all-start = ((f32[1,768,256]{2,0,1:T(1,128)}), f32[1,768,256]{2,0,1:T(1,128)S(1)}, u32[]{:S(2)}, u32[]{:S(2)}) async-start(f32[1,768,256]{2,0,1:T(1,128)} %copy.32), calls=%async_computation | async-start | bytes 1572864 | tf_op jit(solution)/shard_map/all_to_all | solution.py:142
  408.2 13.3 %all-to-all-done = f32[1,768,256]{2,0,1:T(1,128)S(1)} async-done(((f32[1,768,256]{2,0,1:T(1,128)}), f32[1,768,256]{2,0,1:T(1,128)S(1)}, u32[]{:S(2)}, u32[]{:S(2)}) %all-to-all-start) | async-done | bytes 786464 | tf_op jit(solution)/shard_map/all_to_all | solution.py:142
  (95 shorter events, 23.4 us)
Async XLA Ops:
  7.2 324.0 %all-reduce.4.cloned.1.call-start = ((), (), s32[]{:S(2)}) async-start(), calls=%async_computation.3 | async-start | bytes 25165824
  87.1 0.8 copy-start.5
  99.0 7.6 %copy-start.1 = (f32[2,768,256]{2,1,0:T(8,128)S(1)}, f32[2,768,256]{2,1,0:T(8,128)}, u32[]{:S(2)}) copy-start(f32[2,768,256]{2,1,0:T(8,128)} %gather_fusion.5) | copy-start | bytes 4718596
  106.6 7.8 %copy-start.2 = (f32[2,768,256]{2,1,0:T(8,128)S(1)}, f32[2,768,256]{2,1,0:T(8,128)}, u32[]{:S(2)}) copy-start(f32[2,768,256]{2,1,0:T(8,128)} %gather_fusion.4) | copy-start | bytes 4718596
  121.1 1.2 copy-start.4
  122.3 7.6 %copy-start.6 = (s32[3]{0:T(128)S(1)}, s32[3]{0:T(128)}, u32[]{:S(2)}) copy-start(s32[3]{0:T(128)} %constant.256.clone.1) | copy-start | bytes 40
  122.3 7.6 %copy-start.7 = (s32[3]{0:T(128)S(1)}, s32[3]{0:T(128)}, u32[]{:S(2)}) copy-start(s32[3]{0:T(128)} %constant.258.clone.1) | copy-start | bytes 40
  122.3 12.0 %copy-start.3 = (s32[1,1,2,2]{3,2,1,0:T(2,128)S(1)}, s32[1,1,2,2]{3,2,1,0:T(2,128)}, u32[]{:S(2)}) copy-start(s32[1,1,2,2]{3,2,1,0:T(2,128)} %param.25) | copy-start | bytes 52
  129.9 4.5 %copy-start = (f32[16,768,256]{2,1,0:T(8,128)}, f32[16,768,256]{2,1,0:T(8,128)S(1)}, u32[]{:S(2)}) copy-start(f32[16,768,256]{2,1,0:T(8,128)S(1)} %get-tuple-element.454) | copy-start | bytes 37748740
  152.4 5.2 %copy-start.8 = (u32[128]{0:T(128)S(1)}, u32[128]{0:T(128)}, u32[]{:S(2)}) copy-start(u32[128]{0:T(128)} %constant.288) | copy-start | bytes 1540
  152.4 76.9 %all-to-all-start.1 = ((f32[8,1,768,256]{3,2,1,0:T(8,128)}), f32[8,1,768,256]{3,2,1,0:T(8,128)}, u32[]{:S(2)}, u32[]{:S(2)}) async-start(f32[8,1,768,256]{3,2,1,0:T(8,128)} %bitcast.181), calls=%async_computation.1 | async-start | bytes 12582912 | tf_op jit(solution)/shard_map/all_to_all | solution.py:33
  298.0 104.1 %all-to-all-start.2 = ((f32[1,768,256]{2,0,1:T(1,128)}), f32[1,768,256]{2,0,1:T(1,128)S(1)}, u32[]{:S(2)}, u32[]{:S(2)}) async-start(f32[1,768,256]{2,0,1:T(1,128)} %copy.35), calls=%async_computation.2 | async-start | bytes 1572864 | tf_op jit(solution)/shard_map/all_to_all | solution.py:143
  402.1 19.4 %all-to-all-start = ((f32[1,768,256]{2,0,1:T(1,128)}), f32[1,768,256]{2,0,1:T(1,128)S(1)}, u32[]{:S(2)}, u32[]{:S(2)}) async-start(f32[1,768,256]{2,0,1:T(1,128)} %copy.32), calls=%async_computation | async-start | bytes 1572864 | tf_op jit(solution)/shard_map/all_to_all | solution.py:142
Sparse Core Ops, SparseCore 0:
  152.5 178.6 all-reduce.3
where the time goes:
time: 437 us; the launch traced here: 430 us
  other arithmetic  142 us (32%)
  waiting for transfers between devices  114 us (26%)
  local copies, waits for them, and re-layouts  77.3 us (18%)
  blocking collectives  25.2 us (6%)
  between operations  25.2 us (6%)
  matrix products  24.6 us (6%)
  starting transfers between devices  14 us (3%)
  loops' own time  7.41 us (2%)
    all_to_all x1, waiting for transfers between devices, summed_on_arrival(): lax.all_to_all(pieces, axis, split_axis=0, concat_axis=0, tiled=True)  71.1 us
    another operation x14, other arithmetic, apply_factor(): factor = jnp.linalg.cholesky(gram)  69.4 us
    another operation x7, other arithmetic, apply_factor(): lax.linalg.triangular_solve(factor, sketch, left_side=False, lower=True,...  39.7 us
    unnamed x2, waiting for transfers between devices  29.6 us
    all_gather x1, blocking collectives, gather_turned(): filled = lax.all_gather(both, axis, axis=0, tiled=True)  25.2 us
    all_to_all x1, waiting for transfers between devices, per_device(): lax.all_to_all(finished_rows, 'col', split_axis=1, concat_axis=0, tiled=T...  13.3 us
    another operation x17, local copies, waits for them, and re-layouts, apply_factor(): lax.linalg.triangular_solve(factor, sketch, left_side=False, lower=True,...  11.3 us
    mul x2, local copies, waits for them, and re-layouts, make_tiles(): trace_vec[None, :, None, None, None] * voigt_col  10.1 us
  transfers between devices with their start and end apart: 4, of which 3 were waited for; matrix products, arithmetic and copies ran while one was open for 32% of the time, Pallas kernels for 0%

commit v1 on v0

v1 whole, which is shorter than its diff:
```python
import functools
import jax
import jax.numpy as jnp
from jax import lax
from jax.experimental import pallas as pl
from jax.experimental.pallas import tpu as pltpu
from jax.sharding import PartitionSpec as P

COUPLE = 0.25
ROOT_TWO = 1.4142135623730951
HIGH = lax.Precision.HIGHEST
ZC = 128
HEIGHT = 768
SK = 256
NR = 8
NC = 16
ROW_CL = 16
COL_CL = 8
SLOTS = 2
ROW_CUT = HEIGHT // NC
COL_CUT = HEIGHT // NR
TAG = 8
BOTH = ("row", "col")
F32 = jnp.float32
BF16 = jnp.bfloat16


def device(y, core, z, x):
    return (2 * y + core) * NC + 4 * z + x


def point_routes():
    near, far = [], []
    for y in range(4):
        for core in range(2):
            for z in range(4):
                for x in range(4):
                    away = (x // 2) ^ core
                    bit = x % 2
                    target = device(y, core, z, x)
                    first = 2 * core + (bit ^ away)
                    second = 2 * core + (1 ^ bit ^ away)
                    src_y = (z + 2) % 4
                    near.append((device(src_y, away, y, first), target))
                    far.append((device(src_y, away, y, second), target))
    return near, far


def omega_route():
    route = []
    for y in range(4):
        for core in range(2):
            for z in range(4):
                for x in range(4):
                    src = device((2 * (z % 2) + x // 2 + y) % 4, x % 2, y, 2 * core + z // 2)
                    route.append((src, device(y, core, z, x)))
    return route


def psi_route():
    route = []
    for y in range(4):
        for core in range(2):
            for z in range(4):
                for x in range(4):
                    src = device(z, x // 2, (y + z) % 4, 2 * core + x % 2)
                    route.append((src, device(y, core, z, x)))
    return route


def split(value):
    high = value.astype(BF16)
    return high, (value - high.astype(F32)).astype(BF16)


def pair_kernel(meta, own_pts, near_pts, far_pts, src, out, high_t, low_t, high_w, low_w, buf, left, sem, *, cut, turned):
    pieces = HEIGHT // cut
    for slot in range(SLOTS):

        @pl.when(meta[slot, 0] >= 0)
        def _(slot=slot):
            row_id = meta[slot, 0]
            col_id = meta[slot, 1]
            pick = row_id if turned else col_id
            copy = pltpu.make_async_copy(src.at[pick], buf, sem)
            copy.start()
            row_half = row_id // COL_CL
            row_k = row_id % COL_CL
            from_near = row_half == meta[SLOTS, 0]

            def row_line(c):
                a = near_pts[c, pl.ds(row_k, 1), :]
                b = far_pts[c, pl.ds(row_k, 1), :]
                return jnp.where(from_near, a, b)

            rows = [row_line(c) for c in range(4)]
            cols = [own_pts[c, pl.ds(col_id, 1), :] for c in range(4)]
            down, across = (cols, rows) if turned else (rows, cols)
            for c in range(4):
                left[c] = jnp.transpose(jnp.broadcast_to(down[c], (ZC, ZC)))

            def chunk(step, carry):
                at = pl.multiple_of(step * 16, 16)
                wide = [jnp.broadcast_to(v, (16, ZC)) for v in across]
                tall = [left[c, pl.ds(at, 16), :] for c in range(4)]
                dx = tall[0] - wide[0]
                dy = tall[1] - wide[1]
                dz = tall[2] - wide[2]
                inv = lax.rsqrt(dx * dx + dy * dy + dz * dz + 1.0)
                w = (COUPLE * (inv * inv * inv)) * (tall[3] * wide[3])
                nx, ny, nz = dx * inv, dy * inv, dz * inv
                u = [
                    nx * nx,
                    ny * ny,
                    nz * nz,
                    ROOT_TWO * (ny * nz),
                    ROOT_TWO * (nx * nz),
                    ROOT_TWO * (nx * ny),
                ]
                v = [w * t for t in u]
                v5 = [5.0 * t for t in v]
                for p in range(6):
                    for q in range(p, 6):
                        m = -(v5[p] * u[q])
                        if q < 3:
                            m = m + (v[p] + v[q])
                        elif p < 3:
                            m = m + v[q]
                        if p == q:
                            m = m + w
                        hi, lo = split(m)
                        high_t[pl.ds(p * ZC + at, 16), q * ZC : (q + 1) * ZC] = hi
                        low_t[pl.ds(p * ZC + at, 16), q * ZC : (q + 1) * ZC] = lo
                        if p != q:
                            high_t[pl.ds(q * ZC + at, 16), p * ZC : (p + 1) * ZC] = hi
                            low_t[pl.ds(q * ZC + at, 16), p * ZC : (p + 1) * ZC] = lo
                return carry

            lax.fori_loop(0, ZC // 16, chunk, 0)
            copy.wait()
            hi, lo = split(buf[...])
            high_w[...] = hi
            low_w[...] = lo
            step_rows = cut * 2
            for g in range(HEIGHT // step_rows):
                part = pl.ds(g * step_rows, step_rows)
                acc = jnp.dot(high_t[part, :], high_w[...], preferred_element_type=F32)
                acc += jnp.dot(high_t[part, :], low_w[...], preferred_element_type=F32)
                acc += jnp.dot(low_t[part, :], high_w[...], preferred_element_type=F32)
                out[2 * g, slot * cut : (slot + 1) * cut, :] = acc[:cut]
                out[2 * g + 1, slot * cut : (slot + 1) * cut, :] = acc[cut:]

        tag = jnp.full((1, 1, SK), meta[slot, 1 if turned else 0].astype(F32))
        out[:, SLOTS * cut + slot * (TAG // SLOTS) : SLOTS * cut + (slot + 1) * (TAG // SLOTS), :] = (
            jnp.broadcast_to(tag, (pieces, TAG // SLOTS, SK))
        )


def pair_terms(meta, own_pts, near_pts, far_pts, src, cut, turned):
    pieces = HEIGHT // cut
    vmem = pl.BlockSpec(memory_space=pltpu.VMEM)
    return pl.pallas_call(
        functools.partial(pair_kernel, cut=cut, turned=turned),
        out_shape=jax.ShapeDtypeStruct((pieces, SLOTS * cut + TAG, SK), F32),
        in_specs=[pl.BlockSpec(memory_space=pltpu.SMEM), vmem, vmem, vmem, pl.BlockSpec(memory_space=pl.ANY)],
        out_specs=vmem,
        scratch_shapes=[
            pltpu.VMEM((HEIGHT, HEIGHT), BF16),
            pltpu.VMEM((HEIGHT, HEIGHT), BF16),
            pltpu.VMEM((HEIGHT, SK), BF16),
            pltpu.VMEM((HEIGHT, SK), BF16),
            pltpu.VMEM((HEIGHT, SK), F32),
            pltpu.VMEM((4, ZC, ZC), F32),
            pltpu.SemaphoreType.DMA,
        ],
        compiler_params=pltpu.CompilerParams(vmem_limit_bytes=24 << 20),
        cost_estimate=pl.CostEstimate(flops=2_000_000_000, bytes_accessed=4_000_000, transcendentals=32768),
        name="pair_cols" if turned else "pair_rows",
    )(meta, own_pts, near_pts, far_pts, src)


def add_kernel(ids, arrived, out, *, cut):
    out[...] = jnp.zeros_like(out)
    for k in range(arrived.shape[0]):
        for slot in range(SLOTS):

            @pl.when(ids[k, slot] >= 0)
            def _(k=k, slot=slot):
                out[ids[k, slot]] += arrived[k, slot * cut : (slot + 1) * cut, :]


def add_arrived(arrived, clusters, cut):
    ids = arrived[:, SLOTS * cut :: TAG // SLOTS, 0].astype(jnp.int32)
    vmem = pl.BlockSpec(memory_space=pltpu.VMEM)
    return pl.pallas_call(
        functools.partial(add_kernel, cut=cut),
        out_shape=jax.ShapeDtypeStruct((clusters, cut, SK), F32),
        in_specs=[pl.BlockSpec(memory_space=pltpu.SMEM), vmem],
        out_specs=vmem,
        compiler_params=pltpu.CompilerParams(vmem_limit_bytes=16 << 20),
        cost_estimate=pl.CostEstimate(flops=1_000_000, bytes_accessed=3_000_000, transcendentals=0),
        name="add_arrived",
    )(ids, arrived)


BLK = 64


def factor_inverse(diag):
    sub = lax.broadcasted_iota(jnp.int32, (8, 128), 0)
    lane = lax.broadcasted_iota(jnp.int32, (8, 128), 1)
    body = jnp.concatenate([diag, diag], axis=1)
    groups = []
    for g in range(BLK // 8):
        eye = jnp.where(lane == sub + 8 * g, 1.0, 0.0).astype(F32)
        groups.append(jnp.where(lane < BLK, eye, body[8 * g : 8 * g + 8]))
    done = []
    for kb in range(BLK // 8):
        at = BLK + 8 * kb
        spread = {
            g: [jnp.broadcast_to(groups[g][:, at + t : at + t + 1], (8, 128)) for t in range(8)]
            for g in range(kb, BLK // 8)
        }
        rows = [jnp.broadcast_to(groups[kb][t : t + 1, :], (8, 128)) for t in range(8)]
        e = [[jnp.broadcast_to(spread[kb][t][s : s + 1, :], (8, 128)) if s >= t else None for t in range(8)] for s in range(8)]
        final = jnp.zeros((8, 128), F32)
        for t in range(8):
            root = lax.rsqrt(e[t][t])
            inv = 1.0 / e[t][t]
            final = jnp.where(sub == t, rows[t] * root, final)
            scaled = rows[t] * inv
            for s in range(t + 1, 8):
                m = e[s][t] * inv
                for u in range(t + 1, s + 1):
                    e[s][u] = e[s][u] - m * e[u][t]
                rows[s] = rows[s] - e[s][t] * scaled
                for g in range(kb + 1, BLK // 8):
                    spread[g][s] = spread[g][s] - spread[g][t] * m
            for g in range(kb + 1, BLK // 8):
                groups[g] = groups[g] - spread[g][t] * scaled
        done.append(final)
    return jnp.concatenate(done, axis=0)[:, :BLK]


def basis_kernel(rows, self_rows, cols, self_cols, out_rows, out_cols, sk, gram, inverse):
    n = SK // BLK
    dims0 = (((0,), (0,)), ((), ()))
    for w, (got, own) in enumerate(((rows, self_rows), (cols, self_cols))):
        sk[w] = got[...] + own[...]
        gram[w] = lax.dot_general(sk[w], sk[w], dims0, precision=HIGH, preferred_element_type=F32)
        inverse[w] = jnp.zeros((SK, SK), F32)
    for k in range(n):
        here = slice(k * BLK, (k + 1) * BLK)
        low = [factor_inverse(gram[w, here, here]) for w in range(2)]
        for w in range(2):
            if k:
                inverse[w, here, : k * BLK] = jnp.dot(
                    low[w], inverse[w, here, : k * BLK], precision=HIGH, preferred_element_type=F32
                )
            inverse[w, here, here] = low[w]
            if k < n - 1:
                rest = slice((k + 1) * BLK, SK)
                upper = jnp.dot(low[w], gram[w, here, rest], precision=HIGH, preferred_element_type=F32)
                gram[w, rest, rest] = gram[w, rest, rest] - lax.dot_general(
                    upper, upper, dims0, precision=HIGH, preferred_element_type=F32
                )
                inverse[w, rest, : (k + 1) * BLK] = inverse[w, rest, : (k + 1) * BLK] - lax.dot_general(
                    upper, inverse[w, here, : (k + 1) * BLK], dims0, precision=HIGH, preferred_element_type=F32
                )
    for w, out in enumerate((out_rows, out_cols)):
        out[...] = lax.dot_general(
            sk[w], inverse[w], (((1,), (1,)), ((), ())), precision=HIGH, preferred_element_type=F32
        )


def bases(rows, self_rows, cols, self_cols):
    shape = jax.ShapeDtypeStruct((HEIGHT, SK), F32)
    vmem = pl.BlockSpec(memory_space=pltpu.VMEM)
    return pl.pallas_call(
        basis_kernel,
        out_shape=(shape, shape),
        in_specs=[vmem] * 4,
        out_specs=(vmem, vmem),
        scratch_shapes=[
            pltpu.VMEM((2, HEIGHT, SK), F32),
            pltpu.VMEM((2, SK, SK), F32),
            pltpu.VMEM((2, SK, SK), F32),
        ],
        compiler_params=pltpu.CompilerParams(vmem_limit_bytes=32 << 20),
        cost_estimate=pl.CostEstimate(flops=3_000_000_000, bytes_accessed=5_000_000, transcendentals=0),
        name="bases",
    )(rows, self_rows, cols, self_cols)


def trade(value, axis):
    return lax.all_to_all(value, axis, split_axis=0, concat_axis=0, tiled=True)


def per_device(positions, modulus, self_weight, omega, psi, blocks):
    row_at = lax.axis_index("row")
    col_at = lax.axis_index("col")
    near_route, far_route = point_routes()

    points = jnp.concatenate([positions, modulus[None]], axis=0).reshape(4, COL_CL, ZC)
    near_pts = lax.ppermute(points, BOTH, near_route)
    far_pts = lax.ppermute(points, BOTH, far_route)

    src_y, src_core, src_z, src_x = row_at // 2, row_at % 2, col_at // 4, col_at % 4
    bits = (src_y - src_z) % 4
    omega_pick = (bits // 2) * 4 + (bits % 2) * 2 + src_core
    omega_send = omega[omega_pick] * self_weight[omega_pick][:, None]
    psi_pick = (src_x % 2) * 8 + ((src_z - src_y) % 4) * 2 + src_x // 2
    psi_send = psi[psi_pick]
    omega_send, psi_send, near_pts, far_pts = lax.optimization_barrier((omega_send, psi_send, near_pts, far_pts))
    self_rows = lax.ppermute(omega_send, BOTH, omega_route())
    psi_here = lax.ppermute(psi_send, BOTH, psi_route())
    self_cols = psi_here * self_weight[row_at][:, None]

    pairs = blocks.reshape(SLOTS, 2)
    core = row_at % 2
    away = ((col_at % 4) // 2) ^ core
    near_half = (col_at % 2) ^ away
    meta = jnp.concatenate([pairs, jnp.stack([near_half, near_half])[None]], axis=0).astype(jnp.int32)

    row_terms = pair_terms(meta, points, near_pts, far_pts, omega, ROW_CUT, False)
    col_terms = pair_terms(meta, points, near_pts, far_pts, psi, COL_CUT, True)

    row_sum = add_arrived(trade(row_terms, "col"), ROW_CL, ROW_CUT)
    col_sum = add_arrived(trade(col_terms, "row"), COL_CL, COL_CUT)
    rows = trade(row_sum, "col").reshape(HEIGHT, SK)
    cols = trade(col_sum, "row").reshape(HEIGHT, SK)
    row_q, col_q = bases(rows, self_rows, cols, self_cols)
    row_basis = trade(row_q.reshape(NC, ROW_CUT, SK), "col")
    col_basis = trade(col_q.reshape(NR, COL_CUT, SK), "row")
    return (row_basis, col_basis)


def solution(mesh):
    placed = (
        P(None, "col"),
        P("col"),
        P("col", None),
        P("col", None, None),
        P("row", None, None),
        P("row", "col", None, None),
    )
    return jax.shard_map(
        per_device,
        mesh=mesh,
        in_specs=placed,
        out_specs=(P("row", "col", None), P("col", "row", None)),
        check_vma=False,
    )
```

time: 437 us -> 214 us (0.49); the launches traced: 430 us -> 213 us
  other arithmetic: 142 us -> 4.95 us
  local copies, waits for them, and re-layouts: 77.3 us -> 14 us
  waiting for transfers between devices: 114 us -> 53 us
  starting transfers between devices: 14 us -> 63.6 us
  Pallas kernels: 0 us -> 30.1 us
  matrix products: 24.6 us -> 0 us
  between operations: 25.2 us -> 0.76 us
  blocking collectives: 25.2 us -> 46.7 us
  loops' own time: 7.41 us -> 0 us
    another operation x23 -> x0, other arithmetic: 110 us -> none  [the longest x14 69.4 us: apply_factor(): factor = jnp.linalg.cholesky(gram)]
    all_to_all x0 -> x2, blocking collectives: none -> 46.7 us  [trade(): return lax.all_to_all(value, axis, split_axis=0, concat_axis=0, tiled=True)]
    mul x9 -> x0, local copies, waits for them, and re-layouts: 40.3 us -> none  [the longest x2 10.1 us: make_tiles(): trace_vec[None, :, None, None, None] * voigt_col]
    all_to_all x3 -> x4, starting transfers between devices: 13.9 us -> 46.3 us  [trade(): return lax.all_to_all(value, axis, split_axis=0, concat_axis=0, tiled=True)]
    all_to_all x3 -> x4, waiting for transfers between devices: 84.4 us -> 53 us  [trade(): return lax.all_to_all(value, axis, split_axis=0, concat_axis=0, tiled=True)]
    pallas_call x0 -> x5, Pallas kernels: none -> 30.1 us  [the longest x1 19.1 us: bases(): pl.pallas_call(basis_kernel, out_shape=(shape, shape), in_specs=[vmem] *...]
    unnamed x2 -> x0, waiting for transfers between devices: 29.6 us -> none
    all_gather x1 -> x0, blocking collectives: 25.2 us -> none  [gather_turned(): filled = lax.all_gather(both, axis, axis=0, tiled=True)]
  transfers between devices with their start and end apart: 4 -> 8, of which waited for: 3 -> 4; matrix products, arithmetic and copies ran while one was open for 32% -> 4% of each run, Pallas kernels for 0% -> 3%
where the time goes in v1:
time: 214 us; the launch traced here: 213 us
  starting transfers between devices  63.6 us (30%)
  waiting for transfers between devices  53 us (25%)
  blocking collectives  46.7 us (22%)
  Pallas kernels  30.1 us (14%)
  local copies, waits for them, and re-layouts  14 us (7%)
  other arithmetic  4.95 us (2%)
    all_to_all x4, waiting for transfers between devices, trade(): return lax.all_to_all(value, axis, split_axis=0, concat_axis=0, tiled=True)  53 us
    all_to_all x2, blocking collectives, trade(): return lax.all_to_all(value, axis, split_axis=0, concat_axis=0, tiled=True)  46.7 us
    all_to_all x4, starting transfers between devices, trade(): return lax.all_to_all(value, axis, split_axis=0, concat_axis=0, tiled=True)  46.3 us
    pallas_call x1, Pallas kernels, bases(): pl.pallas_call(basis_kernel, out_shape=(shape, shape), in_specs=[vmem] *...  19.1 us
    unnamed x9, local copies, waits for them, and re-layouts  10.7 us
    pallas_call x2, Pallas kernels, pair_terms(): pl.pallas_call(functools.partial(pair_kernel, cut=cut, turned=turned), ou...  8.17 us
    ppermute x1, starting transfers between devices, per_device(): psi_here = lax.ppermute(psi_send, BOTH, psi_route())  7.42 us
  transfers between devices with their start and end apart: 8, of which 4 were waited for; matrix products, arithmetic and copies ran while one was open for 4% of the time, Pallas kernels for 3%

profile of v1, /device:TPU:0, one launch (start us, length us, event | category | flops | bytes accessed | tf_op | source)
XLA Modules:
  0.0 213.1 jit_solution(17500428951356046866)
XLA Ops:
  0.6 0.7 copy.18
  1.3 0.7 pad_maximum_fusion.own_pts
  2.0 4.0 %collective-permute-start = (f32[4,8,128]{2,1,0:T(8,128)S(1)}, f32[4,8,128]{2,1,0:T(8,128)S(1)}, u32[]{:S(2)}, u32[]{:S(2)}) collective-permute-start(f32[4,8,128]{2,1,0:T(8,128)S(1)} %pad_maximum_fusion.own_pts), channel_id=1, source_target_pairs={{64,0},{65,1},{81,2},{80,3},{96,4},{97,5},{113,6},{112,7},{0,8},{1... | collective-permute-start | bytes 49160 | tf_op jit(solution)/shard_map/ppermute | solution.py:305
  6.0 4.1 %collective-permute-start.1 = (f32[4,8,128]{2,1,0:T(8,128)S(1)}, f32[4,8,128]{2,1,0:T(8,128)S(1)}, u32[]{:S(2)}, u32[]{:S(2)}) collective-permute-start(f32[4,8,128]{2,1,0:T(8,128)S(1)} %pad_maximum_fusion.own_pts), channel_id=1, source_target_pairs={{65,0},{64,1},{80,2},{81,3},{97,4},{96,5},{112,6},{113,7},{1,8},{0... | collective-permute-start | bytes 49160 | tf_op jit(solution)/shard_map/ppermute | solution.py:306
  10.1 0.1 add_bitcast_fusion
  10.2 0.8 dynamic-slice_reduce_fusion
  11.1 2.2 %bitcast_multiply_fusion = f32[768,256]{1,0:T(8,128)} fusion(f32[8,768,256]{2,1,0:T(8,128)} %src.2, s32[]{:T(128)S(6)} %select_n.68, f32[768]{0:T(1024)S(1)} %get-tuple-element.15), kind=kLoop, calls=%fused_computation | loop fusion | flops 196608 | bytes 1575940 | tf_op jit(solution)/shard_map/mul | solution.py:311
  13.2 2.1 dynamic-slice_bitcast_fusion
  15.3 0.7 pad_add_fusion.meta
  16.0 0.0 collective-permute-done.near_pts
  16.0 0.0 collective-permute-done.1.far_pts
  16.0 0.0 copy-start
  16.0 4.6 %copy-done = f32[16,768,256]{2,1,0:T(8,128)S(1)} copy-done((f32[16,768,256]{2,1,0:T(8,128)S(1)}, f32[16,768,256]{2,1,0:T(8,128)}, u32[]{:S(2)}) %copy-start) | copy-done | bytes 12582936
  20.6 3.8 %pair_cols.1 = f32[8,200,256]{2,1,0:T(8,128)} custom-call(s32[3,2]{1,0:T(4,128)S(1)} %pad_add_fusion.meta, f32[4,8,128]{2,1,0:T(8,128)S(1)} %pad_maximum_fusion.own_pts, f32[4,8,128]{2,1,0:T(8,128)S(1)} %collective-permute-done.near_pts, f32[4,8,128]{2,1,0:T(8,128)S(1)} %collective-permute-done.1.far_pts, f32[16,768,256]{2,1,0:T(8,128)S(1)} %copy-done), custom_call_target="tpu_custom_call" | custom-call | flops 2000000000 | bytes 4000000 | tf_op jit(solution)/shard_map/pair_cols/pallas_call | solution.py:162
  24.4 5.3 %all-to-all-start.2 = ((f32[8,200,256]{2,1,0:T(8,128)}), f32[8,200,256]{2,1,0:T(8,128)S(1)}, u32[]{:S(2)}, u32[]{:S(2)}) async-start(f32[8,200,256]{2,1,0:T(8,128)} %pair_cols.1), calls=%async_computation.2 | async-start | bytes 3276800 | tf_op jit(solution)/shard_map/all_to_all | solution.py:296
  29.7 0.0 copy-start.1
  29.7 2.8 %copy-done.1 = f32[8,768,256]{2,1,0:T(8,128)S(1)} copy-done((f32[8,768,256]{2,1,0:T(8,128)S(1)}, f32[8,768,256]{2,1,0:T(8,128)}, u32[]{:S(2)}) %copy-start.1) | copy-done | bytes 6291480
  32.5 4.4 %pair_rows.1 = f32[16,104,256]{2,1,0:T(8,128)} custom-call(s32[3,2]{1,0:T(4,128)S(1)} %pad_add_fusion.meta, f32[4,8,128]{2,1,0:T(8,128)S(1)} %pad_maximum_fusion.own_pts, f32[4,8,128]{2,1,0:T(8,128)S(1)} %collective-permute-done.near_pts, f32[4,8,128]{2,1,0:T(8,128)S(1)} %collective-permute-done.1.far_pts, f32[8,768,256]{2,1,0:T(8,128)S(1)} %copy-done.1), custom_call_target="tpu_custom_call" | custom-call | flops 2000000000 | bytes 4000000 | tf_op jit(solution)/shard_map/pair_rows/pallas_call | solution.py:162
  36.9 15.1 %all-to-all-done.2.arrived = f32[8,200,256]{2,1,0:T(8,128)S(1)} async-done(((f32[8,200,256]{2,1,0:T(8,128)}), f32[8,200,256]{2,1,0:T(8,128)S(1)}, u32[]{:S(2)}, u32[]{:S(2)}) %all-to-all-start.2) | async-done | bytes 1638432 | tf_op jit(solution)/shard_map/all_to_all | solution.py:296
  52.0 4.5 %all-to-all-start = ((f32[16,104,256]{2,1,0:T(8,128)}), f32[16,104,256]{2,1,0:T(8,128)S(1)}, u32[]{:S(2)}, u32[]{:S(2)}) async-start(f32[16,104,256]{2,1,0:T(8,128)} %pair_rows.1), calls=%async_computation | async-start | bytes 3407872 | tf_op jit(solution)/shard_map/all_to_all | solution.py:296
  56.5 0.1 copy.14
  56.6 0.1 copy.15.ids
  56.6 0.9 add_arrived.3
  57.5 0.0 copy-start.2
  57.5 0.9 copy-done.2
  58.4 23.8 %all-to-all-done.arrived = f32[16,104,256]{2,1,0:T(8,128)S(1)} async-done(((f32[16,104,256]{2,1,0:T(8,128)}), f32[16,104,256]{2,1,0:T(8,128)S(1)}, u32[]{:S(2)}, u32[]{:S(2)}) %all-to-all-start) | async-done | bytes 1703968 | tf_op jit(solution)/shard_map/all_to_all | solution.py:296
  82.2 3.5 %all-to-all-start.3 = ((f32[8,96,256]{2,1,0:T(8,128)}), f32[8,96,256]{2,1,0:T(8,128)S(1)}, u32[]{:S(2)}, u32[]{:S(2)}) async-start(f32[8,96,256]{2,1,0:T(8,128)} %copy-done.2), calls=%async_computation.3 | async-start | bytes 1572864 | tf_op jit(solution)/shard_map/all_to_all | solution.py:296
  85.7 7.4 %collective-permute-start.3 = (f32[768,256]{1,0:T(8,128)}, f32[768,256]{1,0:T(8,128)}, u32[]{:S(2)}, u32[]{:S(2)}) collective-permute-start(f32[768,256]{1,0:T(8,128)} %dynamic-slice_bitcast_fusion), channel_id=1, source_target_pairs={{0,0},{1,1},{16,2},{17,3},{36,4},{37,5},{52,6},{53,7},{72,8},{73,9... | collective-permute-start | bytes 2359304 | tf_op jit(solution)/shard_map/ppermute | solution.py:316
  93.1 1.8 collective-permute-start.2
  95.0 0.1 copy.12
  95.1 0.1 copy.13.ids
  95.2 2.0 add_arrived.2
  97.1 1.7 all-to-all-done.3
  98.8 32.9 %all-to-all-start.1 = ((f32[16,48,256]{2,1,0:T(8,128)}), f32[16,48,256]{2,1,0:T(8,128)S(1)}, u32[]{:S(2)}, u32[]{:S(2)}) async-start(f32[16,48,256]{2,1,0:T(8,128)} %add_arrived.2), calls=%async_computation.1 | async-start | bytes 1572864 | tf_op jit(solution)/shard_map/all_to_all | solution.py:296
  131.7 0.0 collective-permute-done.3
  131.7 1.3 broadcast_multiply_fusion.self_cols
  133.0 0.0 collective-permute-done.2.self_rows
  133.1 12.5 %all-to-all-done.1 = f32[16,48,256]{2,1,0:T(8,128)S(1)} async-done(((f32[16,48,256]{2,1,0:T(8,128)}), f32[16,48,256]{2,1,0:T(8,128)S(1)}, u32[]{:S(2)}, u32[]{:S(2)}) %all-to-all-start.1) | async-done | bytes 786464 | tf_op jit(solution)/shard_map/all_to_all | solution.py:296
  145.6 19.1 %bases.1 = (f32[768,256]{1,0:T(8,128)S(1)}, f32[768,256]{1,0:T(8,128)S(1)}) custom-call(f32[768,256]{1,0:T(8,128)S(1)} %bitcast.20, f32[768,256]{1,0:T(8,128)S(1)} %collective-permute-done.2.self_rows, f32[768,256]{1,0:T(8,128)S(1)} %bitcast.19, f32[768,256]{1,0:T(8,128)S(1)} %broadcast_multiply_fusion.self_cols), custom_call_target="tpu_custom_call" | custom-call | flops 3000000000 | bytes 5000000 | tf_op jit(solution)/shard_map/bases/pallas_call | solution.py:279
  164.6 28.3 %all_to_all.30 = f32[8,96,256]{2,1,0:T(8,128)S(1)} all-to-all(f32[8,96,256]{2,1,0:T(8,128)S(1)} %bitcast.22), channel_id=1, replica_groups=mesh['row'=8,'col'=16] {'row'}, dimensions={0} | all-to-all | bytes 1572864 | tf_op jit(solution)/shard_map/all_to_all | solution.py:296
  192.9 18.4 %all_to_all.31 = f32[16,48,256]{2,1,0:T(8,128)S(1)} all-to-all(f32[16,48,256]{2,1,0:T(8,128)S(1)} %bitcast.21), channel_id=1, replica_groups=mesh['row'=8,'col'=16] {'col'}, dimensions={0} | all-to-all | bytes 1572864 | tf_op jit(solution)/shard_map/all_to_all | solution.py:296
  211.4 0.9 copy.21
  212.2 0.9 copy.22
  (4 shorter events, 0.1 us)
Async XLA Ops:
  2.0 14.0 %collective-permute-start = (f32[4,8,128]{2,1,0:T(8,128)S(1)}, f32[4,8,128]{2,1,0:T(8,128)S(1)}, u32[]{:S(2)}, u32[]{:S(2)}) collective-permute-start(f32[4,8,128]{2,1,0:T(8,128)S(1)} %pad_maximum_fusion.own_pts), channel_id=1, source_target_pairs={{64,0},{65,1},{81,2},{80,3},{96,4},{97,5},{113,6},{112,7},{0,8},{1... | collective-permute-start | bytes 49160 | tf_op jit(solution)/shard_map/ppermute | solution.py:305
  6.0 10.0 %collective-permute-start.1 = (f32[4,8,128]{2,1,0:T(8,128)S(1)}, f32[4,8,128]{2,1,0:T(8,128)S(1)}, u32[]{:S(2)}, u32[]{:S(2)}) collective-permute-start(f32[4,8,128]{2,1,0:T(8,128)S(1)} %pad_maximum_fusion.own_pts), channel_id=1, source_target_pairs={{65,0},{64,1},{80,2},{81,3},{97,4},{96,5},{112,6},{113,7},{1,8},{0... | collective-permute-start | bytes 49160 | tf_op jit(solution)/shard_map/ppermute | solution.py:306
  16.0 4.6 %copy-start = (f32[16,768,256]{2,1,0:T(8,128)S(1)}, f32[16,768,256]{2,1,0:T(8,128)}, u32[]{:S(2)}) copy-start(f32[16,768,256]{2,1,0:T(8,128)} %src.3) | copy-start | bytes 37748740
  24.4 27.6 %all-to-all-start.2 = ((f32[8,200,256]{2,1,0:T(8,128)}), f32[8,200,256]{2,1,0:T(8,128)S(1)}, u32[]{:S(2)}, u32[]{:S(2)}) async-start(f32[8,200,256]{2,1,0:T(8,128)} %pair_cols.1), calls=%async_computation.2 | async-start | bytes 3276800 | tf_op jit(solution)/shard_map/all_to_all | solution.py:296
  29.7 2.8 %copy-start.1 = (f32[8,768,256]{2,1,0:T(8,128)S(1)}, f32[8,768,256]{2,1,0:T(8,128)}, u32[]{:S(2)}) copy-start(f32[8,768,256]{2,1,0:T(8,128)} %src.2) | copy-start | bytes 18874372
  52.0 30.2 %all-to-all-start = ((f32[16,104,256]{2,1,0:T(8,128)}), f32[16,104,256]{2,1,0:T(8,128)S(1)}, u32[]{:S(2)}, u32[]{:S(2)}) async-start(f32[16,104,256]{2,1,0:T(8,128)} %pair_rows.1), calls=%async_computation | async-start | bytes 3407872 | tf_op jit(solution)/shard_map/all_to_all | solution.py:296
  57.5 0.9 copy-start.2
  82.2 16.6 %all-to-all-start.3 = ((f32[8,96,256]{2,1,0:T(8,128)}), f32[8,96,256]{2,1,0:T(8,128)S(1)}, u32[]{:S(2)}, u32[]{:S(2)}) async-start(f32[8,96,256]{2,1,0:T(8,128)} %copy-done.2), calls=%async_computation.3 | async-start | bytes 1572864 | tf_op jit(solution)/shard_map/all_to_all | solution.py:296
  85.7 46.0 %collective-permute-start.3 = (f32[768,256]{1,0:T(8,128)}, f32[768,256]{1,0:T(8,128)}, u32[]{:S(2)}, u32[]{:S(2)}) collective-permute-start(f32[768,256]{1,0:T(8,128)} %dynamic-slice_bitcast_fusion), channel_id=1, source_target_pairs={{0,0},{1,1},{16,2},{17,3},{36,4},{37,5},{52,6},{53,7},{72,8},{73,9... | collective-permute-start | bytes 2359304 | tf_op jit(solution)/shard_map/ppermute | solution.py:316
  93.1 39.9 %collective-permute-start.2 = (f32[768,256]{1,0:T(8,128)}, f32[768,256]{1,0:T(8,128)S(1)}, u32[]{:S(2)}, u32[]{:S(2)}) collective-permute-start(f32[768,256]{1,0:T(8,128)} %bitcast_multiply_fusion), channel_id=1, source_target_pairs={{0,0},{16,1},{32,2},{48,3},{64,4},{80,5},{96,6},{112,7},{1,8},{17,... | collective-permute-start | bytes 2359304 | tf_op jit(solution)/shard_map/ppermute | solution.py:315
  98.8 46.8 %all-to-all-start.1 = ((f32[16,48,256]{2,1,0:T(8,128)}), f32[16,48,256]{2,1,0:T(8,128)S(1)}, u32[]{:S(2)}, u32[]{:S(2)}) async-start(f32[16,48,256]{2,1,0:T(8,128)} %add_arrived.2), calls=%async_computation.1 | async-start | bytes 1572864 | tf_op jit(solution)/shard_map/all_to_all | solution.py:296

commit v2 on v1

--- a/solution.py
+++ b/solution.py
@@ -46,15 +46,18 @@
     return near, far
 
 
-def omega_route():
-    route = []
+def omega_routes(turn):
+    inside, along = [], []
     for y in range(4):
         for core in range(2):
             for z in range(4):
                 for x in range(4):
-                    src = device((2 * (z % 2) + x // 2 + y) % 4, x % 2, y, 2 * core + z // 2)
-                    route.append((src, device(y, core, z, x)))
-    return route
+                    src_y = y ^ (2 * (x // 2) + z % 2) ^ turn
+                    src_core = core ^ (x % 2)
+                    middle = device(src_y, src_core, z, x)
+                    inside.append((device(src_y, src_core, y, 2 * core + z // 2), middle))
+                    along.append((middle, device(y, core, z, x)))
+    return inside, along
 
 
 def psi_route():
@@ -73,12 +76,14 @@
     return high, (value - high.astype(F32)).astype(BF16)
 
 
-def pair_kernel(meta, own_pts, near_pts, far_pts, src, out, high_t, low_t, high_w, low_w, buf, left, sem, *, cut, turned):
+def pair_kernel(meta, own_pts, near_pts, far_pts, src, *refs, cut, turned):
     pieces = HEIGHT // cut
-    for slot in range(SLOTS):
-
+    outs, refs = (refs[:pieces], refs[pieces:]) if turned else ((), refs)
+    out, high_t, low_t, high_w, low_w, buf, left, sem = refs[:8]
+
+    def visit(slot, outer):
         @pl.when(meta[slot, 0] >= 0)
-        def _(slot=slot):
+        def _():
             row_id = meta[slot, 0]
             col_id = meta[slot, 1]
             pick = row_id if turned else col_id
@@ -142,29 +147,54 @@
             high_w[...] = hi
             low_w[...] = lo
             step_rows = cut * 2
-            for g in range(HEIGHT // step_rows):
-                part = pl.ds(g * step_rows, step_rows)
+
+            def rows_of(g, carry):
+                part = pl.ds(pl.multiple_of(g * step_rows, step_rows), step_rows)
                 acc = jnp.dot(high_t[part, :], high_w[...], preferred_element_type=F32)
                 acc += jnp.dot(high_t[part, :], low_w[...], preferred_element_type=F32)
                 acc += jnp.dot(low_t[part, :], high_w[...], preferred_element_type=F32)
-                out[2 * g, slot * cut : (slot + 1) * cut, :] = acc[:cut]
-                out[2 * g + 1, slot * cut : (slot + 1) * cut, :] = acc[cut:]
-
+                for h in range(2):
+                    out[(2 * g + h) ^ meta[SLOTS, 1], pl.ds(pl.multiple_of(slot * cut, cut), cut), :] = acc[h * cut : (h + 1) * cut]
+                return carry
+
+            lax.fori_loop(0, HEIGHT // step_rows, rows_of, 0)
+
+        return outer
+
+    lax.fori_loop(0, SLOTS, visit, 0)
+    for slot in range(SLOTS):
         tag = jnp.full((1, 1, SK), meta[slot, 1 if turned else 0].astype(F32))
         out[:, SLOTS * cut + slot * (TAG // SLOTS) : SLOTS * cut + (slot + 1) * (TAG // SLOTS), :] = (
             jnp.broadcast_to(tag, (pieces, TAG // SLOTS, SK))
         )
+    send_out(out, outs, refs[8:])
+
+
+def send_out(held, outs, sems):
+    copies = [pltpu.make_async_copy(held.at[k], one.at[0], sems[0].at[k]) for k, one in enumerate(outs)]
+    for copy in copies:
+        copy.start()
+    for copy in copies:
+        copy.wait()
 
 
 def pair_terms(meta, own_pts, near_pts, far_pts, src, cut, turned):
     pieces = HEIGHT // cut
     vmem = pl.BlockSpec(memory_space=pltpu.VMEM)
+    rows = SLOTS * cut + TAG
+    if turned:
+        shape = tuple(jax.ShapeDtypeStruct((1, rows, SK), F32) for _ in range(pieces))
+        specs = tuple(pl.BlockSpec(memory_space=pltpu.HBM) for _ in range(pieces))
+        held, sems = [pltpu.VMEM((pieces, rows, SK), F32)], [pltpu.SemaphoreType.DMA((pieces,))]
+    else:
+        shape, specs, held, sems = jax.ShapeDtypeStruct((pieces, rows, SK), F32), vmem, [], []
     return pl.pallas_call(
         functools.partial(pair_kernel, cut=cut, turned=turned),
-        out_shape=jax.ShapeDtypeStruct((pieces, SLOTS * cut + TAG, SK), F32),
-        in_specs=[pl.BlockSpec(memory_space=pltpu.SMEM), vmem, vmem, vmem, pl.BlockSpec(memory_space=pl.ANY)],
-        out_specs=vmem,
-        scratch_shapes=[
+        out_shape=shape,
+        in_specs=[pl.BlockSpec(memory_space=pltpu.SMEM), vmem, vmem, vmem, pl.BlockSpec(memory_space=pltpu.HBM)],
+        out_specs=specs,
+        scratch_shapes=held
+        + [
             pltpu.VMEM((HEIGHT, HEIGHT), BF16),
             pltpu.VMEM((HEIGHT, HEIGHT), BF16),
             pltpu.VMEM((HEIGHT, SK), BF16),
@@ -172,35 +202,66 @@
             pltpu.VMEM((HEIGHT, SK), F32),
             pltpu.VMEM((4, ZC, ZC), F32),
             pltpu.SemaphoreType.DMA,
-        ],
-        compiler_params=pltpu.CompilerParams(vmem_limit_bytes=24 << 20),
+        ]
+        + sems,
         cost_estimate=pl.CostEstimate(flops=2_000_000_000, bytes_accessed=4_000_000, transcendentals=32768),
         name="pair_cols" if turned else "pair_rows",
     )(meta, own_pts, near_pts, far_pts, src)
 
 
-def add_kernel(ids, arrived, out, *, cut):
+def add_kernel(ids, turn, *refs, cut, parts):
+    arrived, outs, refs = refs[:parts], refs[parts : 2 * parts], refs[2 * parts :]
+    if parts == 1:
+        outs, refs = (), outs + refs
+    out, stage, sems = refs[:3]
+    total = ids.shape[0] * SLOTS
+
+    def fetch(at, n):
+        k, slot = n // SLOTS, n % SLOTS
+        if parts == 1:
+            src = arrived[0].at[k, pl.ds(slot * cut, cut)]
+        else:
+            src = arrived[k].at[0, pl.ds(slot * cut, cut)]
+        return pltpu.make_async_copy(src, stage.at[at], sems.at[at])
+
+    for n in range(total):
+
+        @pl.when(ids[n // SLOTS, n % SLOTS] >= 0)
+        def _(n=n):
+            fetch(n, n).start()
+
     out[...] = jnp.zeros_like(out)
-    for k in range(arrived.shape[0]):
-        for slot in range(SLOTS):
-
-            @pl.when(ids[k, slot] >= 0)
-            def _(k=k, slot=slot):
-                out[ids[k, slot]] += arrived[k, slot * cut : (slot + 1) * cut, :]
-
-
-def add_arrived(arrived, clusters, cut):
-    ids = arrived[:, SLOTS * cut :: TAG // SLOTS, 0].astype(jnp.int32)
-    vmem = pl.BlockSpec(memory_space=pltpu.VMEM)
+    for n in range(total):
+
+        @pl.when(ids[n // SLOTS, n % SLOTS] >= 0)
+        def _(n=n):
+            fetch(n, n).wait()
+            out[ids[n // SLOTS, n % SLOTS] ^ turn[0]] += stage[n]
+
+    send_out(out, outs, refs[3:])
+
+
+def add_arrived(arrived, turn, clusters, cut):
+    ids = [part[:, SLOTS * cut :: TAG // SLOTS, 0] for part in arrived]
+    ids = jnp.concatenate(ids, axis=0).astype(jnp.int32)
+    total = ids.shape[0] * SLOTS
+    smem = pl.BlockSpec(memory_space=pltpu.SMEM)
+    if len(arrived) > 1:
+        shape = tuple(jax.ShapeDtypeStruct((1, cut, SK), F32) for _ in range(clusters))
+        specs = tuple(pl.BlockSpec(memory_space=pltpu.HBM) for _ in range(clusters))
+        held, sems = [pltpu.VMEM((clusters, cut, SK), F32)], [pltpu.SemaphoreType.DMA((clusters,))]
+    else:
+        shape, held, sems = jax.ShapeDtypeStruct((clusters, cut, SK), F32), [], []
+        specs = pl.BlockSpec(memory_space=pltpu.VMEM)
     return pl.pallas_call(
-        functools.partial(add_kernel, cut=cut),
-        out_shape=jax.ShapeDtypeStruct((clusters, cut, SK), F32),
-        in_specs=[pl.BlockSpec(memory_space=pltpu.SMEM), vmem],
-        out_specs=vmem,
-        compiler_params=pltpu.CompilerParams(vmem_limit_bytes=16 << 20),
+        functools.partial(add_kernel, cut=cut, parts=len(arrived)),
+        out_shape=shape,
+        in_specs=[smem, smem] + [pl.BlockSpec(memory_space=pltpu.HBM)] * len(arrived),
+        out_specs=specs,
+        scratch_shapes=held + [pltpu.VMEM((total, cut, SK), F32), pltpu.SemaphoreType.DMA((total,))] + sems,
         cost_estimate=pl.CostEstimate(flops=1_000_000, bytes_accessed=3_000_000, transcendentals=0),
         name="add_arrived",
-    )(ids, arrived)
+    )(ids, turn.reshape(1), *arrived)
 
 
 BLK = 64
@@ -242,11 +303,18 @@
     return jnp.concatenate(done, axis=0)[:, :BLK]
 
 
-def basis_kernel(rows, self_rows, cols, self_cols, out_rows, out_cols, sk, gram, inverse):
+def basis_kernel(turn, rows, self_high, self_low, self_cols, *refs):
+    cols = refs[:NR]
+    out_rows, out_cols, (sk, gram, inverse, low_q) = refs[NR], refs[NR + 1 : 2 * NR + 1], refs[2 * NR + 1 :]
     n = SK // BLK
     dims0 = (((0,), (0,)), ((), ()))
-    for w, (got, own) in enumerate(((rows, self_rows), (cols, self_cols))):
-        sk[w] = got[...] + own[...]
+    half = HEIGHT // 2
+    sk[0, :half] = rows[:half] + self_high[...]
+    sk[0, half:] = rows[half:] + self_low[...]
+    for k in range(NR):
+        part = pl.ds(pl.multiple_of((k ^ turn[0]) * COL_CUT, COL_CUT), COL_CUT)
+        sk[1, part, :] = cols[k][0] + self_cols[part, :]
+    for w in range(2):
         gram[w] = lax.dot_general(sk[w], sk[w], dims0, precision=HIGH, preferred_element_type=F32)
         inverse[w] = jnp.zeros((SK, SK), F32)
     for k in range(n):
@@ -267,36 +335,48 @@
                 inverse[w, rest, : (k + 1) * BLK] = inverse[w, rest, : (k + 1) * BLK] - lax.dot_general(
                     upper, inverse[w, here, : (k + 1) * BLK], dims0, precision=HIGH, preferred_element_type=F32
                 )
-    for w, out in enumerate((out_rows, out_cols)):
-        out[...] = lax.dot_general(
-            sk[w], inverse[w], (((1,), (1,)), ((), ())), precision=HIGH, preferred_element_type=F32
-        )
-
-
-def bases(rows, self_rows, cols, self_cols):
+    dims1 = (((1,), (1,)), ((), ()))
+    q = lax.dot_general(sk[1], inverse[1], dims1, precision=HIGH, preferred_element_type=F32)
+    for g in range(NR):
+        low_q[g ^ turn[0]] = q[g * COL_CUT : (g + 1) * COL_CUT]
+    for k in range(NR):
+        out_cols[k][0] = low_q[k]
+    out_rows[...] = lax.dot_general(sk[0], inverse[0], dims1, precision=HIGH, preferred_element_type=F32)
+
+
+def bases(turn, rows, self_rows, cols, self_cols):
     shape = jax.ShapeDtypeStruct((HEIGHT, SK), F32)
+    shape_c = jax.ShapeDtypeStruct((1, COL_CUT, SK), F32)
     vmem = pl.BlockSpec(memory_space=pltpu.VMEM)
     return pl.pallas_call(
         basis_kernel,
-        out_shape=(shape, shape),
-        in_specs=[vmem] * 4,
-        out_specs=(vmem, vmem),
+        out_shape=(shape,) + (shape_c,) * NR,
+        in_specs=[pl.BlockSpec(memory_space=pltpu.SMEM)] + [vmem] * (4 + NR),
+        out_specs=(vmem,) * (NR + 1),
         scratch_shapes=[
             pltpu.VMEM((2, HEIGHT, SK), F32),
             pltpu.VMEM((2, SK, SK), F32),
             pltpu.VMEM((2, SK, SK), F32),
+            pltpu.VMEM((NR, COL_CUT, SK), F32),
         ],
         compiler_params=pltpu.CompilerParams(vmem_limit_bytes=32 << 20),
         cost_estimate=pl.CostEstimate(flops=3_000_000_000, bytes_accessed=5_000_000, transcendentals=0),
         name="bases",
-    )(rows, self_rows, cols, self_cols)
+    )(turn.reshape(1), rows, *self_rows, self_cols, *cols)
 
 
 def trade(value, axis):
     return lax.all_to_all(value, axis, split_axis=0, concat_axis=0, tiled=True)
 
 
-def per_device(positions, modulus, self_weight, omega, psi, blocks):
+def swap_rows(value):
+    got = [value[0]]
+    for k in range(1, NR):
+        got.append(lax.ppermute(value[k], "row", [(i, i ^ k) for i in range(NR)]))
+    return got
+
+
+def level(positions, modulus, self_weight, omega, psi, blocks):
     row_at = lax.axis_index("row")
     col_at = lax.axis_index("col")
     near_route, far_route = point_routes()
@@ -306,32 +386,42 @@
     far_pts = lax.ppermute(points, BOTH, far_route)
 
     src_y, src_core, src_z, src_x = row_at // 2, row_at % 2, col_at // 4, col_at % 4
-    bits = (src_y - src_z) % 4
-    omega_pick = (bits // 2) * 4 + (bits % 2) * 2 + src_core
-    omega_send = omega[omega_pick] * self_weight[omega_pick][:, None]
+    bits = src_z ^ src_y
+    omega_pick = (bits % 2) * 4 + (bits // 2) * 2 + ((src_x // 2) ^ src_core)
+    half = HEIGHT // 2
+    self_rows = []
+    for h, turn in enumerate((0, 2)):
+        inside, along = omega_routes(turn)
+        pick = omega_pick ^ turn
+        weight = lax.dynamic_slice(self_weight, (pick, h * half), (1, half)).reshape(half, 1)
+        part = lax.dynamic_slice(omega, (pick, h * half, 0), (1, half, SK)).reshape(half, SK) * weight
+        part = lax.ppermute(part, BOTH, inside)
+        self_rows.append(lax.ppermute(part, BOTH, along))
     psi_pick = (src_x % 2) * 8 + ((src_z - src_y) % 4) * 2 + src_x // 2
-    psi_send = psi[psi_pick]
-    omega_send, psi_send, near_pts, far_pts = lax.optimization_barrier((omega_send, psi_send, near_pts, far_pts))
-    self_rows = lax.ppermute(omega_send, BOTH, omega_route())
-    psi_here = lax.ppermute(psi_send, BOTH, psi_route())
+    psi_here = lax.ppermute(psi[psi_pick], BOTH, psi_route())
     self_cols = psi_here * self_weight[row_at][:, None]
 
     pairs = blocks.reshape(SLOTS, 2)
-    core = row_at % 2
-    away = ((col_at % 4) // 2) ^ core
+    away = ((col_at % 4) // 2) ^ (row_at % 2)
     near_half = (col_at % 2) ^ away
-    meta = jnp.concatenate([pairs, jnp.stack([near_half, near_half])[None]], axis=0).astype(jnp.int32)
-
-    row_terms = pair_terms(meta, points, near_pts, far_pts, omega, ROW_CUT, False)
-    col_terms = pair_terms(meta, points, near_pts, far_pts, psi, COL_CUT, True)
-
-    row_sum = add_arrived(trade(row_terms, "col"), ROW_CL, ROW_CUT)
-    col_sum = add_arrived(trade(col_terms, "row"), COL_CL, COL_CUT)
+    none = jnp.int32(0)
+    row_meta = jnp.concatenate([pairs, jnp.stack([near_half, none])[None]], axis=0).astype(jnp.int32)
+    col_meta = jnp.concatenate([pairs, jnp.stack([near_half, row_at])[None]], axis=0).astype(jnp.int32)
+
+    row_terms = pair_terms(row_meta, points, near_pts, far_pts, omega, ROW_CUT, False)
+    col_terms = pair_terms(col_meta, points, near_pts, far_pts, psi, COL_CUT, True)
+
+    row_got = trade(row_terms, "col")
+    col_got = swap_rows(col_terms)
+    row_sum = add_arrived([row_got], none, ROW_CL, ROW_CUT)
+    col_sum = add_arrived(col_got, row_at, COL_CL, COL_CUT)
     rows = trade(row_sum, "col").reshape(HEIGHT, SK)
-    cols = trade(col_sum, "row").reshape(HEIGHT, SK)
-    row_q, col_q = bases(rows, self_rows, cols, self_cols)
+    cols = swap_rows(col_sum)
+    row_q, *col_q = bases(row_at, rows, self_rows, cols, self_cols)
     row_basis = trade(row_q.reshape(NC, ROW_CUT, SK), "col")
-    col_basis = trade(col_q.reshape(NR, COL_CUT, SK), "row")
+    col_basis = jnp.zeros((NR, COL_CUT, SK), F32)
+    for k, part in enumerate(swap_rows(col_q)):
+        col_basis = lax.dynamic_update_slice_in_dim(col_basis, part, row_at ^ k, 0)
     return (row_basis, col_basis)
 
 
@@ -345,7 +435,7 @@
         P("row", "col", None, None),
     )
     return jax.shard_map(
-        per_device,
+        level,
         mesh=mesh,
         in_specs=placed,
         out_specs=(P("row", "col", None), P("col", "row", None)),

time: 214 us -> 190 us (0.89)
  blocking collectives: 46.7 us -> 0 us
  local copies, waits for them, and re-layouts: 14 us -> 31.8 us
  starting transfers between devices: 63.6 us -> 71.3 us
  Pallas kernels: 30.1 us -> 24.2 us
    ppermute x4 -> x28, waiting for transfers between devices: 0.01 us -> 46.9 us  [the longest x21 46.2 us: swap_rows(): got.append(lax.ppermute(value[k], 'row', [(i, i ^ k) for i in range(NR)]))]
    all_to_all x2 -> x0, blocking collectives: 46.7 us -> none  [trade(): return lax.all_to_all(value, axis, split_axis=0, concat_axis=0, tiled=True)]
    all_to_all x4 -> x3, waiting for transfers between devices: 53 us -> 6.66 us  [trade(): return lax.all_to_all(value, axis, split_axis=0, concat_axis=0, tiled=True)]
    ppermute x4 -> x28, starting transfers between devices: 17.3 us -> 54.3 us  [the longest x21 29.2 us: swap_rows(): got.append(lax.ppermute(value[k], 'row', [(i, i ^ k) for i in range(NR)]))]
    all_to_all x4 -> x3, starting transfers between devices: 46.3 us -> 17.1 us  [trade(): return lax.all_to_all(value, axis, split_axis=0, concat_axis=0, tiled=True)]
    pallas_call x0 -> x1, local copies, waits for them, and re-layouts: none -> 21.3 us  [bases(): pl.pallas_call(basis_kernel, out_shape=(shape,) + (shape_c,) * NR, in_spe...]
    pallas_call x3 -> x2, Pallas kernels: 21.9 us -> 6.36 us  [add_arrived(): pl.pallas_call(functools.partial(add_kernel, cut=cut, parts=len(arrived))...]
    pallas_call x2, Pallas kernels: 8.17 us -> 17.8 us  [pair_terms(): pl.pallas_call(functools.partial(pair_kernel, cut=cut, turned=turned), ou...]
  transfers between devices with their start and end apart: 8 -> 31, of which waited for: 4 -> 12; matrix products, arithmetic and copies ran while one was open for 4% -> 7% of each run, Pallas kernels for 3% -> 8%
where the time goes in v2:
time: 190 us; the launch traced here: 188 us
  starting transfers between devices  71.3 us (38%)
  waiting for transfers between devices  53.6 us (28%)
  local copies, waits for them, and re-layouts  31.8 us (17%)
  Pallas kernels  24.2 us (13%)
  other arithmetic  5.93 us (3%)
    ppermute x21, waiting for transfers between devices, swap_rows(): got.append(lax.ppermute(value[k], 'row', [(i, i ^ k) for i in range(NR)]))  46.2 us
    ppermute x21, starting transfers between devices, swap_rows(): got.append(lax.ppermute(value[k], 'row', [(i, i ^ k) for i in range(NR)]))  29.2 us
    pallas_call x1, local copies, waits for them, and re-layouts, bases(): pl.pallas_call(basis_kernel, out_shape=(shape,) + (shape_c,) * NR, in_spe...  21.3 us
    pallas_call x2, Pallas kernels, pair_terms(): pl.pallas_call(functools.partial(pair_kernel, cut=cut, turned=turned), ou...  17.8 us
    all_to_all x3, starting transfers between devices, trade(): return lax.all_to_all(value, axis, split_axis=0, concat_axis=0, tiled=True)  17.1 us
    ppermute x2, starting transfers between devices, level(): self_rows.append(lax.ppermute(part, BOTH, along))  8.16 us
    ppermute x2, starting transfers between devices, level(): part = lax.ppermute(part, BOTH, inside)  8.1 us
    all_to_all x3, waiting for transfers between devices, trade(): return lax.all_to_all(value, axis, split_axis=0, concat_axis=0, tiled=True)  6.66 us
  transfers between devices with their start and end apart: 31, of which 12 were waited for; matrix products, arithmetic and copies ran while one was open for 7% of the time, Pallas kernels for 8%

profile of v2, /device:TPU:0, one launch (start us, length us, event | category | flops | bytes accessed | tf_op | source)
XLA Modules:
  0.0 187.9 jit_solution(15879418565741356894)
XLA Ops:
  0.6 0.7 copy.29
  2.0 4.0 %collective-permute-start = (f32[4,8,128]{2,1,0:T(8,128)S(1)}, f32[4,8,128]{2,1,0:T(8,128)S(1)}, u32[]{:S(2)}, u32[]{:S(2)}) collective-permute-start(f32[4,8,128]{2,1,0:T(8,128)S(1)} %pad_maximum_fusion.own_pts), channel_id=1, source_target_pairs={{64,0},{65,1},{81,2},{80,3},{96,4},{97,5},{113,6},{112,7},{0,8},{1... | collective-permute-start | bytes 49160 | tf_op jit(solution)/shard_map/ppermute | solution.py:385
  6.0 4.1 %collective-permute-start.1 = (f32[4,8,128]{2,1,0:T(8,128)S(1)}, f32[4,8,128]{2,1,0:T(8,128)S(1)}, u32[]{:S(2)}, u32[]{:S(2)}) collective-permute-start(f32[4,8,128]{2,1,0:T(8,128)S(1)} %pad_maximum_fusion.own_pts), channel_id=1, source_target_pairs={{65,0},{64,1},{80,2},{81,3},{97,4},{96,5},{112,6},{113,7},{1,8},{0... | collective-permute-start | bytes 49160 | tf_op jit(solution)/shard_map/ppermute | solution.py:386
  10.2 1.3 pad_add_fusion
  11.5 0.7 collective-permute-done.1.far_pts
  12.8 10.0 %pair_rows.1 = f32[16,104,256]{2,1,0:T(8,128)} custom-call(s32[3,2]{1,0:T(4,128)} %get-tuple-element.75.meta, f32[4,8,128]{2,1,0:T(8,128)} %copy-done.7, f32[4,8,128]{2,1,0:T(8,128)} %copy-done.8, f32[4,8,128]{2,1,0:T(8,128)} %copy-done.9, f32[8,768,256]{2,1,0:T(8,128)} %src.2), custom_call_target="tpu_custom_call" | custom-call | flops 2000000000 | bytes 4000000 | tf_op jit(solution)/shard_map/pair_rows/pallas_call | solution.py:191
  22.8 5.9 %all-to-all-start = ((f32[16,104,256]{2,1,0:T(8,128)}), f32[16,104,256]{2,1,0:T(8,128)S(1)}, u32[]{:S(2)}, u32[]{:S(2)}) async-start(f32[16,104,256]{2,1,0:T(8,128)} %pair_rows.1), calls=%async_computation | async-start | bytes 3407872 | tf_op jit(solution)/shard_map/all_to_all | solution.py:369
  28.7 7.8 %pair_cols.1 = (f32[1,200,256]{2,1,0:T(8,128)}, f32[1,200,256]{2,1,0:T(8,128)}, f32[1,200,256]{2,1,0:T(8,128)}, f32[1,200,256]{2,1,0:T(8,128)}, f32[1,200,256]{2...) custom-call(s32[3,2]{1,0:T(4,128)} %get-tuple-element.74.meta, ...), custom_call_target="tpu_custom_call" | custom-call | flops 2000000000 | bytes 4000000 | tf_op jit(solution)/shard_map/pair_cols/pallas_call | solution.py:191
  36.7 1.2 dynamic-slice_bitcast_fusion
  37.9 0.7 collective-permute-start.6
  38.7 0.7 dynamic-slice_reduce_fusion
  39.4 2.2 %collective-permute-start.8 = (f32[1,200,256]{2,1,0:T(8,128)}, f32[1,200,256]{2,1,0:T(8,128)S(1)}, u32[]{:S(2)}, u32[]{:S(2)}) collective-permute-start(f32[1,200,256]{2,1,0:T(8,128)} %get-tuple-element.29), channel_id=1, source_target_pairs={{0,32},{16,48},{32,0},{48,16},{64,96},{80,112},{96,64},{112,80},{1... | collective-permute-start | bytes 614408 | tf_op jit(solution)/shard_map/ppermute | solution.py:375
  41.6 4.2 %collective-permute-start.9 = (f32[1,200,256]{2,1,0:T(8,128)}, f32[1,200,256]{2,1,0:T(8,128)S(1)}, u32[]{:S(2)}, u32[]{:S(2)}) collective-permute-start(f32[1,200,256]{2,1,0:T(8,128)} %get-tuple-element.30), channel_id=1, source_target_pairs={{0,48},{16,32},{32,16},{48,0},{64,112},{80,96},{96,80},{112,64},{1... | collective-permute-start | bytes 614408 | tf_op jit(solution)/shard_map/ppermute | solution.py:375
  45.8 1.8 collective-permute-start.10
  47.6 1.1 collective-permute-start.11
  48.7 2.2 %bitcast_multiply_fusion = (f32[384,256]{1,0:T(8,128)}, f32[384,256]{1,0:T(8,128)}) fusion(f32[8,768,256]{2,1,0:T(8,128)} %src.2, s32[]{:T(128)S(6)} %select_n.91, f32[384]{0:T(512)S(1)} %get-tuple-element.70, f32[384]{0:T(512)S(1)} %get-tuple-element.71, s32[]{:T(128)S(6)} %select_n.90), kind=kLoop, calls=%fused_computation.1 | loop fusion | flops 196608 | bytes 1575944 | tf_op jit(solution)/shard_map/mul | solution.py:397
  50.9 20.8 %collective-permute-done.8.refs_2_ = f32[1,200,256]{2,1,0:T(8,128)S(1)} collective-permute-done((f32[1,200,256]{2,1,0:T(8,128)}, f32[1,200,256]{2,1,0:T(8,128)S(1)}, u32[]{:S(2)}, u32[]{:S(2)}) %collective-permute-start.8) | collective-permute-done | bytes 204832 | tf_op jit(solution)/shard_map/ppermute | solution.py:375
  71.7 4.5 %collective-permute-start.2 = (f32[384,256]{1,0:T(8,128)}, f32[384,256]{1,0:T(8,128)}, u32[]{:S(2)}, u32[]{:S(2)}) collective-permute-start(f32[384,256]{1,0:T(8,128)} %get-tuple-element.73), channel_id=1, source_target_pairs={{0,0},{16,17},{64,66},{80,83},{32,36},{48,53},{96,102},{112,119},{... | collective-permute-start | bytes 1179656 | tf_op jit(solution)/shard_map/ppermute | solution.py:398
  76.8 3.6 %collective-permute-start.4 = (f32[384,256]{1,0:T(8,128)}, f32[384,256]{1,0:T(8,128)}, u32[]{:S(2)}, u32[]{:S(2)}) collective-permute-start(f32[384,256]{1,0:T(8,128)} %get-tuple-element.72), channel_id=1, source_target_pairs={{64,64},{80,81},{0,2},{16,19},{96,100},{112,117},{32,38},{48,55},{... | collective-permute-start | bytes 1179656 | tf_op jit(solution)/shard_map/ppermute | solution.py:398
  80.6 0.9 copy.26.ids
  81.7 3.2 %add_arrived.2 = f32[16,48,256]{2,1,0:T(8,128)} custom-call(s32[16,2]{1,0:T(8,128)} %copy.26.ids, s32[1]{0:T(128)} %constant.100.clone.1.turn, f32[16,104,256]{2,1,0:T(8,128)} %copy-done), custom_call_target="tpu_custom_call" | custom-call | flops 1000000 | bytes 3000000 | tf_op jit(solution)/shard_map/add_arrived/pallas_call | solution.py:256
  84.9 6.3 %all-to-all-start.1 = ((f32[16,48,256]{2,1,0:T(8,128)}), f32[16,48,256]{2,1,0:T(8,128)S(1)}, u32[]{:S(2)}, u32[]{:S(2)}) async-start(f32[16,48,256]{2,1,0:T(8,128)} %add_arrived.2), calls=%async_computation.1 | async-start | bytes 1572864 | tf_op jit(solution)/shard_map/all_to_all | solution.py:369
  91.8 1.9 collective-permute-start.13
  97.8 2.8 %collective-permute-done.12.refs_6_ = f32[1,200,256]{2,1,0:T(8,128)S(1)} collective-permute-done((f32[1,200,256]{2,1,0:T(8,128)}, f32[1,200,256]{2,1,0:T(8,128)S(1)}, u32[]{:S(2)}, u32[]{:S(2)}) %collective-permute-start.12) | collective-permute-done | bytes 204832 | tf_op jit(solution)/shard_map/ppermute | solution.py:375
  100.8 1.9 %collective-permute-done.13.refs_7_ = f32[1,200,256]{2,1,0:T(8,128)S(1)} collective-permute-done((f32[1,200,256]{2,1,0:T(8,128)}, f32[1,200,256]{2,1,0:T(8,128)S(1)}, u32[]{:S(2)}, u32[]{:S(2)}) %collective-permute-start.13) | collective-permute-done | bytes 204832 | tf_op jit(solution)/shard_map/ppermute | solution.py:375
  103.5 3.2 %add_arrived.3 = (f32[1,96,256]{2,1,0:T(8,128)}, f32[1,96,256]{2,1,0:T(8,128)}, f32[1,96,256]{2,1,0:T(8,128)}, f32[1,96,256]{2,1,0:T(8,128)}, f32[1,96,256]{2,1,...) custom-call(s32[8,2]{1,0:T(8,128)} %convert_element_type.10.ids, s32[1]{0:T(128)} %bitcast.turn, ...), custom_call_target="tpu_custom_call" | custom-call | flops 1000000 | bytes 3000000 | tf_op jit(solution)/shard_map/add_arrived/pallas_call | solution.py:256
  106.7 1.1 collective-permute-start.14
  107.8 1.6 collective-permute-start.15
  109.4 4.5 %collective-permute-start.3 = (f32[384,256]{1,0:T(8,128)}, f32[384,256]{1,0:T(8,128)}, u32[]{:S(2)}, u32[]{:S(2)}) collective-permute-start(f32[384,256]{1,0:T(8,128)} %collective-permute-done.2), channel_id=1, source_target_pairs={{0,0},{17,1},{66,2},{83,3},{36,4},{53,5},{102,6},{119,7},{8,8},{25... | collective-permute-start | bytes 1179656 | tf_op jit(solution)/shard_map/ppermute | solution.py:399
  113.9 3.7 %collective-permute-start.5 = (f32[384,256]{1,0:T(8,128)}, f32[384,256]{1,0:T(8,128)}, u32[]{:S(2)}, u32[]{:S(2)}) collective-permute-start(f32[384,256]{1,0:T(8,128)} %collective-permute-done.4), channel_id=1, source_target_pairs={{64,0},{81,1},{2,2},{19,3},{100,4},{117,5},{38,6},{55,7},{72,8},{8... | collective-permute-start | bytes 1179656 | tf_op jit(solution)/shard_map/ppermute | solution.py:399
  118.2 1.3 collective-permute-start.17
  119.5 0.8 fusion
  120.3 9.2 %collective-permute-done.16 = f32[1,96,256]{2,1,0:T(8,128)S(1)} collective-permute-done((f32[1,96,256]{2,1,0:T(8,128)}, f32[1,96,256]{2,1,0:T(8,128)S(1)}, u32[]{:S(2)}, u32[]{:S(2)}) %collective-permute-start.16) | collective-permute-done | bytes 98336 | tf_op jit(solution)/shard_map/ppermute | solution.py:375
  129.5 2.4 %collective-permute-start.18 = (f32[1,96,256]{2,1,0:T(8,128)}, f32[1,96,256]{2,1,0:T(8,128)S(1)}, u32[]{:S(2)}, u32[]{:S(2)}) collective-permute-start(f32[1,96,256]{2,1,0:T(8,128)} %get-tuple-element.40), channel_id=1, source_target_pairs={{0,80},{16,64},{32,112},{48,96},{64,16},{80,0},{96,48},{112,32},{1... | collective-permute-start | bytes 294920 | tf_op jit(solution)/shard_map/ppermute | solution.py:375
  132.5 2.3 %collective-permute-start.19 = (f32[1,96,256]{2,1,0:T(8,128)}, f32[1,96,256]{2,1,0:T(8,128)S(1)}, u32[]{:S(2)}, u32[]{:S(2)}) collective-permute-start(f32[1,96,256]{2,1,0:T(8,128)} %get-tuple-element.41), channel_id=1, source_target_pairs={{0,96},{16,112},{32,64},{48,80},{64,32},{80,48},{96,0},{112,16},{1... | collective-permute-start | bytes 294920 | tf_op jit(solution)/shard_map/ppermute | solution.py:375
  135.3 3.3 %collective-permute-done.19 = f32[1,96,256]{2,1,0:T(8,128)S(1)} collective-permute-done((f32[1,96,256]{2,1,0:T(8,128)}, f32[1,96,256]{2,1,0:T(8,128)S(1)}, u32[]{:S(2)}, u32[]{:S(2)}) %collective-permute-start.19) | collective-permute-done | bytes 98336 | tf_op jit(solution)/shard_map/ppermute | solution.py:375
  138.6 2.1 %collective-permute-done.20 = f32[1,96,256]{2,1,0:T(8,128)S(1)} collective-permute-done((f32[1,96,256]{2,1,0:T(8,128)}, f32[1,96,256]{2,1,0:T(8,128)S(1)}, u32[]{:S(2)}, u32[]{:S(2)}) %collective-permute-start.20) | collective-permute-done | bytes 98336 | tf_op jit(solution)/shard_map/ppermute | solution.py:375
  140.8 21.3 %bases.1 = (f32[8,96,256]{2,1,0:T(8,128)S(1)}, f32[768,256]{1,0:T(8,128)}, f32[1,96,256]{2,1,0:T(8,128)S(1)}, f32[1,96,256]{2,1,0:T(8,128)S(1)}, f32[1,96,256]{2...) fusion(f32[8,96,256]{2,1,0:T(8,128)S(1)} %broadcast_in_dim.12, ...), kind=kCustom, calls=%fused_computation.13 | custom fusion | bytes 4718600 | tf_op jit(solution)/shard_map/bases/pallas_call | solution.py:351
  162.5 1.5 collective-permute-start.23
  164.0 1.8 collective-permute-start.24
  165.8 1.4 collective-permute-start.25
  167.1 4.9 %all-to-all-start.2 = ((f32[16,48,256]{2,1,0:T(8,128)}), f32[16,48,256]{2,1,0:T(8,128)S(1)}, u32[]{:S(2)}, u32[]{:S(2)}) async-start(f32[16,48,256]{2,1,0:T(8,128)} %bitcast.11), calls=%async_computation.2 | async-start | bytes 1572864 | tf_op jit(solution)/shard_map/all_to_all | solution.py:369
  172.0 2.0 %collective-permute-start.26 = (f32[1,96,256]{2,1,0:T(8,128)S(1)}, f32[1,96,256]{2,1,0:T(8,128)S(1)}, u32[]{:S(2)}, u32[]{:S(2)}) collective-permute-start(f32[1,96,256]{2,1,0:T(8,128)S(1)} %get-tuple-element.67), channel_id=1, source_target_pairs={{0,96},{16,112},{32,64},{48,80},{64,32},{80,48},{96,0},{112,16},{1... | collective-permute-start | bytes 294920 | tf_op jit(solution)/shard_map/ppermute | solution.py:375
  174.1 0.9 collective-permute-start.27
  175.1 3.1 %collective-permute-done.26 = f32[1,96,256]{2,1,0:T(8,128)S(1)} collective-permute-done((f32[1,96,256]{2,1,0:T(8,128)S(1)}, f32[1,96,256]{2,1,0:T(8,128)S(1)}, u32[]{:S(2)}, u32[]{:S(2)}) %collective-permute-start.26) | collective-permute-done | bytes 98336 | tf_op jit(solution)/shard_map/ppermute | solution.py:375
  178.2 2.1 %collective-permute-done.27 = f32[1,96,256]{2,1,0:T(8,128)S(1)} collective-permute-done((f32[1,96,256]{2,1,0:T(8,128)S(1)}, f32[1,96,256]{2,1,0:T(8,128)S(1)}, u32[]{:S(2)}, u32[]{:S(2)}) %collective-permute-start.27) | collective-permute-done | bytes 98336 | tf_op jit(solution)/shard_map/ppermute | solution.py:375
  180.4 6.7 %all-to-all-done.2 = f32[16,48,256]{2,1,0:T(8,128)S(1)} async-done(((f32[16,48,256]{2,1,0:T(8,128)}), f32[16,48,256]{2,1,0:T(8,128)S(1)}, u32[]{:S(2)}, u32[]{:S(2)}) %all-to-all-start.2) | async-done | bytes 786464 | tf_op jit(solution)/shard_map/all_to_all | solution.py:369
  187.0 0.9 copy.39
  (87 shorter events, 10.4 us)
Async XLA Ops:
  2.0 10.2 %copy-start.7 = (f32[4,8,128]{2,1,0:T(8,128)}, f32[4,8,128]{2,1,0:T(8,128)S(1)}, u32[]{:S(2)}) copy-start(f32[4,8,128]{2,1,0:T(8,128)S(1)} %pad_maximum_fusion.own_pts) | copy-start | bytes 49156
  2.0 9.5 %collective-permute-start = (f32[4,8,128]{2,1,0:T(8,128)S(1)}, f32[4,8,128]{2,1,0:T(8,128)S(1)}, u32[]{:S(2)}, u32[]{:S(2)}) collective-permute-start(f32[4,8,128]{2,1,0:T(8,128)S(1)} %pad_maximum_fusion.own_pts), channel_id=1, source_target_pairs={{64,0},{65,1},{81,2},{80,3},{96,4},{97,5},{113,6},{112,7},{0,8},{1... | collective-permute-start | bytes 49160 | tf_op jit(solution)/shard_map/ppermute | solution.py:385
  6.0 6.2 %collective-permute-start.1 = (f32[4,8,128]{2,1,0:T(8,128)S(1)}, f32[4,8,128]{2,1,0:T(8,128)S(1)}, u32[]{:S(2)}, u32[]{:S(2)}) collective-permute-start(f32[4,8,128]{2,1,0:T(8,128)S(1)} %pad_maximum_fusion.own_pts), channel_id=1, source_target_pairs={{65,0},{64,1},{80,2},{81,3},{97,4},{96,5},{112,6},{113,7},{1,8},{0... | collective-permute-start | bytes 49160 | tf_op jit(solution)/shard_map/ppermute | solution.py:386
  11.5 0.7 copy-start.8
  12.2 0.6 copy-start.9
  22.8 57.7 %all-to-all-start = ((f32[16,104,256]{2,1,0:T(8,128)}), f32[16,104,256]{2,1,0:T(8,128)S(1)}, u32[]{:S(2)}, u32[]{:S(2)}) async-start(f32[16,104,256]{2,1,0:T(8,128)} %pair_rows.1), calls=%async_computation | async-start | bytes 3407872 | tf_op jit(solution)/shard_map/all_to_all | solution.py:369
  36.5 11.1 %collective-permute-start.7 = (f32[1,200,256]{2,1,0:T(8,128)}, f32[1,200,256]{2,1,0:T(8,128)S(1)}, u32[]{:S(2)}, u32[]{:S(2)}) collective-permute-start(f32[1,200,256]{2,1,0:T(8,128)} %get-tuple-element.28), channel_id=1, source_target_pairs={{0,16},{16,0},{32,48},{48,32},{64,80},{80,64},{96,112},{112,96},{1... | collective-permute-start | bytes 614408 | tf_op jit(solution)/shard_map/ppermute | solution.py:375
  37.9 97.0 %collective-permute-start.6 = (f32[768,256]{1,0:T(8,128)S(1)}, f32[768,256]{1,0:T(8,128)S(1)}, u32[]{:S(2)}, u32[]{:S(2)}) collective-permute-start(f32[768,256]{1,0:T(8,128)S(1)} %dynamic-slice_bitcast_fusion), channel_id=1, source_target_pairs={{0,0},{1,1},{16,2},{17,3},{36,4},{37,5},{52,6},{53,7},{72,8},{73,9... | collective-permute-start | bytes 2359304 | tf_op jit(solution)/shard_map/ppermute | solution.py:401
  39.4 32.3 %collective-permute-start.8 = (f32[1,200,256]{2,1,0:T(8,128)}, f32[1,200,256]{2,1,0:T(8,128)S(1)}, u32[]{:S(2)}, u32[]{:S(2)}) collective-permute-start(f32[1,200,256]{2,1,0:T(8,128)} %get-tuple-element.29), channel_id=1, source_target_pairs={{0,32},{16,48},{32,0},{48,16},{64,96},{80,112},{96,64},{112,80},{1... | collective-permute-start | bytes 614408 | tf_op jit(solution)/shard_map/ppermute | solution.py:375
  41.6 34.6 %collective-permute-start.9 = (f32[1,200,256]{2,1,0:T(8,128)}, f32[1,200,256]{2,1,0:T(8,128)S(1)}, u32[]{:S(2)}, u32[]{:S(2)}) collective-permute-start(f32[1,200,256]{2,1,0:T(8,128)} %get-tuple-element.30), channel_id=1, source_target_pairs={{0,48},{16,32},{32,16},{48,0},{64,112},{80,96},{96,80},{112,64},{1... | collective-permute-start | bytes 614408 | tf_op jit(solution)/shard_map/ppermute | solution.py:375
  45.8 45.4 %collective-permute-start.10 = (f32[1,200,256]{2,1,0:T(8,128)}, f32[1,200,256]{2,1,0:T(8,128)}, u32[]{:S(2)}, u32[]{:S(2)}) collective-permute-start(f32[1,200,256]{2,1,0:T(8,128)} %get-tuple-element.31), channel_id=1, source_target_pairs={{0,64},{16,80},{32,96},{48,112},{64,0},{80,16},{96,32},{112,48},{1... | collective-permute-start | bytes 614408 | tf_op jit(solution)/shard_map/ppermute | solution.py:375
  47.6 55.9 %copy-start.2 = (f32[1,200,256]{2,1,0:T(8,128)}, f32[1,200,256]{2,1,0:T(8,128)S(1)}, u32[]{:S(2)}) copy-start(f32[1,200,256]{2,1,0:T(8,128)S(1)} %collective-permute-done.7.refs_1_) | copy-start | bytes 614404
  47.6 44.2 %collective-permute-start.11 = (f32[1,200,256]{2,1,0:T(8,128)}, f32[1,200,256]{2,1,0:T(8,128)}, u32[]{:S(2)}, u32[]{:S(2)}) collective-permute-start(f32[1,200,256]{2,1,0:T(8,128)} %get-tuple-element.32), channel_id=1, source_target_pairs={{0,80},{16,64},{32,112},{48,96},{64,16},{80,0},{96,48},{112,32},{1... | collective-permute-start | bytes 614408 | tf_op jit(solution)/shard_map/ppermute | solution.py:375
  71.7 4.5 %copy-start.3 = (f32[1,200,256]{2,1,0:T(8,128)}, f32[1,200,256]{2,1,0:T(8,128)S(1)}, u32[]{:S(2)}) copy-start(f32[1,200,256]{2,1,0:T(8,128)S(1)} %collective-permute-done.8.refs_2_) | copy-start | bytes 614404
  71.7 37.7 %collective-permute-start.2 = (f32[384,256]{1,0:T(8,128)}, f32[384,256]{1,0:T(8,128)}, u32[]{:S(2)}, u32[]{:S(2)}) collective-permute-start(f32[384,256]{1,0:T(8,128)} %get-tuple-element.73), channel_id=1, source_target_pairs={{0,0},{16,17},{64,66},{80,83},{32,36},{48,53},{96,102},{112,119},{... | collective-permute-start | bytes 1179656 | tf_op jit(solution)/shard_map/ppermute | solution.py:398
  76.1 0.7 copy-start.4
  76.8 37.1 %collective-permute-start.4 = (f32[384,256]{1,0:T(8,128)}, f32[384,256]{1,0:T(8,128)}, u32[]{:S(2)}, u32[]{:S(2)}) collective-permute-start(f32[384,256]{1,0:T(8,128)} %get-tuple-element.72), channel_id=1, source_target_pairs={{64,64},{80,81},{0,2},{16,19},{96,100},{112,117},{32,38},{48,55},{... | collective-permute-start | bytes 1179656 | tf_op jit(solution)/shard_map/ppermute | solution.py:398
  80.5 1.2 copy-start
  84.9 55.8 %all-to-all-start.1 = ((f32[16,48,256]{2,1,0:T(8,128)}), f32[16,48,256]{2,1,0:T(8,128)S(1)}, u32[]{:S(2)}, u32[]{:S(2)}) async-start(f32[16,48,256]{2,1,0:T(8,128)} %add_arrived.2), calls=%async_computation.1 | async-start | bytes 1572864 | tf_op jit(solution)/shard_map/all_to_all | solution.py:369
  91.2 9.5 %collective-permute-start.12 = (f32[1,200,256]{2,1,0:T(8,128)}, f32[1,200,256]{2,1,0:T(8,128)S(1)}, u32[]{:S(2)}, u32[]{:S(2)}) collective-permute-start(f32[1,200,256]{2,1,0:T(8,128)} %get-tuple-element.33), channel_id=1, source_target_pairs={{0,96},{16,112},{32,64},{48,80},{64,32},{80,48},{96,0},{112,16},{1... | collective-permute-start | bytes 614408 | tf_op jit(solution)/shard_map/ppermute | solution.py:375
  91.8 10.9 %collective-permute-start.13 = (f32[1,200,256]{2,1,0:T(8,128)}, f32[1,200,256]{2,1,0:T(8,128)S(1)}, u32[]{:S(2)}, u32[]{:S(2)}) collective-permute-start(f32[1,200,256]{2,1,0:T(8,128)} %get-tuple-element.34), channel_id=1, source_target_pairs={{0,112},{16,96},{32,80},{48,64},{64,48},{80,32},{96,16},{112,0},{1... | collective-permute-start | bytes 614408 | tf_op jit(solution)/shard_map/ppermute | solution.py:375
  100.7 2.8 %copy-start.5 = (f32[1,200,256]{2,1,0:T(8,128)}, f32[1,200,256]{2,1,0:T(8,128)S(1)}, u32[]{:S(2)}) copy-start(f32[1,200,256]{2,1,0:T(8,128)S(1)} %collective-permute-done.12.refs_6_) | copy-start | bytes 614404
  102.7 0.8 copy-start.6
  106.7 10.9 %collective-permute-start.14 = (f32[1,96,256]{2,1,0:T(8,128)}, f32[1,96,256]{2,1,0:T(8,128)S(1)}, u32[]{:S(2)}, u32[]{:S(2)}) collective-permute-start(f32[1,96,256]{2,1,0:T(8,128)} %get-tuple-element.36), channel_id=1, source_target_pairs={{0,16},{16,0},{32,48},{48,32},{64,80},{80,64},{96,112},{112,96},{1... | collective-permute-start | bytes 294920 | tf_op jit(solution)/shard_map/ppermute | solution.py:375
  107.8 10.5 %collective-permute-start.15 = (f32[1,96,256]{2,1,0:T(8,128)}, f32[1,96,256]{2,1,0:T(8,128)S(1)}, u32[]{:S(2)}, u32[]{:S(2)}) collective-permute-start(f32[1,96,256]{2,1,0:T(8,128)} %get-tuple-element.37), channel_id=1, source_target_pairs={{0,32},{16,48},{32,0},{48,16},{64,96},{80,112},{96,64},{112,80},{1... | collective-permute-start | bytes 294920 | tf_op jit(solution)/shard_map/ppermute | solution.py:375
  109.4 31.3 %collective-permute-start.3 = (f32[384,256]{1,0:T(8,128)}, f32[384,256]{1,0:T(8,128)}, u32[]{:S(2)}, u32[]{:S(2)}) collective-permute-start(f32[384,256]{1,0:T(8,128)} %collective-permute-done.2), channel_id=1, source_target_pairs={{0,0},{17,1},{66,2},{83,3},{36,4},{53,5},{102,6},{119,7},{8,8},{25... | collective-permute-start | bytes 1179656 | tf_op jit(solution)/shard_map/ppermute | solution.py:399
  113.9 26.8 %collective-permute-start.5 = (f32[384,256]{1,0:T(8,128)}, f32[384,256]{1,0:T(8,128)}, u32[]{:S(2)}, u32[]{:S(2)}) collective-permute-start(f32[384,256]{1,0:T(8,128)} %collective-permute-done.4), channel_id=1, source_target_pairs={{64,0},{81,1},{2,2},{19,3},{100,4},{117,5},{38,6},{55,7},{72,8},{8... | collective-permute-start | bytes 1179656 | tf_op jit(solution)/shard_map/ppermute | solution.py:399
  117.6 11.9 %collective-permute-start.16 = (f32[1,96,256]{2,1,0:T(8,128)}, f32[1,96,256]{2,1,0:T(8,128)S(1)}, u32[]{:S(2)}, u32[]{:S(2)}) collective-permute-start(f32[1,96,256]{2,1,0:T(8,128)} %get-tuple-element.38), channel_id=1, source_target_pairs={{0,48},{16,32},{32,16},{48,0},{64,112},{80,96},{96,80},{112,64},{1... | collective-permute-start | bytes 294920 | tf_op jit(solution)/shard_map/ppermute | solution.py:375
  118.2 14.3 %collective-permute-start.17 = (f32[1,96,256]{2,1,0:T(8,128)}, f32[1,96,256]{2,1,0:T(8,128)S(1)}, u32[]{:S(2)}, u32[]{:S(2)}) collective-permute-start(f32[1,96,256]{2,1,0:T(8,128)} %get-tuple-element.39), channel_id=1, source_target_pairs={{0,64},{16,80},{32,96},{48,112},{64,0},{80,16},{96,32},{112,48},{1... | collective-permute-start | bytes 294920 | tf_op jit(solution)/shard_map/ppermute | solution.py:375
  129.5 11.2 %copy-start.10 = (f32[1,96,256]{2,1,0:T(8,128)}, f32[1,96,256]{2,1,0:T(8,128)S(1)}, u32[]{:S(2)}) copy-start(f32[1,96,256]{2,1,0:T(8,128)S(1)} %collective-permute-done.16) | copy-start | bytes 294916
  129.5 5.8 %collective-permute-start.18 = (f32[1,96,256]{2,1,0:T(8,128)}, f32[1,96,256]{2,1,0:T(8,128)S(1)}, u32[]{:S(2)}, u32[]{:S(2)}) collective-permute-start(f32[1,96,256]{2,1,0:T(8,128)} %get-tuple-element.40), channel_id=1, source_target_pairs={{0,80},{16,64},{32,112},{48,96},{64,16},{80,0},{96,48},{112,32},{1... | collective-permute-start | bytes 294920 | tf_op jit(solution)/shard_map/ppermute | solution.py:375
  132.5 2.4 %copy-start.11 = (f32[1,96,256]{2,1,0:T(8,128)}, f32[1,96,256]{2,1,0:T(8,128)S(1)}, u32[]{:S(2)}) copy-start(f32[1,96,256]{2,1,0:T(8,128)S(1)} %collective-permute-done.17) | copy-start | bytes 294916
  132.5 6.0 %collective-permute-start.19 = (f32[1,96,256]{2,1,0:T(8,128)}, f32[1,96,256]{2,1,0:T(8,128)S(1)}, u32[]{:S(2)}, u32[]{:S(2)}) collective-permute-start(f32[1,96,256]{2,1,0:T(8,128)} %get-tuple-element.41), channel_id=1, source_target_pairs={{0,96},{16,112},{32,64},{48,80},{64,32},{80,48},{96,0},{112,16},{1... | collective-permute-start | bytes 294920 | tf_op jit(solution)/shard_map/ppermute | solution.py:375
  134.9 5.8 %collective-permute-start.20 = (f32[1,96,256]{2,1,0:T(8,128)}, f32[1,96,256]{2,1,0:T(8,128)S(1)}, u32[]{:S(2)}, u32[]{:S(2)}) collective-permute-start(f32[1,96,256]{2,1,0:T(8,128)} %get-tuple-element.42), channel_id=1, source_target_pairs={{0,112},{16,96},{32,80},{48,64},{64,48},{80,32},{96,16},{112,0},{1... | collective-permute-start | bytes 294920 | tf_op jit(solution)/shard_map/ppermute | solution.py:375
  135.2 5.4 %copy-start.12 = (f32[1,96,256]{2,1,0:T(8,128)}, f32[1,96,256]{2,1,0:T(8,128)S(1)}, u32[]{:S(2)}) copy-start(f32[1,96,256]{2,1,0:T(8,128)S(1)} %collective-permute-done.18) | copy-start | bytes 294916
  138.6 2.1 %copy-start.13 = (f32[1,96,256]{2,1,0:T(8,128)}, f32[1,96,256]{2,1,0:T(8,128)S(1)}, u32[]{:S(2)}) copy-start(f32[1,96,256]{2,1,0:T(8,128)S(1)} %collective-permute-done.19) | copy-start | bytes 294916
  162.1 9.9 %collective-permute-start.21 = (f32[1,96,256]{2,1,0:T(8,128)S(1)}, f32[1,96,256]{2,1,0:T(8,128)S(1)}, u32[]{:S(2)}, u32[]{:S(2)}) collective-permute-start(f32[1,96,256]{2,1,0:T(8,128)S(1)} %get-tuple-element.57), channel_id=1, source_target_pairs={{0,16},{16,0},{32,48},{48,32},{64,80},{80,64},{96,112},{112,96},{1... | collective-permute-start | bytes 294920 | tf_op jit(solution)/shard_map/ppermute | solution.py:375
  162.1 11.9 %collective-permute-start.22 = (f32[1,96,256]{2,1,0:T(8,128)S(1)}, f32[1,96,256]{2,1,0:T(8,128)S(1)}, u32[]{:S(2)}, u32[]{:S(2)}) collective-permute-start(f32[1,96,256]{2,1,0:T(8,128)S(1)} %get-tuple-element.59), channel_id=1, source_target_pairs={{0,32},{16,48},{32,0},{48,16},{64,96},{80,112},{96,64},{112,80},{1... | collective-permute-start | bytes 294920 | tf_op jit(solution)/shard_map/ppermute | solution.py:375
  162.5 12.5 %collective-permute-start.23 = (f32[1,96,256]{2,1,0:T(8,128)S(1)}, f32[1,96,256]{2,1,0:T(8,128)S(1)}, u32[]{:S(2)}, u32[]{:S(2)}) collective-permute-start(f32[1,96,256]{2,1,0:T(8,128)S(1)} %get-tuple-element.61), channel_id=1, source_target_pairs={{0,48},{16,32},{32,16},{48,0},{64,112},{80,96},{96,80},{112,64},{1... | collective-permute-start | bytes 294920 | tf_op jit(solution)/shard_map/ppermute | solution.py:375
  164.0 11.1 %collective-permute-start.24 = (f32[1,96,256]{2,1,0:T(8,128)S(1)}, f32[1,96,256]{2,1,0:T(8,128)S(1)}, u32[]{:S(2)}, u32[]{:S(2)}) collective-permute-start(f32[1,96,256]{2,1,0:T(8,128)S(1)} %get-tuple-element.63), channel_id=1, source_target_pairs={{0,64},{16,80},{32,96},{48,112},{64,0},{80,16},{96,32},{112,48},{1... | collective-permute-start | bytes 294920 | tf_op jit(solution)/shard_map/ppermute | solution.py:375
  165.8 9.3 %collective-permute-start.25 = (f32[1,96,256]{2,1,0:T(8,128)S(1)}, f32[1,96,256]{2,1,0:T(8,128)S(1)}, u32[]{:S(2)}, u32[]{:S(2)}) collective-permute-start(f32[1,96,256]{2,1,0:T(8,128)S(1)} %get-tuple-element.65), channel_id=1, source_target_pairs={{0,80},{16,64},{32,112},{48,96},{64,16},{80,0},{96,48},{112,32},{1... | collective-permute-start | bytes 294920 | tf_op jit(solution)/shard_map/ppermute | solution.py:375
  167.1 19.9 %all-to-all-start.2 = ((f32[16,48,256]{2,1,0:T(8,128)}), f32[16,48,256]{2,1,0:T(8,128)S(1)}, u32[]{:S(2)}, u32[]{:S(2)}) async-start(f32[16,48,256]{2,1,0:T(8,128)} %bitcast.11), calls=%async_computation.2 | async-start | bytes 1572864 | tf_op jit(solution)/shard_map/all_to_all | solution.py:369
  172.0 6.2 %collective-permute-start.26 = (f32[1,96,256]{2,1,0:T(8,128)S(1)}, f32[1,96,256]{2,1,0:T(8,128)S(1)}, u32[]{:S(2)}, u32[]{:S(2)}) collective-permute-start(f32[1,96,256]{2,1,0:T(8,128)S(1)} %get-tuple-element.67), channel_id=1, source_target_pairs={{0,96},{16,112},{32,64},{48,80},{64,32},{80,48},{96,0},{112,16},{1... | collective-permute-start | bytes 294920 | tf_op jit(solution)/shard_map/ppermute | solution.py:375
  174.1 6.3 %collective-permute-start.27 = (f32[1,96,256]{2,1,0:T(8,128)S(1)}, f32[1,96,256]{2,1,0:T(8,128)S(1)}, u32[]{:S(2)}, u32[]{:S(2)}) collective-permute-start(f32[1,96,256]{2,1,0:T(8,128)S(1)} %get-tuple-element.69), channel_id=1, source_target_pairs={{0,112},{16,96},{32,80},{48,64},{64,48},{80,32},{96,16},{112,0},{1... | collective-permute-start | bytes 294920 | tf_op jit(solution)/shard_map/ppermute | solution.py:375
  180.4 7.5 %copy-start.1 = (f32[8,96,256]{2,1,0:T(8,128)}, f32[8,96,256]{2,1,0:T(8,128)S(1)}, u32[]{:S(2)}) copy-start(f32[8,96,256]{2,1,0:T(8,128)S(1)} %constant_dynamic-update-slice_fusion) | copy-start | bytes 2359300

commit v3 on v2

--- a/solution.py
+++ b/solution.py
@@ -46,13 +46,13 @@
     return near, far
 
 
-def omega_routes(turn):
+def omega_routes():
     inside, along = [], []
     for y in range(4):
         for core in range(2):
             for z in range(4):
                 for x in range(4):
-                    src_y = y ^ (2 * (x // 2) + z % 2) ^ turn
+                    src_y = y ^ (2 * (x // 2) + z % 2)
                     src_core = core ^ (x % 2)
                     middle = device(src_y, src_core, z, x)
                     inside.append((device(src_y, src_core, y, 2 * core + z // 2), middle))
@@ -209,42 +209,34 @@
     )(meta, own_pts, near_pts, far_pts, src)
 
 
-def add_kernel(ids, turn, *refs, cut, parts):
+def add_kernel(turn, *refs, cut, parts):
     arrived, outs, refs = refs[:parts], refs[parts : 2 * parts], refs[2 * parts :]
     if parts == 1:
         outs, refs = (), outs + refs
     out, stage, sems = refs[:3]
-    total = ids.shape[0] * SLOTS
-
-    def fetch(at, n):
-        k, slot = n // SLOTS, n % SLOTS
-        if parts == 1:
-            src = arrived[0].at[k, pl.ds(slot * cut, cut)]
-        else:
-            src = arrived[k].at[0, pl.ds(slot * cut, cut)]
-        return pltpu.make_async_copy(src, stage.at[at], sems.at[at])
-
-    for n in range(total):
-
-        @pl.when(ids[n // SLOTS, n % SLOTS] >= 0)
-        def _(n=n):
-            fetch(n, n).start()
-
+    total = stage.shape[0]
+    copies = [
+        pltpu.make_async_copy(arrived[0].at[k] if parts == 1 else arrived[k].at[0], stage.at[k], sems.at[k])
+        for k in range(total)
+    ]
+    for copy in copies:
+        copy.start()
     out[...] = jnp.zeros_like(out)
-    for n in range(total):
-
-        @pl.when(ids[n // SLOTS, n % SLOTS] >= 0)
-        def _(n=n):
-            fetch(n, n).wait()
-            out[ids[n // SLOTS, n % SLOTS] ^ turn[0]] += stage[n]
+    for k in range(total):
+        copies[k].wait()
+        tags = stage[k, SLOTS * cut : SLOTS * cut + TAG, :128]
+        for slot in range(SLOTS):
+            pick = jnp.max(tags[slot * (TAG // SLOTS) : (slot + 1) * (TAG // SLOTS)]).astype(jnp.int32)
+
+            @pl.when(pick >= 0)
+            def _(k=k, slot=slot, pick=pick):
+                out[pick ^ turn[0]] += stage[k, slot * cut : (slot + 1) * cut, :]
 
     send_out(out, outs, refs[3:])
 
 
 def add_arrived(arrived, turn, clusters, cut):
-    ids = [part[:, SLOTS * cut :: TAG // SLOTS, 0] for part in arrived]
-    ids = jnp.concatenate(ids, axis=0).astype(jnp.int32)
-    total = ids.shape[0] * SLOTS
+    total = sum(part.shape[0] for part in arrived)
     smem = pl.BlockSpec(memory_space=pltpu.SMEM)
     if len(arrived) > 1:
         shape = tuple(jax.ShapeDtypeStruct((1, cut, SK), F32) for _ in range(clusters))
@@ -256,12 +248,14 @@
     return pl.pallas_call(
         functools.partial(add_kernel, cut=cut, parts=len(arrived)),
         out_shape=shape,
-        in_specs=[smem, smem] + [pl.BlockSpec(memory_space=pltpu.HBM)] * len(arrived),
+        in_specs=[smem] + [pl.BlockSpec(memory_space=pltpu.HBM)] * len(arrived),
         out_specs=specs,
-        scratch_shapes=held + [pltpu.VMEM((total, cut, SK), F32), pltpu.SemaphoreType.DMA((total,))] + sems,
+        scratch_shapes=held
+        + [pltpu.VMEM((total, SLOTS * cut + TAG, SK), F32), pltpu.SemaphoreType.DMA((total,))]
+        + sems,
         cost_estimate=pl.CostEstimate(flops=1_000_000, bytes_accessed=3_000_000, transcendentals=0),
         name="add_arrived",
-    )(ids, turn.reshape(1), *arrived)
+    )(turn.reshape(1), *arrived)
 
 
 BLK = 64
@@ -303,19 +297,22 @@
     return jnp.concatenate(done, axis=0)[:, :BLK]
 
 
-def basis_kernel(turn, rows, self_high, self_low, self_cols, *refs):
+def basis_kernel(turn, rows, self_rows, self_cols, *refs):
     cols = refs[:NR]
-    out_rows, out_cols, (sk, gram, inverse, low_q) = refs[NR], refs[NR + 1 : 2 * NR + 1], refs[2 * NR + 1 :]
+    out_rows, out_cols = refs[NR], refs[NR + 1 : 2 * NR + 1]
+    sk, sk_high, sk_low, gram, inverse, low_q = refs[2 * NR + 1 :]
     n = SK // BLK
     dims0 = (((0,), (0,)), ((), ()))
-    half = HEIGHT // 2
-    sk[0, :half] = rows[:half] + self_high[...]
-    sk[0, half:] = rows[half:] + self_low[...]
+    sk[0] = rows[...] + self_rows[...]
     for k in range(NR):
         part = pl.ds(pl.multiple_of((k ^ turn[0]) * COL_CUT, COL_CUT), COL_CUT)
         sk[1, part, :] = cols[k][0] + self_cols[part, :]
     for w in range(2):
-        gram[w] = lax.dot_general(sk[w], sk[w], dims0, precision=HIGH, preferred_element_type=F32)
+        hi, lo = split(sk[w])
+        sk_high[w] = hi
+        sk_low[w] = lo
+        cross = lax.dot_general(sk_high[w], sk_low[w], dims0, preferred_element_type=F32)
+        gram[w] = lax.dot_general(sk_high[w], sk_high[w], dims0, preferred_element_type=F32) + (cross + cross.T)
         inverse[w] = jnp.zeros((SK, SK), F32)
     for k in range(n):
         here = slice(k * BLK, (k + 1) * BLK)
@@ -336,12 +333,19 @@
                     upper, inverse[w, here, : (k + 1) * BLK], dims0, precision=HIGH, preferred_element_type=F32
                 )
     dims1 = (((1,), (1,)), ((), ()))
-    q = lax.dot_general(sk[1], inverse[1], dims1, precision=HIGH, preferred_element_type=F32)
+
+    def product(w):
+        hi, lo = split(inverse[w])
+        q = lax.dot_general(sk_high[w], hi, dims1, preferred_element_type=F32)
+        q += lax.dot_general(sk_high[w], lo, dims1, preferred_element_type=F32)
+        return q + lax.dot_general(sk_low[w], hi, dims1, preferred_element_type=F32)
+
+    q = product(1)
     for g in range(NR):
         low_q[g ^ turn[0]] = q[g * COL_CUT : (g + 1) * COL_CUT]
     for k in range(NR):
         out_cols[k][0] = low_q[k]
-    out_rows[...] = lax.dot_general(sk[0], inverse[0], dims1, precision=HIGH, preferred_element_type=F32)
+    out_rows[...] = product(0)
 
 
 def bases(turn, rows, self_rows, cols, self_cols):
@@ -351,10 +355,12 @@
     return pl.pallas_call(
         basis_kernel,
         out_shape=(shape,) + (shape_c,) * NR,
-        in_specs=[pl.BlockSpec(memory_space=pltpu.SMEM)] + [vmem] * (4 + NR),
+        in_specs=[pl.BlockSpec(memory_space=pltpu.SMEM)] + [vmem] * (3 + NR),
         out_specs=(vmem,) * (NR + 1),
         scratch_shapes=[
             pltpu.VMEM((2, HEIGHT, SK), F32),
+            pltpu.VMEM((2, HEIGHT, SK), BF16),
+            pltpu.VMEM((2, HEIGHT, SK), BF16),
             pltpu.VMEM((2, SK, SK), F32),
             pltpu.VMEM((2, SK, SK), F32),
             pltpu.VMEM((NR, COL_CUT, SK), F32),
@@ -362,7 +368,7 @@
         compiler_params=pltpu.CompilerParams(vmem_limit_bytes=32 << 20),
         cost_estimate=pl.CostEstimate(flops=3_000_000_000, bytes_accessed=5_000_000, transcendentals=0),
         name="bases",
-    )(turn.reshape(1), rows, *self_rows, self_cols, *cols)
+    )(turn.reshape(1), rows, self_rows, self_cols, *cols)
 
 
 def trade(value, axis):
@@ -388,15 +394,10 @@
     src_y, src_core, src_z, src_x = row_at // 2, row_at % 2, col_at // 4, col_at % 4
     bits = src_z ^ src_y
     omega_pick = (bits % 2) * 4 + (bits // 2) * 2 + ((src_x // 2) ^ src_core)
-    half = HEIGHT // 2
-    self_rows = []
-    for h, turn in enumerate((0, 2)):
-        inside, along = omega_routes(turn)
-        pick = omega_pick ^ turn
-        weight = lax.dynamic_slice(self_weight, (pick, h * half), (1, half)).reshape(half, 1)
-        part = lax.dynamic_slice(omega, (pick, h * half, 0), (1, half, SK)).reshape(half, SK) * weight
-        part = lax.ppermute(part, BOTH, inside)
-        self_rows.append(lax.ppermute(part, BOTH, along))
+    inside, along = omega_routes()
+    weighted = omega[omega_pick] * self_weight[omega_pick][:, None]
+    weighted = lax.ppermute(weighted, BOTH, inside)
+    self_rows = lax.ppermute(weighted, BOTH, along)
     psi_pick = (src_x % 2) * 8 + ((src_z - src_y) % 4) * 2 + src_x // 2
     psi_here = lax.ppermute(psi[psi_pick], BOTH, psi_route())
     self_cols = psi_here * self_weight[row_at][:, None]

time: 190 us -> 195 us (1.026)
  starting transfers between devices: 71.3 us -> 105 us
  waiting for transfers between devices: 53.6 us -> 29.2 us
  local copies, waits for them, and re-layouts: 31.8 us -> 26.2 us
  Pallas kernels: 24.2 us -> 27.8 us
    ppermute x21, starting transfers between devices: 29.2 us -> 62.2 us  [swap_rows(): got.append(lax.ppermute(value[k], 'row', [(i, i ^ k) for i in range(NR)]))]
    ppermute x21, waiting for transfers between devices: 46.2 us -> 22.5 us  [swap_rows(): got.append(lax.ppermute(value[k], 'row', [(i, i ^ k) for i in range(NR)]))]
    pallas_call x2, Pallas kernels: 6.36 us -> 10 us  [add_arrived(): pl.pallas_call(functools.partial(add_kernel, cut=cut, parts=len(arrived))...]
    slice x9 -> x0, local copies, waits for them, and re-layouts: 3.54 us -> none  [add_arrived(): ids = [part[:, SLOTS * cut::TAG // SLOTS, 0] for part in arrived]]
    ppermute x4 -> x2, starting transfers between devices: 16.3 us -> 14.8 us  [the longest x1 7.41 us: level(): weighted = lax.ppermute(weighted, BOTH, inside)]
    unnamed x30 -> x28, local copies, waits for them, and re-layouts: 3.14 us -> 4.12 us
  transfers between devices with their start and end apart: 31 -> 29, of which waited for: 12 -> 11; matrix products, arithmetic and copies ran while one was open for 7% -> 3% of each run, Pallas kernels for 8% -> 9%
where the time goes in v3:
time: 195 us; the launch traced here: 193 us
  starting transfers between devices  105 us (54%)
  waiting for transfers between devices  29.2 us (15%)
  Pallas kernels  27.8 us (14%)
  local copies, waits for them, and re-layouts  26.2 us (13%)
  other arithmetic  4.39 us (2%)
    ppermute x21, starting transfers between devices, swap_rows(): got.append(lax.ppermute(value[k], 'row', [(i, i ^ k) for i in range(NR)]))  62.2 us
    ppermute x21, waiting for transfers between devices, swap_rows(): got.append(lax.ppermute(value[k], 'row', [(i, i ^ k) for i in range(NR)]))  22.5 us
    pallas_call x1, local copies, waits for them, and re-layouts, bases(): pl.pallas_call(basis_kernel, out_shape=(shape,) + (shape_c,) * NR, in_spe...  19.9 us
    all_to_all x3, starting transfers between devices, trade(): return lax.all_to_all(value, axis, split_axis=0, concat_axis=0, tiled=True)  18.7 us
    pallas_call x2, Pallas kernels, pair_terms(): pl.pallas_call(functools.partial(pair_kernel, cut=cut, turned=turned), ou...  17.8 us
    pallas_call x2, Pallas kernels, add_arrived(): pl.pallas_call(functools.partial(add_kernel, cut=cut, parts=len(arrived))...  10 us
    ppermute x1, starting transfers between devices, level(): weighted = lax.ppermute(weighted, BOTH, inside)  7.41 us
    ppermute x1, starting transfers between devices, level(): self_rows = lax.ppermute(weighted, BOTH, along)  7.4 us
  transfers between devices with their start and end apart: 29, of which 11 were waited for; matrix products, arithmetic and copies ran while one was open for 3% of the time, Pallas kernels for 9%

profile of v3, /device:TPU:0, one launch (start us, length us, event | category | flops | bytes accessed | tf_op | source)
XLA Modules:
  0.0 193.1 jit_solution(1040359995584812899)
XLA Ops:
  0.6 0.7 copy.10
  1.3 0.7 pad_maximum_fusion.own_pts
  2.0 4.0 %collective-permute-start = (f32[4,8,128]{2,1,0:T(8,128)S(1)}, f32[4,8,128]{2,1,0:T(8,128)S(1)}, u32[]{:S(2)}, u32[]{:S(2)}) collective-permute-start(f32[4,8,128]{2,1,0:T(8,128)S(1)} %pad_maximum_fusion.own_pts), channel_id=1, source_target_pairs={{64,0},{65,1},{81,2},{80,3},{96,4},{97,5},{113,6},{112,7},{0,8},{1... | collective-permute-start | bytes 49160 | tf_op jit(solution)/shard_map/ppermute | solution.py:391
  6.0 4.1 %collective-permute-start.1 = (f32[4,8,128]{2,1,0:T(8,128)S(1)}, f32[4,8,128]{2,1,0:T(8,128)S(1)}, u32[]{:S(2)}, u32[]{:S(2)}) collective-permute-start(f32[4,8,128]{2,1,0:T(8,128)S(1)} %pad_maximum_fusion.own_pts), channel_id=1, source_target_pairs={{65,0},{64,1},{80,2},{81,3},{97,4},{96,5},{112,6},{113,7},{1,8},{0... | collective-permute-start | bytes 49160 | tf_op jit(solution)/shard_map/ppermute | solution.py:392
  10.2 1.3 pad_add_fusion
  11.5 0.7 collective-permute-done.1.far_pts
  12.8 9.9 %pair_rows.1 = f32[16,104,256]{2,1,0:T(8,128)} custom-call(s32[3,2]{1,0:T(4,128)} %get-tuple-element.73.meta, f32[4,8,128]{2,1,0:T(8,128)} %copy-done.6, f32[4,8,128]{2,1,0:T(8,128)} %copy-done.7, f32[4,8,128]{2,1,0:T(8,128)} %copy-done.8, f32[8,768,256]{2,1,0:T(8,128)} %src.2), custom_call_target="tpu_custom_call" | custom-call | flops 2000000000 | bytes 4000000 | tf_op jit(solution)/shard_map/pair_rows/pallas_call | solution.py:191
  22.8 5.9 %all-to-all-start = ((f32[16,104,256]{2,1,0:T(8,128)}), f32[16,104,256]{2,1,0:T(8,128)S(1)}, u32[]{:S(2)}, u32[]{:S(2)}) async-start(f32[16,104,256]{2,1,0:T(8,128)} %pair_rows.1), calls=%async_computation | async-start | bytes 3407872 | tf_op jit(solution)/shard_map/all_to_all | solution.py:375
  28.7 0.8 dynamic-slice_reduce_fusion
  29.6 2.2 %bitcast_multiply_fusion = f32[768,256]{1,0:T(8,128)} fusion(f32[8,768,256]{2,1,0:T(8,128)} %src.2, s32[]{:T(128)S(6)} %select_n.86, f32[768]{0:T(1024)S(1)} %get-tuple-element.71), kind=kLoop, calls=%fused_computation | loop fusion | flops 196608 | bytes 1575940 | tf_op jit(solution)/shard_map/mul | solution.py:398
  31.7 7.4 %collective-permute-start.2 = (f32[768,256]{1,0:T(8,128)}, f32[768,256]{1,0:T(8,128)}, u32[]{:S(2)}, u32[]{:S(2)}) collective-permute-start(f32[768,256]{1,0:T(8,128)} %bitcast_multiply_fusion), channel_id=1, source_target_pairs={{0,0},{16,17},{64,66},{80,83},{32,36},{48,53},{96,102},{112,119},{... | collective-permute-start | bytes 2359304 | tf_op jit(solution)/shard_map/ppermute | solution.py:399
  39.2 1.2 dynamic-slice_bitcast_fusion
  40.3 0.7 collective-permute-start.4
  41.1 7.8 %pair_cols.1 = (f32[1,200,256]{2,1,0:T(8,128)}, f32[1,200,256]{2,1,0:T(8,128)}, f32[1,200,256]{2,1,0:T(8,128)}, f32[1,200,256]{2,1,0:T(8,128)}, f32[1,200,256]{2...) custom-call(s32[3,2]{1,0:T(4,128)} %get-tuple-element.72.meta, ...), custom_call_target="tpu_custom_call" | custom-call | flops 2000000000 | bytes 4000000 | tf_op jit(solution)/shard_map/pair_cols/pallas_call | solution.py:191
  48.9 4.8 %collective-permute-start.10 = (f32[1,200,256]{2,1,0:T(8,128)}, f32[1,200,256]{2,1,0:T(8,128)S(1)}, u32[]{:S(2)}, u32[]{:S(2)}) collective-permute-start(f32[1,200,256]{2,1,0:T(8,128)} %get-tuple-element.33), channel_id=1, source_target_pairs={{0,96},{16,112},{32,64},{48,80},{64,32},{80,48},{96,0},{112,16},{1... | collective-permute-start | bytes 614408 | tf_op jit(solution)/shard_map/ppermute | solution.py:381
  53.8 7.4 %collective-permute-start.3 = (f32[768,256]{1,0:T(8,128)}, f32[768,256]{1,0:T(8,128)}, u32[]{:S(2)}, u32[]{:S(2)}) collective-permute-start(f32[768,256]{1,0:T(8,128)} %collective-permute-done.2), channel_id=1, source_target_pairs={{0,0},{17,1},{66,2},{83,3},{36,4},{53,5},{102,6},{119,7},{8,8},{25... | collective-permute-start | bytes 2359304 | tf_op jit(solution)/shard_map/ppermute | solution.py:400
  61.2 26.4 %collective-permute-start.11 = (f32[1,200,256]{2,1,0:T(8,128)}, f32[1,200,256]{2,1,0:T(8,128)}, u32[]{:S(2)}, u32[]{:S(2)}) collective-permute-start(f32[1,200,256]{2,1,0:T(8,128)} %get-tuple-element.34), channel_id=1, source_target_pairs={{0,112},{16,96},{32,80},{48,64},{64,48},{80,32},{96,16},{112,0},{1... | collective-permute-start | bytes 614408 | tf_op jit(solution)/shard_map/ppermute | solution.py:381
  87.6 5.5 %collective-permute-start.5 = (f32[1,200,256]{2,1,0:T(8,128)}, f32[1,200,256]{2,1,0:T(8,128)}, u32[]{:S(2)}, u32[]{:S(2)}) collective-permute-start(f32[1,200,256]{2,1,0:T(8,128)} %get-tuple-element.28), channel_id=1, source_target_pairs={{0,16},{16,0},{32,48},{48,32},{64,80},{80,64},{96,112},{112,96},{1... | collective-permute-start | bytes 614408 | tf_op jit(solution)/shard_map/ppermute | solution.py:381
  93.2 1.2 copy-done
  94.4 6.0 %add_arrived.2 = f32[16,48,256]{2,1,0:T(8,128)} custom-call(s32[1]{0:T(128)} %constant.92.clone.1.turn, f32[16,104,256]{2,1,0:T(8,128)} %copy-done), custom_call_target="tpu_custom_call" | custom-call | flops 1000000 | bytes 3000000 | tf_op jit(solution)/shard_map/add_arrived/pallas_call | solution.py:248
  100.4 3.6 %all-to-all-start.1 = ((f32[16,48,256]{2,1,0:T(8,128)}), f32[16,48,256]{2,1,0:T(8,128)S(1)}, u32[]{:S(2)}, u32[]{:S(2)}) async-start(f32[16,48,256]{2,1,0:T(8,128)} %add_arrived.2), calls=%async_computation.1 | async-start | bytes 1572864 | tf_op jit(solution)/shard_map/all_to_all | solution.py:375
  104.0 1.5 collective-permute-start.7
  105.6 3.5 %collective-permute-start.9 = (f32[1,200,256]{2,1,0:T(8,128)}, f32[1,200,256]{2,1,0:T(8,128)S(1)}, u32[]{:S(2)}, u32[]{:S(2)}) collective-permute-start(f32[1,200,256]{2,1,0:T(8,128)} %get-tuple-element.32), channel_id=1, source_target_pairs={{0,80},{16,64},{32,112},{48,96},{64,16},{80,0},{96,48},{112,32},{1... | collective-permute-start | bytes 614408 | tf_op jit(solution)/shard_map/ppermute | solution.py:381
  109.1 2.1 %collective-permute-done.7.refs_3_ = f32[1,200,256]{2,1,0:T(8,128)S(1)} collective-permute-done((f32[1,200,256]{2,1,0:T(8,128)}, f32[1,200,256]{2,1,0:T(8,128)S(1)}, u32[]{:S(2)}, u32[]{:S(2)}) %collective-permute-start.7) | collective-permute-done | bytes 204832 | tf_op jit(solution)/shard_map/ppermute | solution.py:381
  111.2 4.9 %collective-permute-done.8.refs_4_ = f32[1,200,256]{2,1,0:T(8,128)S(1)} collective-permute-done((f32[1,200,256]{2,1,0:T(8,128)}, f32[1,200,256]{2,1,0:T(8,128)S(1)}, u32[]{:S(2)}, u32[]{:S(2)}) %collective-permute-start.8) | collective-permute-done | bytes 204832 | tf_op jit(solution)/shard_map/ppermute | solution.py:381
  116.1 3.9 %collective-permute-done.9.refs_5_ = f32[1,200,256]{2,1,0:T(8,128)S(1)} collective-permute-done((f32[1,200,256]{2,1,0:T(8,128)}, f32[1,200,256]{2,1,0:T(8,128)S(1)}, u32[]{:S(2)}, u32[]{:S(2)}) %collective-permute-start.9) | collective-permute-done | bytes 204832 | tf_op jit(solution)/shard_map/ppermute | solution.py:381
  120.0 0.7 copy-done.5
  120.7 4.0 %add_arrived.3 = (f32[1,96,256]{2,1,0:T(8,128)}, f32[1,96,256]{2,1,0:T(8,128)}, f32[1,96,256]{2,1,0:T(8,128)}, f32[1,96,256]{2,1,0:T(8,128)}, f32[1,96,256]{2,1,...) custom-call(s32[1]{0:T(128)} %bitcast.turn, ...), custom_call_target="tpu_custom_call" | custom-call | flops 1000000 | bytes 3000000 | tf_op jit(solution)/shard_map/add_arrived/pallas_call | solution.py:248
  125.0 0.9 collective-permute-start.13
  125.9 0.8 collective-permute-start.14
  126.7 3.9 %collective-permute-start.15 = (f32[1,96,256]{2,1,0:T(8,128)}, f32[1,96,256]{2,1,0:T(8,128)S(1)}, u32[]{:S(2)}, u32[]{:S(2)}) collective-permute-start(f32[1,96,256]{2,1,0:T(8,128)} %get-tuple-element.39), channel_id=1, source_target_pairs={{0,64},{16,80},{32,96},{48,112},{64,0},{80,16},{96,32},{112,48},{1... | collective-permute-start | bytes 294920 | tf_op jit(solution)/shard_map/ppermute | solution.py:381
  130.9 2.4 %collective-permute-start.16 = (f32[1,96,256]{2,1,0:T(8,128)}, f32[1,96,256]{2,1,0:T(8,128)S(1)}, u32[]{:S(2)}, u32[]{:S(2)}) collective-permute-start(f32[1,96,256]{2,1,0:T(8,128)} %get-tuple-element.40), channel_id=1, source_target_pairs={{0,80},{16,64},{32,112},{48,96},{64,16},{80,0},{96,48},{112,32},{1... | collective-permute-start | bytes 294920 | tf_op jit(solution)/shard_map/ppermute | solution.py:381
  133.3 1.7 collective-permute-start.17
  135.0 2.4 %collective-permute-start.18 = (f32[1,96,256]{2,1,0:T(8,128)}, f32[1,96,256]{2,1,0:T(8,128)S(1)}, u32[]{:S(2)}, u32[]{:S(2)}) collective-permute-start(f32[1,96,256]{2,1,0:T(8,128)} %get-tuple-element.42), channel_id=1, source_target_pairs={{0,112},{16,96},{32,80},{48,64},{64,48},{80,32},{96,16},{112,0},{1... | collective-permute-start | bytes 294920 | tf_op jit(solution)/shard_map/ppermute | solution.py:381
  137.6 0.8 collective-permute-done.16
  138.4 2.4 %collective-permute-done.17 = f32[1,96,256]{2,1,0:T(8,128)S(1)} collective-permute-done((f32[1,96,256]{2,1,0:T(8,128)}, f32[1,96,256]{2,1,0:T(8,128)S(1)}, u32[]{:S(2)}, u32[]{:S(2)}) %collective-permute-start.17) | collective-permute-done | bytes 98336 | tf_op jit(solution)/shard_map/ppermute | solution.py:381
  140.7 2.2 %collective-permute-done.18 = f32[1,96,256]{2,1,0:T(8,128)S(1)} collective-permute-done((f32[1,96,256]{2,1,0:T(8,128)}, f32[1,96,256]{2,1,0:T(8,128)S(1)}, u32[]{:S(2)}, u32[]{:S(2)}) %collective-permute-start.18) | collective-permute-done | bytes 98336 | tf_op jit(solution)/shard_map/ppermute | solution.py:381
  143.1 19.9 %bases.1 = (f32[8,96,256]{2,1,0:T(8,128)S(1)}, f32[768,256]{1,0:T(8,128)}, f32[1,96,256]{2,1,0:T(8,128)S(1)}, f32[1,96,256]{2,1,0:T(8,128)S(1)}, f32[1,96,256]{2...) fusion(f32[8,96,256]{2,1,0:T(8,128)S(1)} %broadcast_in_dim.12, ...), kind=kCustom, calls=%fused_computation.14 | custom fusion | bytes 4718600 | tf_op jit(solution)/shard_map/bases/pallas_call | solution.py:355
  162.9 1.2 collective-permute-start.20
  164.1 0.7 collective-permute-start.21
  164.8 2.0 %collective-permute-start.22 = (f32[1,96,256]{2,1,0:T(8,128)S(1)}, f32[1,96,256]{2,1,0:T(8,128)S(1)}, u32[]{:S(2)}, u32[]{:S(2)}) collective-permute-start(f32[1,96,256]{2,1,0:T(8,128)S(1)} %get-tuple-element.63), channel_id=1, source_target_pairs={{0,64},{16,80},{32,96},{48,112},{64,0},{80,16},{96,32},{112,48},{1... | collective-permute-start | bytes 294920 | tf_op jit(solution)/shard_map/ppermute | solution.py:381
  166.8 1.2 collective-permute-start.23
  167.9 9.2 %all-to-all-start.2 = ((f32[16,48,256]{2,1,0:T(8,128)}), f32[16,48,256]{2,1,0:T(8,128)S(1)}, u32[]{:S(2)}, u32[]{:S(2)}) async-start(f32[16,48,256]{2,1,0:T(8,128)} %bitcast.9), calls=%async_computation.2 | async-start | bytes 1572864 | tf_op jit(solution)/shard_map/all_to_all | solution.py:375
  177.2 2.7 %collective-permute-start.24 = (f32[1,96,256]{2,1,0:T(8,128)S(1)}, f32[1,96,256]{2,1,0:T(8,128)S(1)}, u32[]{:S(2)}, u32[]{:S(2)}) collective-permute-start(f32[1,96,256]{2,1,0:T(8,128)S(1)} %get-tuple-element.67), channel_id=1, source_target_pairs={{0,96},{16,112},{32,64},{48,80},{64,32},{80,48},{96,0},{112,16},{1... | collective-permute-start | bytes 294920 | tf_op jit(solution)/shard_map/ppermute | solution.py:381
  180.3 3.1 %collective-permute-done.24 = f32[1,96,256]{2,1,0:T(8,128)S(1)} collective-permute-done((f32[1,96,256]{2,1,0:T(8,128)S(1)}, f32[1,96,256]{2,1,0:T(8,128)S(1)}, u32[]{:S(2)}, u32[]{:S(2)}) %collective-permute-start.24) | collective-permute-done | bytes 98336 | tf_op jit(solution)/shard_map/ppermute | solution.py:381
  183.4 2.8 %collective-permute-done.25 = f32[1,96,256]{2,1,0:T(8,128)S(1)} collective-permute-done((f32[1,96,256]{2,1,0:T(8,128)S(1)}, f32[1,96,256]{2,1,0:T(8,128)S(1)}, u32[]{:S(2)}, u32[]{:S(2)}) %collective-permute-start.25) | collective-permute-done | bytes 98336 | tf_op jit(solution)/shard_map/ppermute | solution.py:381
  186.2 5.9 %all-to-all-done.2 = f32[16,48,256]{2,1,0:T(8,128)S(1)} async-done(((f32[16,48,256]{2,1,0:T(8,128)}), f32[16,48,256]{2,1,0:T(8,128)S(1)}, u32[]{:S(2)}, u32[]{:S(2)}) %all-to-all-start.2) | async-done | bytes 786464 | tf_op jit(solution)/shard_map/all_to_all | solution.py:375
  192.2 0.9 copy.20
  (58 shorter events, 2.1 us)
Async XLA Ops:
  2.0 10.2 %copy-start.6 = (f32[4,8,128]{2,1,0:T(8,128)}, f32[4,8,128]{2,1,0:T(8,128)S(1)}, u32[]{:S(2)}) copy-start(f32[4,8,128]{2,1,0:T(8,128)S(1)} %pad_maximum_fusion.own_pts) | copy-start | bytes 49156
  2.0 9.5 %collective-permute-start = (f32[4,8,128]{2,1,0:T(8,128)S(1)}, f32[4,8,128]{2,1,0:T(8,128)S(1)}, u32[]{:S(2)}, u32[]{:S(2)}) collective-permute-start(f32[4,8,128]{2,1,0:T(8,128)S(1)} %pad_maximum_fusion.own_pts), channel_id=1, source_target_pairs={{64,0},{65,1},{81,2},{80,3},{96,4},{97,5},{113,6},{112,7},{0,8},{1... | collective-permute-start | bytes 49160 | tf_op jit(solution)/shard_map/ppermute | solution.py:391
  6.0 6.2 %collective-permute-start.1 = (f32[4,8,128]{2,1,0:T(8,128)S(1)}, f32[4,8,128]{2,1,0:T(8,128)S(1)}, u32[]{:S(2)}, u32[]{:S(2)}) collective-permute-start(f32[4,8,128]{2,1,0:T(8,128)S(1)} %pad_maximum_fusion.own_pts), channel_id=1, source_target_pairs={{65,0},{64,1},{80,2},{81,3},{97,4},{96,5},{112,6},{113,7},{1,8},{0... | collective-permute-start | bytes 49160 | tf_op jit(solution)/shard_map/ppermute | solution.py:392
  11.5 0.7 copy-start.7
  12.2 0.6 copy-start.8
  22.8 70.4 %all-to-all-start = ((f32[16,104,256]{2,1,0:T(8,128)}), f32[16,104,256]{2,1,0:T(8,128)S(1)}, u32[]{:S(2)}, u32[]{:S(2)}) async-start(f32[16,104,256]{2,1,0:T(8,128)} %pair_rows.1), calls=%async_computation | async-start | bytes 3407872 | tf_op jit(solution)/shard_map/all_to_all | solution.py:375
  31.7 22.0 %collective-permute-start.2 = (f32[768,256]{1,0:T(8,128)}, f32[768,256]{1,0:T(8,128)}, u32[]{:S(2)}, u32[]{:S(2)}) collective-permute-start(f32[768,256]{1,0:T(8,128)} %bitcast_multiply_fusion), channel_id=1, source_target_pairs={{0,0},{16,17},{64,66},{80,83},{32,36},{48,53},{96,102},{112,119},{... | collective-permute-start | bytes 2359304 | tf_op jit(solution)/shard_map/ppermute | solution.py:399
  40.3 94.7 %collective-permute-start.4 = (f32[768,256]{1,0:T(8,128)S(1)}, f32[768,256]{1,0:T(8,128)S(1)}, u32[]{:S(2)}, u32[]{:S(2)}) collective-permute-start(f32[768,256]{1,0:T(8,128)S(1)} %dynamic-slice_bitcast_fusion), channel_id=1, source_target_pairs={{0,0},{1,1},{16,2},{17,3},{36,4},{37,5},{52,6},{53,7},{72,8},{73,9... | collective-permute-start | bytes 2359304 | tf_op jit(solution)/shard_map/ppermute | solution.py:402
  48.9 44.2 %collective-permute-start.10 = (f32[1,200,256]{2,1,0:T(8,128)}, f32[1,200,256]{2,1,0:T(8,128)S(1)}, u32[]{:S(2)}, u32[]{:S(2)}) collective-permute-start(f32[1,200,256]{2,1,0:T(8,128)} %get-tuple-element.33), channel_id=1, source_target_pairs={{0,96},{16,112},{32,64},{48,80},{64,32},{80,48},{96,0},{112,16},{1... | collective-permute-start | bytes 614408 | tf_op jit(solution)/shard_map/ppermute | solution.py:381
  53.8 89.2 %collective-permute-start.3 = (f32[768,256]{1,0:T(8,128)}, f32[768,256]{1,0:T(8,128)}, u32[]{:S(2)}, u32[]{:S(2)}) collective-permute-start(f32[768,256]{1,0:T(8,128)} %collective-permute-done.2), channel_id=1, source_target_pairs={{0,0},{17,1},{66,2},{83,3},{36,4},{53,5},{102,6},{119,7},{8,8},{25... | collective-permute-start | bytes 2359304 | tf_op jit(solution)/shard_map/ppermute | solution.py:400
  61.2 42.9 %collective-permute-start.11 = (f32[1,200,256]{2,1,0:T(8,128)}, f32[1,200,256]{2,1,0:T(8,128)}, u32[]{:S(2)}, u32[]{:S(2)}) collective-permute-start(f32[1,200,256]{2,1,0:T(8,128)} %get-tuple-element.34), channel_id=1, source_target_pairs={{0,112},{16,96},{32,80},{48,64},{64,48},{80,32},{96,16},{112,0},{1... | collective-permute-start | bytes 614408 | tf_op jit(solution)/shard_map/ppermute | solution.py:381
  87.6 17.9 %collective-permute-start.5 = (f32[1,200,256]{2,1,0:T(8,128)}, f32[1,200,256]{2,1,0:T(8,128)}, u32[]{:S(2)}, u32[]{:S(2)}) collective-permute-start(f32[1,200,256]{2,1,0:T(8,128)} %get-tuple-element.28), channel_id=1, source_target_pairs={{0,16},{16,0},{32,48},{48,32},{64,80},{80,64},{96,112},{112,96},{1... | collective-permute-start | bytes 614408 | tf_op jit(solution)/shard_map/ppermute | solution.py:381
  93.1 26.9 %copy-start.2 = (f32[1,200,256]{2,1,0:T(8,128)}, f32[1,200,256]{2,1,0:T(8,128)S(1)}, u32[]{:S(2)}) copy-start(f32[1,200,256]{2,1,0:T(8,128)S(1)} %collective-permute-done.10.refs_6_) | copy-start | bytes 614404
  93.1 12.5 %collective-permute-start.6 = (f32[1,200,256]{2,1,0:T(8,128)}, f32[1,200,256]{2,1,0:T(8,128)}, u32[]{:S(2)}, u32[]{:S(2)}) collective-permute-start(f32[1,200,256]{2,1,0:T(8,128)} %get-tuple-element.29), channel_id=1, source_target_pairs={{0,32},{16,48},{32,0},{48,16},{64,96},{80,112},{96,64},{112,80},{1... | collective-permute-start | bytes 614408 | tf_op jit(solution)/shard_map/ppermute | solution.py:381
  93.2 1.2 copy-start
  100.4 42.6 %all-to-all-start.1 = ((f32[16,48,256]{2,1,0:T(8,128)}), f32[16,48,256]{2,1,0:T(8,128)S(1)}, u32[]{:S(2)}, u32[]{:S(2)}) async-start(f32[16,48,256]{2,1,0:T(8,128)} %add_arrived.2), calls=%async_computation.1 | async-start | bytes 1572864 | tf_op jit(solution)/shard_map/all_to_all | solution.py:375
  104.0 7.2 %collective-permute-start.7 = (f32[1,200,256]{2,1,0:T(8,128)}, f32[1,200,256]{2,1,0:T(8,128)S(1)}, u32[]{:S(2)}, u32[]{:S(2)}) collective-permute-start(f32[1,200,256]{2,1,0:T(8,128)} %get-tuple-element.30), channel_id=1, source_target_pairs={{0,48},{16,32},{32,16},{48,0},{64,112},{80,96},{96,80},{112,64},{1... | collective-permute-start | bytes 614408 | tf_op jit(solution)/shard_map/ppermute | solution.py:381
  105.5 10.6 %collective-permute-start.8 = (f32[1,200,256]{2,1,0:T(8,128)}, f32[1,200,256]{2,1,0:T(8,128)S(1)}, u32[]{:S(2)}, u32[]{:S(2)}) collective-permute-start(f32[1,200,256]{2,1,0:T(8,128)} %get-tuple-element.31), channel_id=1, source_target_pairs={{0,64},{16,80},{32,96},{48,112},{64,0},{80,16},{96,32},{112,48},{1... | collective-permute-start | bytes 614408 | tf_op jit(solution)/shard_map/ppermute | solution.py:381
  105.6 14.4 %collective-permute-start.9 = (f32[1,200,256]{2,1,0:T(8,128)}, f32[1,200,256]{2,1,0:T(8,128)S(1)}, u32[]{:S(2)}, u32[]{:S(2)}) collective-permute-start(f32[1,200,256]{2,1,0:T(8,128)} %get-tuple-element.32), channel_id=1, source_target_pairs={{0,80},{16,64},{32,112},{48,96},{64,16},{80,0},{96,48},{112,32},{1... | collective-permute-start | bytes 614408 | tf_op jit(solution)/shard_map/ppermute | solution.py:381
  111.2 8.8 %copy-start.3 = (f32[1,200,256]{2,1,0:T(8,128)}, f32[1,200,256]{2,1,0:T(8,128)S(1)}, u32[]{:S(2)}) copy-start(f32[1,200,256]{2,1,0:T(8,128)S(1)} %collective-permute-done.7.refs_3_) | copy-start | bytes 614404
  116.1 3.9 %copy-start.4 = (f32[1,200,256]{2,1,0:T(8,128)}, f32[1,200,256]{2,1,0:T(8,128)S(1)}, u32[]{:S(2)}) copy-start(f32[1,200,256]{2,1,0:T(8,128)S(1)} %collective-permute-done.8.refs_4_) | copy-start | bytes 614404
  120.0 0.7 copy-start.5
  124.7 1.9 %collective-permute-start.12 = (f32[1,96,256]{2,1,0:T(8,128)}, f32[1,96,256]{2,1,0:T(8,128)S(1)}, u32[]{:S(2)}, u32[]{:S(2)}) collective-permute-start(f32[1,96,256]{2,1,0:T(8,128)} %get-tuple-element.36), channel_id=1, source_target_pairs={{0,16},{16,0},{32,48},{48,32},{64,80},{80,64},{96,112},{112,96},{1... | collective-permute-start | bytes 294920 | tf_op jit(solution)/shard_map/ppermute | solution.py:381
  125.0 5.9 %collective-permute-start.13 = (f32[1,96,256]{2,1,0:T(8,128)}, f32[1,96,256]{2,1,0:T(8,128)S(1)}, u32[]{:S(2)}, u32[]{:S(2)}) collective-permute-start(f32[1,96,256]{2,1,0:T(8,128)} %get-tuple-element.37), channel_id=1, source_target_pairs={{0,32},{16,48},{32,0},{48,16},{64,96},{80,112},{96,64},{112,80},{1... | collective-permute-start | bytes 294920 | tf_op jit(solution)/shard_map/ppermute | solution.py:381
  125.9 7.4 %collective-permute-start.14 = (f32[1,96,256]{2,1,0:T(8,128)}, f32[1,96,256]{2,1,0:T(8,128)S(1)}, u32[]{:S(2)}, u32[]{:S(2)}) collective-permute-start(f32[1,96,256]{2,1,0:T(8,128)} %get-tuple-element.38), channel_id=1, source_target_pairs={{0,48},{16,32},{32,16},{48,0},{64,112},{80,96},{96,80},{112,64},{1... | collective-permute-start | bytes 294920 | tf_op jit(solution)/shard_map/ppermute | solution.py:381
  126.7 10.9 %collective-permute-start.15 = (f32[1,96,256]{2,1,0:T(8,128)}, f32[1,96,256]{2,1,0:T(8,128)S(1)}, u32[]{:S(2)}, u32[]{:S(2)}) collective-permute-start(f32[1,96,256]{2,1,0:T(8,128)} %get-tuple-element.39), channel_id=1, source_target_pairs={{0,64},{16,80},{32,96},{48,112},{64,0},{80,16},{96,32},{112,48},{1... | collective-permute-start | bytes 294920 | tf_op jit(solution)/shard_map/ppermute | solution.py:381
  130.9 7.5 %collective-permute-start.16 = (f32[1,96,256]{2,1,0:T(8,128)}, f32[1,96,256]{2,1,0:T(8,128)S(1)}, u32[]{:S(2)}, u32[]{:S(2)}) collective-permute-start(f32[1,96,256]{2,1,0:T(8,128)} %get-tuple-element.40), channel_id=1, source_target_pairs={{0,80},{16,64},{32,112},{48,96},{64,16},{80,0},{96,48},{112,32},{1... | collective-permute-start | bytes 294920 | tf_op jit(solution)/shard_map/ppermute | solution.py:381
  133.3 4.1 %copy-start.9 = (f32[1,96,256]{2,1,0:T(8,128)}, f32[1,96,256]{2,1,0:T(8,128)S(1)}, u32[]{:S(2)}) copy-start(f32[1,96,256]{2,1,0:T(8,128)S(1)} %collective-permute-done.14) | copy-start | bytes 294916
  133.3 7.4 %collective-permute-start.17 = (f32[1,96,256]{2,1,0:T(8,128)}, f32[1,96,256]{2,1,0:T(8,128)S(1)}, u32[]{:S(2)}, u32[]{:S(2)}) collective-permute-start(f32[1,96,256]{2,1,0:T(8,128)} %get-tuple-element.41), channel_id=1, source_target_pairs={{0,96},{16,112},{32,64},{48,80},{64,32},{80,48},{96,0},{112,16},{1... | collective-permute-start | bytes 294920 | tf_op jit(solution)/shard_map/ppermute | solution.py:381
  135.0 7.9 %collective-permute-start.18 = (f32[1,96,256]{2,1,0:T(8,128)}, f32[1,96,256]{2,1,0:T(8,128)S(1)}, u32[]{:S(2)}, u32[]{:S(2)}) collective-permute-start(f32[1,96,256]{2,1,0:T(8,128)} %get-tuple-element.42), channel_id=1, source_target_pairs={{0,112},{16,96},{32,80},{48,64},{64,48},{80,32},{96,16},{112,0},{1... | collective-permute-start | bytes 294920 | tf_op jit(solution)/shard_map/ppermute | solution.py:381
  137.6 5.4 %copy-start.10 = (f32[1,96,256]{2,1,0:T(8,128)}, f32[1,96,256]{2,1,0:T(8,128)S(1)}, u32[]{:S(2)}) copy-start(f32[1,96,256]{2,1,0:T(8,128)S(1)} %collective-permute-done.15) | copy-start | bytes 294916
  138.3 4.6 %copy-start.11 = (f32[1,96,256]{2,1,0:T(8,128)}, f32[1,96,256]{2,1,0:T(8,128)S(1)}, u32[]{:S(2)}) copy-start(f32[1,96,256]{2,1,0:T(8,128)S(1)} %collective-permute-done.16) | copy-start | bytes 294916
  140.7 2.2 %copy-start.12 = (f32[1,96,256]{2,1,0:T(8,128)}, f32[1,96,256]{2,1,0:T(8,128)S(1)}, u32[]{:S(2)}) copy-start(f32[1,96,256]{2,1,0:T(8,128)S(1)} %collective-permute-done.17) | copy-start | bytes 294916
  162.9 14.2 %collective-permute-start.19 = (f32[1,96,256]{2,1,0:T(8,128)S(1)}, f32[1,96,256]{2,1,0:T(8,128)S(1)}, u32[]{:S(2)}, u32[]{:S(2)}) collective-permute-start(f32[1,96,256]{2,1,0:T(8,128)S(1)} %get-tuple-element.57), channel_id=1, source_target_pairs={{0,16},{16,0},{32,48},{48,32},{64,80},{80,64},{96,112},{112,96},{1... | collective-permute-start | bytes 294920 | tf_op jit(solution)/shard_map/ppermute | solution.py:381
  162.9 16.9 %collective-permute-start.20 = (f32[1,96,256]{2,1,0:T(8,128)S(1)}, f32[1,96,256]{2,1,0:T(8,128)S(1)}, u32[]{:S(2)}, u32[]{:S(2)}) collective-permute-start(f32[1,96,256]{2,1,0:T(8,128)S(1)} %get-tuple-element.59), channel_id=1, source_target_pairs={{0,32},{16,48},{32,0},{48,16},{64,96},{80,112},{96,64},{112,80},{1... | collective-permute-start | bytes 294920 | tf_op jit(solution)/shard_map/ppermute | solution.py:381
  164.1 16.0 %collective-permute-start.21 = (f32[1,96,256]{2,1,0:T(8,128)S(1)}, f32[1,96,256]{2,1,0:T(8,128)S(1)}, u32[]{:S(2)}, u32[]{:S(2)}) collective-permute-start(f32[1,96,256]{2,1,0:T(8,128)S(1)} %get-tuple-element.61), channel_id=1, source_target_pairs={{0,48},{16,32},{32,16},{48,0},{64,112},{80,96},{96,80},{112,64},{1... | collective-permute-start | bytes 294920 | tf_op jit(solution)/shard_map/ppermute | solution.py:381
  164.8 15.4 %collective-permute-start.22 = (f32[1,96,256]{2,1,0:T(8,128)S(1)}, f32[1,96,256]{2,1,0:T(8,128)S(1)}, u32[]{:S(2)}, u32[]{:S(2)}) collective-permute-start(f32[1,96,256]{2,1,0:T(8,128)S(1)} %get-tuple-element.63), channel_id=1, source_target_pairs={{0,64},{16,80},{32,96},{48,112},{64,0},{80,16},{96,32},{112,48},{1... | collective-permute-start | bytes 294920 | tf_op jit(solution)/shard_map/ppermute | solution.py:381
  166.8 13.5 %collective-permute-start.23 = (f32[1,96,256]{2,1,0:T(8,128)S(1)}, f32[1,96,256]{2,1,0:T(8,128)S(1)}, u32[]{:S(2)}, u32[]{:S(2)}) collective-permute-start(f32[1,96,256]{2,1,0:T(8,128)S(1)} %get-tuple-element.65), channel_id=1, source_target_pairs={{0,80},{16,64},{32,112},{48,96},{64,16},{80,0},{96,48},{112,32},{1... | collective-permute-start | bytes 294920 | tf_op jit(solution)/shard_map/ppermute | solution.py:381
  167.9 24.2 %all-to-all-start.2 = ((f32[16,48,256]{2,1,0:T(8,128)}), f32[16,48,256]{2,1,0:T(8,128)S(1)}, u32[]{:S(2)}, u32[]{:S(2)}) async-start(f32[16,48,256]{2,1,0:T(8,128)} %bitcast.9), calls=%async_computation.2 | async-start | bytes 1572864 | tf_op jit(solution)/shard_map/all_to_all | solution.py:375
  177.2 6.2 %collective-permute-start.24 = (f32[1,96,256]{2,1,0:T(8,128)S(1)}, f32[1,96,256]{2,1,0:T(8,128)S(1)}, u32[]{:S(2)}, u32[]{:S(2)}) collective-permute-start(f32[1,96,256]{2,1,0:T(8,128)S(1)} %get-tuple-element.67), channel_id=1, source_target_pairs={{0,96},{16,112},{32,64},{48,80},{64,32},{80,48},{96,0},{112,16},{1... | collective-permute-start | bytes 294920 | tf_op jit(solution)/shard_map/ppermute | solution.py:381
  179.8 6.4 %collective-permute-start.25 = (f32[1,96,256]{2,1,0:T(8,128)S(1)}, f32[1,96,256]{2,1,0:T(8,128)S(1)}, u32[]{:S(2)}, u32[]{:S(2)}) collective-permute-start(f32[1,96,256]{2,1,0:T(8,128)S(1)} %get-tuple-element.69), channel_id=1, source_target_pairs={{0,112},{16,96},{32,80},{48,64},{64,48},{80,32},{96,16},{112,0},{1... | collective-permute-start | bytes 294920 | tf_op jit(solution)/shard_map/ppermute | solution.py:381
  186.2 6.8 %copy-start.1 = (f32[8,96,256]{2,1,0:T(8,128)}, f32[8,96,256]{2,1,0:T(8,128)S(1)}, u32[]{:S(2)}) copy-start(f32[8,96,256]{2,1,0:T(8,128)S(1)} %constant_dynamic-update-slice_fusion) | copy-start | bytes 2359300

commit v4 on v3

--- a/solution.py
+++ b/solution.py
@@ -46,13 +46,13 @@
     return near, far
 
 
-def omega_routes():
+def omega_routes(turn):
     inside, along = [], []
     for y in range(4):
         for core in range(2):
             for z in range(4):
                 for x in range(4):
-                    src_y = y ^ (2 * (x // 2) + z % 2)
+                    src_y = y ^ (2 * (x // 2) + z % 2) ^ turn
                     src_core = core ^ (x % 2)
                     middle = device(src_y, src_core, z, x)
                     inside.append((device(src_y, src_core, y, 2 * core + z // 2), middle))
@@ -209,6 +209,43 @@
     )(meta, own_pts, near_pts, far_pts, src)
 
 
+def add_rows_kernel(ids, arrived, out, stage, sems, *, cut):
+    total = ids.shape[0] * SLOTS
+
+    def fetch(at, n):
+        k, slot = n // SLOTS, n % SLOTS
+        src = arrived.at[k, pl.ds(slot * cut, cut)]
+        return pltpu.make_async_copy(src, stage.at[at], sems.at[at])
+
+    for n in range(total):
+
+        @pl.when(ids[n // SLOTS, n % SLOTS] >= 0)
+        def _(n=n):
+            fetch(n, n).start()
+
+    out[...] = jnp.zeros_like(out)
+    for n in range(total):
+
+        @pl.when(ids[n // SLOTS, n % SLOTS] >= 0)
+        def _(n=n):
+            fetch(n, n).wait()
+            out[ids[n // SLOTS, n % SLOTS]] += stage[n]
+
+
+def add_rows(arrived, clusters, cut):
+    ids = arrived[:, SLOTS * cut :: TAG // SLOTS, 0].astype(jnp.int32)
+    total = ids.shape[0] * SLOTS
+    return pl.pallas_call(
+        functools.partial(add_rows_kernel, cut=cut),
+        out_shape=jax.ShapeDtypeStruct((clusters, cut, SK), F32),
+        in_specs=[pl.BlockSpec(memory_space=pltpu.SMEM), pl.BlockSpec(memory_space=pltpu.HBM)],
+        out_specs=pl.BlockSpec(memory_space=pltpu.VMEM),
+        scratch_shapes=[pltpu.VMEM((total, cut, SK), F32), pltpu.SemaphoreType.DMA((total,))],
+        cost_estimate=pl.CostEstimate(flops=1_000_000, bytes_accessed=3_000_000, transcendentals=0),
+        name="add_rows",
+    )(ids, arrived)
+
+
 def add_kernel(turn, *refs, cut, parts):
     arrived, outs, refs = refs[:parts], refs[parts : 2 * parts], refs[2 * parts :]
     if parts == 1:
@@ -297,13 +334,15 @@
     return jnp.concatenate(done, axis=0)[:, :BLK]
 
 
-def basis_kernel(turn, rows, self_rows, self_cols, *refs):
+def basis_kernel(turn, rows, self_high, self_low, self_cols, *refs):
     cols = refs[:NR]
     out_rows, out_cols = refs[NR], refs[NR + 1 : 2 * NR + 1]
     sk, sk_high, sk_low, gram, inverse, low_q = refs[2 * NR + 1 :]
     n = SK // BLK
     dims0 = (((0,), (0,)), ((), ()))
-    sk[0] = rows[...] + self_rows[...]
+    half = HEIGHT // 2
+    sk[0, :half] = rows[:half] + self_high[...]
+    sk[0, half:] = rows[half:] + self_low[...]
     for k in range(NR):
         part = pl.ds(pl.multiple_of((k ^ turn[0]) * COL_CUT, COL_CUT), COL_CUT)
         sk[1, part, :] = cols[k][0] + self_cols[part, :]
@@ -355,7 +394,7 @@
     return pl.pallas_call(
         basis_kernel,
         out_shape=(shape,) + (shape_c,) * NR,
-        in_specs=[pl.BlockSpec(memory_space=pltpu.SMEM)] + [vmem] * (3 + NR),
+        in_specs=[pl.BlockSpec(memory_space=pltpu.SMEM)] + [vmem] * (4 + NR),
         out_specs=(vmem,) * (NR + 1),
         scratch_shapes=[
             pltpu.VMEM((2, HEIGHT, SK), F32),
@@ -368,7 +407,7 @@
         compiler_params=pltpu.CompilerParams(vmem_limit_bytes=32 << 20),
         cost_estimate=pl.CostEstimate(flops=3_000_000_000, bytes_accessed=5_000_000, transcendentals=0),
         name="bases",
-    )(turn.reshape(1), rows, self_rows, self_cols, *cols)
+    )(turn.reshape(1), rows, *self_rows, self_cols, *cols)
 
 
 def trade(value, axis):
@@ -394,10 +433,15 @@
     src_y, src_core, src_z, src_x = row_at // 2, row_at % 2, col_at // 4, col_at % 4
     bits = src_z ^ src_y
     omega_pick = (bits % 2) * 4 + (bits // 2) * 2 + ((src_x // 2) ^ src_core)
-    inside, along = omega_routes()
-    weighted = omega[omega_pick] * self_weight[omega_pick][:, None]
-    weighted = lax.ppermute(weighted, BOTH, inside)
-    self_rows = lax.ppermute(weighted, BOTH, along)
+    half = HEIGHT // 2
+    self_rows = []
+    for h, turn in enumerate((0, 2)):
+        inside, along = omega_routes(turn)
+        pick = omega_pick ^ turn
+        weight = lax.dynamic_slice(self_weight, (pick, h * half), (1, half)).reshape(half, 1)
+        part = lax.dynamic_slice(omega, (pick, h * half, 0), (1, half, SK)).reshape(half, SK) * weight
+        part = lax.ppermute(part, BOTH, inside)
+        self_rows.append(lax.ppermute(part, BOTH, along))
     psi_pick = (src_x % 2) * 8 + ((src_z - src_y) % 4) * 2 + src_x // 2
     psi_here = lax.ppermute(psi[psi_pick], BOTH, psi_route())
     self_cols = psi_here * self_weight[row_at][:, None]
@@ -414,7 +458,7 @@
 
     row_got = trade(row_terms, "col")
     col_got = swap_rows(col_terms)
-    row_sum = add_arrived([row_got], none, ROW_CL, ROW_CUT)
+    row_sum = add_rows(row_got, ROW_CL, ROW_CUT)
     col_sum = add_arrived(col_got, row_at, COL_CL, COL_CUT)
     rows = trade(row_sum, "col").reshape(HEIGHT, SK)
     cols = swap_rows(col_sum)

time: 195 us -> 185 us (0.949)
  starting transfers between devices: 105 us -> 79.3 us
  waiting for transfers between devices: 29.2 us -> 46.5 us
  Pallas kernels: 27.8 us -> 25 us
    ppermute x21, starting transfers between devices: 62.2 us -> 34.8 us  [swap_rows(): got.append(lax.ppermute(value[k], 'row', [(i, i ^ k) for i in range(NR)]))]
    ppermute x21, waiting for transfers between devices: 22.5 us -> 38.9 us  [swap_rows(): got.append(lax.ppermute(value[k], 'row', [(i, i ^ k) for i in range(NR)]))]
    pallas_call x2 -> x1, Pallas kernels: 10 us -> 4.04 us  [add_arrived(): pl.pallas_call(functools.partial(add_kernel, cut=cut, parts=len(arrived))...]
    pallas_call x0 -> x1, Pallas kernels: none -> 3.16 us  [add_rows(): pl.pallas_call(functools.partial(add_rows_kernel, cut=cut), out_shape=jax...]
    all_to_all x3, starting transfers between devices: 18.7 us -> 21.6 us  [trade(): return lax.all_to_all(value, axis, split_axis=0, concat_axis=0, tiled=True)]
    ppermute x2 -> x4, starting transfers between devices: 14.8 us -> 14 us  [the longest x2 7.23 us: level(): self_rows.append(lax.ppermute(part, BOTH, along))]
    unnamed x28 -> x30, local copies, waits for them, and re-layouts: 4.12 us -> 3.74 us
  transfers between devices with their start and end apart: 29 -> 31, of which waited for: 11 -> 12; matrix products, arithmetic and copies ran while one was open for 3% -> 4% of each run, Pallas kernels for 9% -> 8%
where the time goes in v4:
time: 185 us; the launch traced here: 184 us
  starting transfers between devices  79.3 us (43%)
  waiting for transfers between devices  46.5 us (25%)
  local copies, waits for them, and re-layouts  27.4 us (15%)
  Pallas kernels  25 us (14%)
  other arithmetic  4.38 us (2%)
    ppermute x21, waiting for transfers between devices, swap_rows(): got.append(lax.ppermute(value[k], 'row', [(i, i ^ k) for i in range(NR)]))  38.9 us
    ppermute x21, starting transfers between devices, swap_rows(): got.append(lax.ppermute(value[k], 'row', [(i, i ^ k) for i in range(NR)]))  34.8 us
    all_to_all x3, starting transfers between devices, trade(): return lax.all_to_all(value, axis, split_axis=0, concat_axis=0, tiled=True)  21.6 us
    pallas_call x1, local copies, waits for them, and re-layouts, bases(): pl.pallas_call(basis_kernel, out_shape=(shape,) + (shape_c,) * NR, in_spe...  19.9 us
    pallas_call x2, Pallas kernels, pair_terms(): pl.pallas_call(functools.partial(pair_kernel, cut=cut, turned=turned), ou...  17.8 us
    ppermute x2, starting transfers between devices, level(): self_rows.append(lax.ppermute(part, BOTH, along))  7.23 us
    all_to_all x3, waiting for transfers between devices, trade(): return lax.all_to_all(value, axis, split_axis=0, concat_axis=0, tiled=True)  6.85 us
    ppermute x2, starting transfers between devices, level(): part = lax.ppermute(part, BOTH, inside)  6.81 us
  transfers between devices with their start and end apart: 31, of which 12 were waited for; matrix products, arithmetic and copies ran while one was open for 4% of the time, Pallas kernels for 8%

profile of v4, /device:TPU:0, one launch (start us, length us, event | category | flops | bytes accessed | tf_op | source)
XLA Modules:
  0.0 183.6 jit_solution(3620195388588975573)
XLA Ops:
  0.6 0.7 copy.14
  2.0 4.0 %collective-permute-start = (f32[4,8,128]{2,1,0:T(8,128)S(1)}, f32[4,8,128]{2,1,0:T(8,128)S(1)}, u32[]{:S(2)}, u32[]{:S(2)}) collective-permute-start(f32[4,8,128]{2,1,0:T(8,128)S(1)} %pad_maximum_fusion.own_pts), channel_id=1, source_target_pairs={{64,0},{65,1},{81,2},{80,3},{96,4},{97,5},{113,6},{112,7},{0,8},{1... | collective-permute-start | bytes 49160 | tf_op jit(solution)/shard_map/ppermute | solution.py:430
  6.0 4.1 %collective-permute-start.1 = (f32[4,8,128]{2,1,0:T(8,128)S(1)}, f32[4,8,128]{2,1,0:T(8,128)S(1)}, u32[]{:S(2)}, u32[]{:S(2)}) collective-permute-start(f32[4,8,128]{2,1,0:T(8,128)S(1)} %pad_maximum_fusion.own_pts), channel_id=1, source_target_pairs={{65,0},{64,1},{80,2},{81,3},{97,4},{96,5},{112,6},{113,7},{1,8},{0... | collective-permute-start | bytes 49160 | tf_op jit(solution)/shard_map/ppermute | solution.py:431
  10.2 1.3 pad_add_fusion
  11.5 0.7 collective-permute-done.1.far_pts
  12.8 9.9 %pair_rows.1 = f32[16,104,256]{2,1,0:T(8,128)} custom-call(s32[3,2]{1,0:T(4,128)} %get-tuple-element.75.meta, f32[4,8,128]{2,1,0:T(8,128)} %copy-done.7, f32[4,8,128]{2,1,0:T(8,128)} %copy-done.8, f32[4,8,128]{2,1,0:T(8,128)} %copy-done.9, f32[8,768,256]{2,1,0:T(8,128)} %src.2), custom_call_target="tpu_custom_call" | custom-call | flops 2000000000 | bytes 4000000 | tf_op jit(solution)/shard_map/pair_rows/pallas_call | solution.py:191
  22.8 5.9 %all-to-all-start = ((f32[16,104,256]{2,1,0:T(8,128)}), f32[16,104,256]{2,1,0:T(8,128)S(1)}, u32[]{:S(2)}, u32[]{:S(2)}) async-start(f32[16,104,256]{2,1,0:T(8,128)} %pair_rows.1), calls=%async_computation | async-start | bytes 3407872 | tf_op jit(solution)/shard_map/all_to_all | solution.py:414
  28.6 7.9 %pair_cols.1 = (f32[1,200,256]{2,1,0:T(8,128)}, f32[1,200,256]{2,1,0:T(8,128)}, f32[1,200,256]{2,1,0:T(8,128)}, f32[1,200,256]{2,1,0:T(8,128)}, f32[1,200,256]{2...) custom-call(s32[3,2]{1,0:T(4,128)} %get-tuple-element.74.meta, ...), custom_call_target="tpu_custom_call" | custom-call | flops 2000000000 | bytes 4000000 | tf_op jit(solution)/shard_map/pair_cols/pallas_call | solution.py:191
  36.7 1.2 dynamic-slice_bitcast_fusion
  37.9 0.7 collective-permute-start.6
  38.6 0.7 dynamic-slice_reduce_fusion
  39.4 7.4 %collective-permute-start.11 = (f32[1,200,256]{2,1,0:T(8,128)}, f32[1,200,256]{2,1,0:T(8,128)S(1)}, u32[]{:S(2)}, u32[]{:S(2)}) collective-permute-start(f32[1,200,256]{2,1,0:T(8,128)} %get-tuple-element.32), channel_id=1, source_target_pairs={{0,80},{16,64},{32,112},{48,96},{64,16},{80,0},{96,48},{112,32},{1... | collective-permute-start | bytes 614408 | tf_op jit(solution)/shard_map/ppermute | solution.py:420
  46.8 4.4 %collective-permute-start.12 = (f32[1,200,256]{2,1,0:T(8,128)}, f32[1,200,256]{2,1,0:T(8,128)S(1)}, u32[]{:S(2)}, u32[]{:S(2)}) collective-permute-start(f32[1,200,256]{2,1,0:T(8,128)} %get-tuple-element.33), channel_id=1, source_target_pairs={{0,96},{16,112},{32,64},{48,80},{64,32},{80,48},{96,0},{112,16},{1... | collective-permute-start | bytes 614408 | tf_op jit(solution)/shard_map/ppermute | solution.py:420
  51.3 2.2 %bitcast_multiply_fusion = (f32[384,256]{1,0:T(8,128)}, f32[384,256]{1,0:T(8,128)}) fusion(f32[8,768,256]{2,1,0:T(8,128)} %src.2, s32[]{:T(128)S(6)} %select_n.91, f32[384]{0:T(512)S(1)} %get-tuple-element.70, f32[384]{0:T(512)S(1)} %get-tuple-element.71, s32[]{:T(128)S(6)} %select_n.90), kind=kLoop, calls=%fused_computation.1 | loop fusion | flops 196608 | bytes 1575944 | tf_op jit(solution)/shard_map/mul | solution.py:442
  53.4 4.5 %collective-permute-start.2 = (f32[384,256]{1,0:T(8,128)}, f32[384,256]{1,0:T(8,128)}, u32[]{:S(2)}, u32[]{:S(2)}) collective-permute-start(f32[384,256]{1,0:T(8,128)} %get-tuple-element.73), channel_id=1, source_target_pairs={{0,0},{16,17},{64,66},{80,83},{32,36},{48,53},{96,102},{112,119},{... | collective-permute-start | bytes 1179656 | tf_op jit(solution)/shard_map/ppermute | solution.py:443
  57.9 11.9 %collective-permute-done.12.refs_6_ = f32[1,200,256]{2,1,0:T(8,128)S(1)} collective-permute-done((f32[1,200,256]{2,1,0:T(8,128)}, f32[1,200,256]{2,1,0:T(8,128)S(1)}, u32[]{:S(2)}, u32[]{:S(2)}) %collective-permute-start.12) | collective-permute-done | bytes 204832 | tf_op jit(solution)/shard_map/ppermute | solution.py:420
  70.4 2.3 %collective-permute-start.4 = (f32[384,256]{1,0:T(8,128)}, f32[384,256]{1,0:T(8,128)}, u32[]{:S(2)}, u32[]{:S(2)}) collective-permute-start(f32[384,256]{1,0:T(8,128)} %get-tuple-element.72), channel_id=1, source_target_pairs={{64,64},{80,81},{0,2},{16,19},{96,100},{112,117},{32,38},{48,55},{... | collective-permute-start | bytes 1179656 | tf_op jit(solution)/shard_map/ppermute | solution.py:443
  72.9 0.9 copy.11.ids
  74.0 3.2 %add_rows.1 = f32[16,48,256]{2,1,0:T(8,128)} custom-call(s32[16,2]{1,0:T(8,128)} %copy.11.ids, f32[16,104,256]{2,1,0:T(8,128)} %copy-done), custom_call_target="tpu_custom_call" | custom-call | flops 1000000 | bytes 3000000 | tf_op jit(solution)/shard_map/add_rows/pallas_call | solution.py:238
  77.1 10.5 %all-to-all-start.1 = ((f32[16,48,256]{2,1,0:T(8,128)}), f32[16,48,256]{2,1,0:T(8,128)S(1)}, u32[]{:S(2)}, u32[]{:S(2)}) async-start(f32[16,48,256]{2,1,0:T(8,128)} %add_rows.1), calls=%async_computation.1 | async-start | bytes 1572864 | tf_op jit(solution)/shard_map/all_to_all | solution.py:414
  87.7 1.4 collective-permute-start.8
  89.0 2.6 %collective-permute-start.9 = (f32[1,200,256]{2,1,0:T(8,128)}, f32[1,200,256]{2,1,0:T(8,128)S(1)}, u32[]{:S(2)}, u32[]{:S(2)}) collective-permute-start(f32[1,200,256]{2,1,0:T(8,128)} %get-tuple-element.30), channel_id=1, source_target_pairs={{0,48},{16,32},{32,16},{48,0},{64,112},{80,96},{96,80},{112,64},{1... | collective-permute-start | bytes 614408 | tf_op jit(solution)/shard_map/ppermute | solution.py:420
  91.6 2.8 %collective-permute-done.8.refs_2_ = f32[1,200,256]{2,1,0:T(8,128)S(1)} collective-permute-done((f32[1,200,256]{2,1,0:T(8,128)}, f32[1,200,256]{2,1,0:T(8,128)S(1)}, u32[]{:S(2)}, u32[]{:S(2)}) %collective-permute-start.8) | collective-permute-done | bytes 204832 | tf_op jit(solution)/shard_map/ppermute | solution.py:420
  94.4 5.9 %collective-permute-done.9.refs_3_ = f32[1,200,256]{2,1,0:T(8,128)S(1)} collective-permute-done((f32[1,200,256]{2,1,0:T(8,128)}, f32[1,200,256]{2,1,0:T(8,128)S(1)}, u32[]{:S(2)}, u32[]{:S(2)}) %collective-permute-start.9) | collective-permute-done | bytes 204832 | tf_op jit(solution)/shard_map/ppermute | solution.py:420
  101.0 4.0 %add_arrived.1 = (f32[1,96,256]{2,1,0:T(8,128)}, f32[1,96,256]{2,1,0:T(8,128)}, f32[1,96,256]{2,1,0:T(8,128)}, f32[1,96,256]{2,1,0:T(8,128)}, f32[1,96,256]{2,1,...) custom-call(s32[1]{0:T(128)} %bitcast.turn, ...), custom_call_target="tpu_custom_call" | custom-call | flops 1000000 | bytes 3000000 | tf_op jit(solution)/shard_map/add_arrived/pallas_call | solution.py:285
  105.1 1.4 collective-permute-start.15
  106.5 4.5 %collective-permute-start.3 = (f32[384,256]{1,0:T(8,128)}, f32[384,256]{1,0:T(8,128)}, u32[]{:S(2)}, u32[]{:S(2)}) collective-permute-start(f32[384,256]{1,0:T(8,128)} %collective-permute-done.2), channel_id=1, source_target_pairs={{0,0},{17,1},{66,2},{83,3},{36,4},{53,5},{102,6},{119,7},{8,8},{25... | collective-permute-start | bytes 1179656 | tf_op jit(solution)/shard_map/ppermute | solution.py:444
  111.0 2.8 %collective-permute-start.5 = (f32[384,256]{1,0:T(8,128)}, f32[384,256]{1,0:T(8,128)}, u32[]{:S(2)}, u32[]{:S(2)}) collective-permute-start(f32[384,256]{1,0:T(8,128)} %collective-permute-done.4), channel_id=1, source_target_pairs={{64,0},{81,1},{2,2},{19,3},{100,4},{117,5},{38,6},{55,7},{72,8},{8... | collective-permute-start | bytes 1179656 | tf_op jit(solution)/shard_map/ppermute | solution.py:444
  114.2 3.1 %collective-permute-start.17 = (f32[1,96,256]{2,1,0:T(8,128)}, f32[1,96,256]{2,1,0:T(8,128)S(1)}, u32[]{:S(2)}, u32[]{:S(2)}) collective-permute-start(f32[1,96,256]{2,1,0:T(8,128)} %get-tuple-element.39), channel_id=1, source_target_pairs={{0,64},{16,80},{32,96},{48,112},{64,0},{80,16},{96,32},{112,48},{1... | collective-permute-start | bytes 294920 | tf_op jit(solution)/shard_map/ppermute | solution.py:420
  117.3 0.8 fusion
  118.1 7.6 %collective-permute-done.16 = f32[1,96,256]{2,1,0:T(8,128)S(1)} collective-permute-done((f32[1,96,256]{2,1,0:T(8,128)}, f32[1,96,256]{2,1,0:T(8,128)S(1)}, u32[]{:S(2)}, u32[]{:S(2)}) %collective-permute-start.16) | collective-permute-done | bytes 98336 | tf_op jit(solution)/shard_map/ppermute | solution.py:420
  125.6 4.1 %collective-permute-start.18 = (f32[1,96,256]{2,1,0:T(8,128)}, f32[1,96,256]{2,1,0:T(8,128)S(1)}, u32[]{:S(2)}, u32[]{:S(2)}) collective-permute-start(f32[1,96,256]{2,1,0:T(8,128)} %get-tuple-element.40), channel_id=1, source_target_pairs={{0,80},{16,64},{32,112},{48,96},{64,16},{80,0},{96,48},{112,32},{1... | collective-permute-start | bytes 294920 | tf_op jit(solution)/shard_map/ppermute | solution.py:420
  129.9 1.0 collective-permute-start.19
  130.9 0.9 collective-permute-start.20
  132.0 0.8 collective-permute-done.18
  132.8 3.8 %collective-permute-done.19 = f32[1,96,256]{2,1,0:T(8,128)S(1)} collective-permute-done((f32[1,96,256]{2,1,0:T(8,128)}, f32[1,96,256]{2,1,0:T(8,128)S(1)}, u32[]{:S(2)}, u32[]{:S(2)}) %collective-permute-start.19) | collective-permute-done | bytes 98336 | tf_op jit(solution)/shard_map/ppermute | solution.py:420
  136.6 0.8 collective-permute-done.20
  137.5 19.9 %bases.1 = (f32[8,96,256]{2,1,0:T(8,128)S(1)}, f32[768,256]{1,0:T(8,128)}, f32[1,96,256]{2,1,0:T(8,128)S(1)}, f32[1,96,256]{2,1,0:T(8,128)S(1)}, f32[1,96,256]{2...) fusion(f32[8,96,256]{2,1,0:T(8,128)S(1)} %broadcast_in_dim.12, ...), kind=kCustom, calls=%fused_computation.13 | custom fusion | bytes 4718600 | tf_op jit(solution)/shard_map/bases/pallas_call | solution.py:394
  157.9 1.4 collective-permute-start.23
  159.2 1.5 collective-permute-start.24
  160.8 2.1 %collective-permute-start.25 = (f32[1,96,256]{2,1,0:T(8,128)S(1)}, f32[1,96,256]{2,1,0:T(8,128)S(1)}, u32[]{:S(2)}, u32[]{:S(2)}) collective-permute-start(f32[1,96,256]{2,1,0:T(8,128)S(1)} %get-tuple-element.65), channel_id=1, source_target_pairs={{0,80},{16,64},{32,112},{48,96},{64,16},{80,0},{96,48},{112,32},{1... | collective-permute-start | bytes 294920 | tf_op jit(solution)/shard_map/ppermute | solution.py:420
  162.9 5.2 %all-to-all-start.2 = ((f32[16,48,256]{2,1,0:T(8,128)}), f32[16,48,256]{2,1,0:T(8,128)S(1)}, u32[]{:S(2)}, u32[]{:S(2)}) async-start(f32[16,48,256]{2,1,0:T(8,128)} %bitcast.11), calls=%async_computation.2 | async-start | bytes 1572864 | tf_op jit(solution)/shard_map/all_to_all | solution.py:414
  168.1 1.3 collective-permute-start.26
  169.5 1.1 collective-permute-start.27
  170.7 3.6 %collective-permute-done.26 = f32[1,96,256]{2,1,0:T(8,128)S(1)} collective-permute-done((f32[1,96,256]{2,1,0:T(8,128)S(1)}, f32[1,96,256]{2,1,0:T(8,128)S(1)}, u32[]{:S(2)}, u32[]{:S(2)}) %collective-permute-start.26) | collective-permute-done | bytes 98336 | tf_op jit(solution)/shard_map/ppermute | solution.py:420
  174.3 1.5 collective-permute-done.27
  175.9 6.8 %all-to-all-done.2 = f32[16,48,256]{2,1,0:T(8,128)S(1)} async-done(((f32[16,48,256]{2,1,0:T(8,128)}), f32[16,48,256]{2,1,0:T(8,128)S(1)}, u32[]{:S(2)}, u32[]{:S(2)}) %all-to-all-start.2) | async-done | bytes 786464 | tf_op jit(solution)/shard_map/all_to_all | solution.py:414
  182.7 0.9 copy.24
  (69 shorter events, 4.9 us)
Async XLA Ops:
  2.0 10.2 %copy-start.7 = (f32[4,8,128]{2,1,0:T(8,128)}, f32[4,8,128]{2,1,0:T(8,128)S(1)}, u32[]{:S(2)}) copy-start(f32[4,8,128]{2,1,0:T(8,128)S(1)} %pad_maximum_fusion.own_pts) | copy-start | bytes 49156
  2.0 9.5 %collective-permute-start = (f32[4,8,128]{2,1,0:T(8,128)S(1)}, f32[4,8,128]{2,1,0:T(8,128)S(1)}, u32[]{:S(2)}, u32[]{:S(2)}) collective-permute-start(f32[4,8,128]{2,1,0:T(8,128)S(1)} %pad_maximum_fusion.own_pts), channel_id=1, source_target_pairs={{64,0},{65,1},{81,2},{80,3},{96,4},{97,5},{113,6},{112,7},{0,8},{1... | collective-permute-start | bytes 49160 | tf_op jit(solution)/shard_map/ppermute | solution.py:430
  6.0 6.2 %collective-permute-start.1 = (f32[4,8,128]{2,1,0:T(8,128)S(1)}, f32[4,8,128]{2,1,0:T(8,128)S(1)}, u32[]{:S(2)}, u32[]{:S(2)}) collective-permute-start(f32[4,8,128]{2,1,0:T(8,128)S(1)} %pad_maximum_fusion.own_pts), channel_id=1, source_target_pairs={{65,0},{64,1},{80,2},{81,3},{97,4},{96,5},{112,6},{113,7},{1,8},{0... | collective-permute-start | bytes 49160 | tf_op jit(solution)/shard_map/ppermute | solution.py:431
  11.5 0.7 copy-start.8
  12.2 0.6 copy-start.9
  22.8 50.0 %all-to-all-start = ((f32[16,104,256]{2,1,0:T(8,128)}), f32[16,104,256]{2,1,0:T(8,128)S(1)}, u32[]{:S(2)}, u32[]{:S(2)}) async-start(f32[16,104,256]{2,1,0:T(8,128)} %pair_rows.1), calls=%async_computation | async-start | bytes 3407872 | tf_op jit(solution)/shard_map/all_to_all | solution.py:414
  36.5 14.6 %collective-permute-start.10 = (f32[1,200,256]{2,1,0:T(8,128)}, f32[1,200,256]{2,1,0:T(8,128)S(1)}, u32[]{:S(2)}, u32[]{:S(2)}) collective-permute-start(f32[1,200,256]{2,1,0:T(8,128)} %get-tuple-element.31), channel_id=1, source_target_pairs={{0,64},{16,80},{32,96},{48,112},{64,0},{80,16},{96,32},{112,48},{1... | collective-permute-start | bytes 614408 | tf_op jit(solution)/shard_map/ppermute | solution.py:420
  37.9 93.0 %collective-permute-start.6 = (f32[768,256]{1,0:T(8,128)S(1)}, f32[768,256]{1,0:T(8,128)S(1)}, u32[]{:S(2)}, u32[]{:S(2)}) collective-permute-start(f32[768,256]{1,0:T(8,128)S(1)} %dynamic-slice_bitcast_fusion), channel_id=1, source_target_pairs={{0,0},{1,1},{16,2},{17,3},{36,4},{37,5},{52,6},{53,7},{72,8},{73,9... | collective-permute-start | bytes 2359304 | tf_op jit(solution)/shard_map/ppermute | solution.py:446
  39.4 14.0 %collective-permute-start.11 = (f32[1,200,256]{2,1,0:T(8,128)}, f32[1,200,256]{2,1,0:T(8,128)S(1)}, u32[]{:S(2)}, u32[]{:S(2)}) collective-permute-start(f32[1,200,256]{2,1,0:T(8,128)} %get-tuple-element.32), channel_id=1, source_target_pairs={{0,80},{16,64},{32,112},{48,96},{64,16},{80,0},{96,48},{112,32},{1... | collective-permute-start | bytes 614408 | tf_op jit(solution)/shard_map/ppermute | solution.py:420
  46.8 23.0 %collective-permute-start.12 = (f32[1,200,256]{2,1,0:T(8,128)}, f32[1,200,256]{2,1,0:T(8,128)S(1)}, u32[]{:S(2)}, u32[]{:S(2)}) collective-permute-start(f32[1,200,256]{2,1,0:T(8,128)} %get-tuple-element.33), channel_id=1, source_target_pairs={{0,96},{16,112},{32,64},{48,80},{64,32},{80,48},{96,0},{112,16},{1... | collective-permute-start | bytes 614408 | tf_op jit(solution)/shard_map/ppermute | solution.py:420
  51.1 36.5 %collective-permute-start.13 = (f32[1,200,256]{2,1,0:T(8,128)}, f32[1,200,256]{2,1,0:T(8,128)}, u32[]{:S(2)}, u32[]{:S(2)}) collective-permute-start(f32[1,200,256]{2,1,0:T(8,128)} %get-tuple-element.34), channel_id=1, source_target_pairs={{0,112},{16,96},{32,80},{48,64},{64,48},{80,32},{96,16},{112,0},{1... | collective-permute-start | bytes 614408 | tf_op jit(solution)/shard_map/ppermute | solution.py:420
  51.1 49.2 %copy-start.2 = (f32[1,200,256]{2,1,0:T(8,128)}, f32[1,200,256]{2,1,0:T(8,128)S(1)}, u32[]{:S(2)}) copy-start(f32[1,200,256]{2,1,0:T(8,128)S(1)} %collective-permute-done.10.refs_4_) | copy-start | bytes 614404
  51.1 37.9 %collective-permute-start.7 = (f32[1,200,256]{2,1,0:T(8,128)}, f32[1,200,256]{2,1,0:T(8,128)}, u32[]{:S(2)}, u32[]{:S(2)}) collective-permute-start(f32[1,200,256]{2,1,0:T(8,128)} %get-tuple-element.28), channel_id=1, source_target_pairs={{0,16},{16,0},{32,48},{48,32},{64,80},{80,64},{96,112},{112,96},{1... | collective-permute-start | bytes 614408 | tf_op jit(solution)/shard_map/ppermute | solution.py:420
  53.4 16.4 %copy-start.3 = (f32[1,200,256]{2,1,0:T(8,128)}, f32[1,200,256]{2,1,0:T(8,128)S(1)}, u32[]{:S(2)}) copy-start(f32[1,200,256]{2,1,0:T(8,128)S(1)} %collective-permute-done.11.refs_5_) | copy-start | bytes 614404
  53.4 53.1 %collective-permute-start.2 = (f32[384,256]{1,0:T(8,128)}, f32[384,256]{1,0:T(8,128)}, u32[]{:S(2)}, u32[]{:S(2)}) collective-permute-start(f32[384,256]{1,0:T(8,128)} %get-tuple-element.73), channel_id=1, source_target_pairs={{0,0},{16,17},{64,66},{80,83},{32,36},{48,53},{96,102},{112,119},{... | collective-permute-start | bytes 1179656 | tf_op jit(solution)/shard_map/ppermute | solution.py:443
  69.8 0.7 copy-start.4
  70.4 40.5 %collective-permute-start.4 = (f32[384,256]{1,0:T(8,128)}, f32[384,256]{1,0:T(8,128)}, u32[]{:S(2)}, u32[]{:S(2)}) collective-permute-start(f32[384,256]{1,0:T(8,128)} %get-tuple-element.72), channel_id=1, source_target_pairs={{64,64},{80,81},{0,2},{16,19},{96,100},{112,117},{32,38},{48,55},{... | collective-permute-start | bytes 1179656 | tf_op jit(solution)/shard_map/ppermute | solution.py:443
  72.8 1.2 copy-start
  77.1 60.3 %all-to-all-start.1 = ((f32[16,48,256]{2,1,0:T(8,128)}), f32[16,48,256]{2,1,0:T(8,128)S(1)}, u32[]{:S(2)}, u32[]{:S(2)}) async-start(f32[16,48,256]{2,1,0:T(8,128)} %add_rows.1), calls=%async_computation.1 | async-start | bytes 1572864 | tf_op jit(solution)/shard_map/all_to_all | solution.py:414
  87.7 6.8 %collective-permute-start.8 = (f32[1,200,256]{2,1,0:T(8,128)}, f32[1,200,256]{2,1,0:T(8,128)S(1)}, u32[]{:S(2)}, u32[]{:S(2)}) collective-permute-start(f32[1,200,256]{2,1,0:T(8,128)} %get-tuple-element.29), channel_id=1, source_target_pairs={{0,32},{16,48},{32,0},{48,16},{64,96},{80,112},{96,64},{112,80},{1... | collective-permute-start | bytes 614408 | tf_op jit(solution)/shard_map/ppermute | solution.py:420
  89.0 11.3 %collective-permute-start.9 = (f32[1,200,256]{2,1,0:T(8,128)}, f32[1,200,256]{2,1,0:T(8,128)S(1)}, u32[]{:S(2)}, u32[]{:S(2)}) collective-permute-start(f32[1,200,256]{2,1,0:T(8,128)} %get-tuple-element.30), channel_id=1, source_target_pairs={{0,48},{16,32},{32,16},{48,0},{64,112},{80,96},{96,80},{112,64},{1... | collective-permute-start | bytes 614408 | tf_op jit(solution)/shard_map/ppermute | solution.py:420
  94.4 5.9 %copy-start.5 = (f32[1,200,256]{2,1,0:T(8,128)}, f32[1,200,256]{2,1,0:T(8,128)S(1)}, u32[]{:S(2)}) copy-start(f32[1,200,256]{2,1,0:T(8,128)S(1)} %collective-permute-done.8.refs_2_) | copy-start | bytes 614404
  100.3 0.7 copy-start.6
  105.0 8.7 %collective-permute-start.14 = (f32[1,96,256]{2,1,0:T(8,128)}, f32[1,96,256]{2,1,0:T(8,128)S(1)}, u32[]{:S(2)}, u32[]{:S(2)}) collective-permute-start(f32[1,96,256]{2,1,0:T(8,128)} %get-tuple-element.36), channel_id=1, source_target_pairs={{0,16},{16,0},{32,48},{48,32},{64,80},{80,64},{96,112},{112,96},{1... | collective-permute-start | bytes 294920 | tf_op jit(solution)/shard_map/ppermute | solution.py:420
  105.1 9.1 %collective-permute-start.15 = (f32[1,96,256]{2,1,0:T(8,128)}, f32[1,96,256]{2,1,0:T(8,128)S(1)}, u32[]{:S(2)}, u32[]{:S(2)}) collective-permute-start(f32[1,96,256]{2,1,0:T(8,128)} %get-tuple-element.37), channel_id=1, source_target_pairs={{0,32},{16,48},{32,0},{48,16},{64,96},{80,112},{96,64},{112,80},{1... | collective-permute-start | bytes 294920 | tf_op jit(solution)/shard_map/ppermute | solution.py:420
  106.5 30.9 %collective-permute-start.3 = (f32[384,256]{1,0:T(8,128)}, f32[384,256]{1,0:T(8,128)}, u32[]{:S(2)}, u32[]{:S(2)}) collective-permute-start(f32[384,256]{1,0:T(8,128)} %collective-permute-done.2), channel_id=1, source_target_pairs={{0,0},{17,1},{66,2},{83,3},{36,4},{53,5},{102,6},{119,7},{8,8},{25... | collective-permute-start | bytes 1179656 | tf_op jit(solution)/shard_map/ppermute | solution.py:444
  111.0 26.5 %collective-permute-start.5 = (f32[384,256]{1,0:T(8,128)}, f32[384,256]{1,0:T(8,128)}, u32[]{:S(2)}, u32[]{:S(2)}) collective-permute-start(f32[384,256]{1,0:T(8,128)} %collective-permute-done.4), channel_id=1, source_target_pairs={{64,0},{81,1},{2,2},{19,3},{100,4},{117,5},{38,6},{55,7},{72,8},{8... | collective-permute-start | bytes 1179656 | tf_op jit(solution)/shard_map/ppermute | solution.py:444
  113.7 11.9 %collective-permute-start.16 = (f32[1,96,256]{2,1,0:T(8,128)}, f32[1,96,256]{2,1,0:T(8,128)S(1)}, u32[]{:S(2)}, u32[]{:S(2)}) collective-permute-start(f32[1,96,256]{2,1,0:T(8,128)} %get-tuple-element.38), channel_id=1, source_target_pairs={{0,48},{16,32},{32,16},{48,0},{64,112},{80,96},{96,80},{112,64},{1... | collective-permute-start | bytes 294920 | tf_op jit(solution)/shard_map/ppermute | solution.py:420
  114.2 15.7 %collective-permute-start.17 = (f32[1,96,256]{2,1,0:T(8,128)}, f32[1,96,256]{2,1,0:T(8,128)S(1)}, u32[]{:S(2)}, u32[]{:S(2)}) collective-permute-start(f32[1,96,256]{2,1,0:T(8,128)} %get-tuple-element.39), channel_id=1, source_target_pairs={{0,64},{16,80},{32,96},{48,112},{64,0},{80,16},{96,32},{112,48},{1... | collective-permute-start | bytes 294920 | tf_op jit(solution)/shard_map/ppermute | solution.py:420
  125.6 11.8 %copy-start.10 = (f32[1,96,256]{2,1,0:T(8,128)}, f32[1,96,256]{2,1,0:T(8,128)S(1)}, u32[]{:S(2)}) copy-start(f32[1,96,256]{2,1,0:T(8,128)S(1)} %collective-permute-done.16) | copy-start | bytes 294916
  125.6 7.2 %collective-permute-start.18 = (f32[1,96,256]{2,1,0:T(8,128)}, f32[1,96,256]{2,1,0:T(8,128)S(1)}, u32[]{:S(2)}, u32[]{:S(2)}) collective-permute-start(f32[1,96,256]{2,1,0:T(8,128)} %get-tuple-element.40), channel_id=1, source_target_pairs={{0,80},{16,64},{32,112},{48,96},{64,16},{80,0},{96,48},{112,32},{1... | collective-permute-start | bytes 294920 | tf_op jit(solution)/shard_map/ppermute | solution.py:420
  129.9 1.0 copy-start.11
  129.9 6.7 %collective-permute-start.19 = (f32[1,96,256]{2,1,0:T(8,128)}, f32[1,96,256]{2,1,0:T(8,128)S(1)}, u32[]{:S(2)}, u32[]{:S(2)}) collective-permute-start(f32[1,96,256]{2,1,0:T(8,128)} %get-tuple-element.41), channel_id=1, source_target_pairs={{0,96},{16,112},{32,64},{48,80},{64,32},{80,48},{96,0},{112,16},{1... | collective-permute-start | bytes 294920 | tf_op jit(solution)/shard_map/ppermute | solution.py:420
  130.9 6.5 %collective-permute-start.20 = (f32[1,96,256]{2,1,0:T(8,128)}, f32[1,96,256]{2,1,0:T(8,128)S(1)}, u32[]{:S(2)}, u32[]{:S(2)}) collective-permute-start(f32[1,96,256]{2,1,0:T(8,128)} %get-tuple-element.42), channel_id=1, source_target_pairs={{0,112},{16,96},{32,80},{48,64},{64,48},{80,32},{96,16},{112,0},{1... | collective-permute-start | bytes 294920 | tf_op jit(solution)/shard_map/ppermute | solution.py:420
  132.8 4.6 %copy-start.12 = (f32[1,96,256]{2,1,0:T(8,128)}, f32[1,96,256]{2,1,0:T(8,128)S(1)}, u32[]{:S(2)}) copy-start(f32[1,96,256]{2,1,0:T(8,128)S(1)} %collective-permute-done.18) | copy-start | bytes 294916
  136.6 0.8 copy-start.13
  157.4 10.7 %collective-permute-start.21 = (f32[1,96,256]{2,1,0:T(8,128)S(1)}, f32[1,96,256]{2,1,0:T(8,128)S(1)}, u32[]{:S(2)}, u32[]{:S(2)}) collective-permute-start(f32[1,96,256]{2,1,0:T(8,128)S(1)} %get-tuple-element.57), channel_id=1, source_target_pairs={{0,16},{16,0},{32,48},{48,32},{64,80},{80,64},{96,112},{112,96},{1... | collective-permute-start | bytes 294920 | tf_op jit(solution)/shard_map/ppermute | solution.py:420
  157.9 11.6 %collective-permute-start.22 = (f32[1,96,256]{2,1,0:T(8,128)S(1)}, f32[1,96,256]{2,1,0:T(8,128)S(1)}, u32[]{:S(2)}, u32[]{:S(2)}) collective-permute-start(f32[1,96,256]{2,1,0:T(8,128)S(1)} %get-tuple-element.59), channel_id=1, source_target_pairs={{0,32},{16,48},{32,0},{48,16},{64,96},{80,112},{96,64},{112,80},{1... | collective-permute-start | bytes 294920 | tf_op jit(solution)/shard_map/ppermute | solution.py:420
  157.9 12.8 %collective-permute-start.23 = (f32[1,96,256]{2,1,0:T(8,128)S(1)}, f32[1,96,256]{2,1,0:T(8,128)S(1)}, u32[]{:S(2)}, u32[]{:S(2)}) collective-permute-start(f32[1,96,256]{2,1,0:T(8,128)S(1)} %get-tuple-element.61), channel_id=1, source_target_pairs={{0,48},{16,32},{32,16},{48,0},{64,112},{80,96},{96,80},{112,64},{1... | collective-permute-start | bytes 294920 | tf_op jit(solution)/shard_map/ppermute | solution.py:420
  159.2 11.4 %collective-permute-start.24 = (f32[1,96,256]{2,1,0:T(8,128)S(1)}, f32[1,96,256]{2,1,0:T(8,128)S(1)}, u32[]{:S(2)}, u32[]{:S(2)}) collective-permute-start(f32[1,96,256]{2,1,0:T(8,128)S(1)} %get-tuple-element.63), channel_id=1, source_target_pairs={{0,64},{16,80},{32,96},{48,112},{64,0},{80,16},{96,32},{112,48},{1... | collective-permute-start | bytes 294920 | tf_op jit(solution)/shard_map/ppermute | solution.py:420
  160.8 9.9 %collective-permute-start.25 = (f32[1,96,256]{2,1,0:T(8,128)S(1)}, f32[1,96,256]{2,1,0:T(8,128)S(1)}, u32[]{:S(2)}, u32[]{:S(2)}) collective-permute-start(f32[1,96,256]{2,1,0:T(8,128)S(1)} %get-tuple-element.65), channel_id=1, source_target_pairs={{0,80},{16,64},{32,112},{48,96},{64,16},{80,0},{96,48},{112,32},{1... | collective-permute-start | bytes 294920 | tf_op jit(solution)/shard_map/ppermute | solution.py:420
  162.9 19.9 %all-to-all-start.2 = ((f32[16,48,256]{2,1,0:T(8,128)}), f32[16,48,256]{2,1,0:T(8,128)S(1)}, u32[]{:S(2)}, u32[]{:S(2)}) async-start(f32[16,48,256]{2,1,0:T(8,128)} %bitcast.11), calls=%async_computation.2 | async-start | bytes 1572864 | tf_op jit(solution)/shard_map/all_to_all | solution.py:414
  168.1 6.2 %collective-permute-start.26 = (f32[1,96,256]{2,1,0:T(8,128)S(1)}, f32[1,96,256]{2,1,0:T(8,128)S(1)}, u32[]{:S(2)}, u32[]{:S(2)}) collective-permute-start(f32[1,96,256]{2,1,0:T(8,128)S(1)} %get-tuple-element.67), channel_id=1, source_target_pairs={{0,96},{16,112},{32,64},{48,80},{64,32},{80,48},{96,0},{112,16},{1... | collective-permute-start | bytes 294920 | tf_op jit(solution)/shard_map/ppermute | solution.py:420
  169.5 6.4 %collective-permute-start.27 = (f32[1,96,256]{2,1,0:T(8,128)S(1)}, f32[1,96,256]{2,1,0:T(8,128)S(1)}, u32[]{:S(2)}, u32[]{:S(2)}) collective-permute-start(f32[1,96,256]{2,1,0:T(8,128)S(1)} %get-tuple-element.69), channel_id=1, source_target_pairs={{0,112},{16,96},{32,80},{48,64},{64,48},{80,32},{96,16},{112,0},{1... | collective-permute-start | bytes 294920 | tf_op jit(solution)/shard_map/ppermute | solution.py:420
  175.9 7.7 %copy-start.1 = (f32[8,96,256]{2,1,0:T(8,128)}, f32[8,96,256]{2,1,0:T(8,128)S(1)}, u32[]{:S(2)}) copy-start(f32[8,96,256]{2,1,0:T(8,128)S(1)} %constant_dynamic-update-slice_fusion) | copy-start | bytes 2359300

commit v5 on v4

--- a/solution.py
+++ b/solution.py
@@ -298,7 +298,11 @@
 BLK = 64
 
 
-def factor_inverse(diag):
+def spread_lane(value, lane):
+    return jnp.broadcast_to(value[:, lane : lane + 1], (8, 128))
+
+
+def factor_inverse(diag, held):
     sub = lax.broadcasted_iota(jnp.int32, (8, 128), 0)
     lane = lax.broadcasted_iota(jnp.int32, (8, 128), 1)
     body = jnp.concatenate([diag, diag], axis=1)
@@ -310,26 +314,35 @@
     for kb in range(BLK // 8):
         at = BLK + 8 * kb
         spread = {
-            g: [jnp.broadcast_to(groups[g][:, at + t : at + t + 1], (8, 128)) for t in range(8)]
-            for g in range(kb, BLK // 8)
+            g: [spread_lane(groups[g], at + t) for t in range(8)]
+            for g in range(kb + 1, BLK // 8)
         }
         rows = [jnp.broadcast_to(groups[kb][t : t + 1, :], (8, 128)) for t in range(8)]
-        e = [[jnp.broadcast_to(spread[kb][t][s : s + 1, :], (8, 128)) if s >= t else None for t in range(8)] for s in range(8)]
+        for t in range(8):
+            held[kb, t] = spread_lane(groups[kb], at + t)
+        e = [
+            [jnp.broadcast_to(held[kb, t, r : r + 1, :], (8, 128)) if r >= t else None for t in range(8)]
+            for r in range(8)
+        ]
         final = jnp.zeros((8, 128), F32)
+        scaled = []
+        m = {}
         for t in range(8):
             root = lax.rsqrt(e[t][t])
             inv = 1.0 / e[t][t]
             final = jnp.where(sub == t, rows[t] * root, final)
-            scaled = rows[t] * inv
-            for s in range(t + 1, 8):
-                m = e[s][t] * inv
-                for u in range(t + 1, s + 1):
-                    e[s][u] = e[s][u] - m * e[u][t]
-                rows[s] = rows[s] - e[s][t] * scaled
-                for g in range(kb + 1, BLK // 8):
-                    spread[g][s] = spread[g][s] - spread[g][t] * m
-            for g in range(kb + 1, BLK // 8):
-                groups[g] = groups[g] - spread[g][t] * scaled
+            scaled.append(rows[t] * inv)
+            for r in range(t + 1, 8):
+                m[r, t] = e[r][t] * inv
+                for u in range(t + 1, r + 1):
+                    e[r][u] = e[r][u] - m[r, t] * e[u][t]
+                rows[r] = rows[r] - e[r][t] * scaled[t]
+        for t in range(6, -1, -1):
+            for r in range(7, t, -1):
+                scaled[t] = scaled[t] - m[r, t] * scaled[r]
+        for g in range(kb + 1, BLK // 8):
+            for t in range(8):
+                groups[g] = groups[g] - spread[g][t] * scaled[t]
         done.append(final)
     return jnp.concatenate(done, axis=0)[:, :BLK]
 
@@ -337,7 +350,7 @@
 def basis_kernel(turn, rows, self_high, self_low, self_cols, *refs):
     cols = refs[:NR]
     out_rows, out_cols = refs[NR], refs[NR + 1 : 2 * NR + 1]
-    sk, sk_high, sk_low, gram, inverse, low_q = refs[2 * NR + 1 :]
+    sk, sk_high, sk_low, gram, inverse, low_q, pivots = refs[2 * NR + 1 :]
     n = SK // BLK
     dims0 = (((0,), (0,)), ((), ()))
     half = HEIGHT // 2
@@ -355,7 +368,7 @@
         inverse[w] = jnp.zeros((SK, SK), F32)
     for k in range(n):
         here = slice(k * BLK, (k + 1) * BLK)
-        low = [factor_inverse(gram[w, here, here]) for w in range(2)]
+        low = [factor_inverse(gram[w, here, here], pivots.at[w]) for w in range(2)]
         for w in range(2):
             if k:
                 inverse[w, here, : k * BLK] = jnp.dot(
@@ -403,6 +416,7 @@
             pltpu.VMEM((2, SK, SK), F32),
             pltpu.VMEM((2, SK, SK), F32),
             pltpu.VMEM((NR, COL_CUT, SK), F32),
+            pltpu.VMEM((2, BLK // 8, 8, 8, 128), F32),
         ],
         compiler_params=pltpu.CompilerParams(vmem_limit_bytes=32 << 20),
         cost_estimate=pl.CostEstimate(flops=3_000_000_000, bytes_accessed=5_000_000, transcendentals=0),

time: 185 us -> 182 us (0.984)
  local copies, waits for them, and re-layouts: 27.4 us -> 24.2 us
    pallas_call x1, local copies, waits for them, and re-layouts: 19.9 us -> 16.6 us  [bases(): pl.pallas_call(basis_kernel, out_shape=(shape,) + (shape_c,) * NR, in_spe...]
where the time goes in v5:
time: 182 us; the launch traced here: 180 us
  starting transfers between devices  79.3 us (44%)
  waiting for transfers between devices  46.5 us (26%)
  Pallas kernels  25 us (14%)
  local copies, waits for them, and re-layouts  24.2 us (13%)
  other arithmetic  4.38 us (2%)
    ppermute x21, waiting for transfers between devices, swap_rows(): got.append(lax.ppermute(value[k], 'row', [(i, i ^ k) for i in range(NR)]))  38.9 us
    ppermute x21, starting transfers between devices, swap_rows(): got.append(lax.ppermute(value[k], 'row', [(i, i ^ k) for i in range(NR)]))  34.8 us
    all_to_all x3, starting transfers between devices, trade(): return lax.all_to_all(value, axis, split_axis=0, concat_axis=0, tiled=True)  21.6 us
    pallas_call x2, Pallas kernels, pair_terms(): pl.pallas_call(functools.partial(pair_kernel, cut=cut, turned=turned), ou...  17.8 us
    pallas_call x1, local copies, waits for them, and re-layouts, bases(): pl.pallas_call(basis_kernel, out_shape=(shape,) + (shape_c,) * NR, in_spe...  16.6 us
    ppermute x2, starting transfers between devices, level(): self_rows.append(lax.ppermute(part, BOTH, along))  7.23 us
    all_to_all x3, waiting for transfers between devices, trade(): return lax.all_to_all(value, axis, split_axis=0, concat_axis=0, tiled=True)  6.84 us
    ppermute x2, starting transfers between devices, level(): part = lax.ppermute(part, BOTH, inside)  6.81 us
  transfers between devices with their start and end apart: 31, of which 12 were waited for; matrix products, arithmetic and copies ran while one was open for 4% of the time, Pallas kernels for 8%

profile of v5, /device:TPU:0, one launch (start us, length us, event | category | flops | bytes accessed | tf_op | source)
XLA Modules:
  0.0 180.3 jit_solution(898533884152225188)
XLA Ops:
  0.6 0.7 copy.14
  2.0 4.0 %collective-permute-start = (f32[4,8,128]{2,1,0:T(8,128)S(1)}, f32[4,8,128]{2,1,0:T(8,128)S(1)}, u32[]{:S(2)}, u32[]{:S(2)}) collective-permute-start(f32[4,8,128]{2,1,0:T(8,128)S(1)} %pad_maximum_fusion.own_pts), channel_id=1, source_target_pairs={{64,0},{65,1},{81,2},{80,3},{96,4},{97,5},{113,6},{112,7},{0,8},{1... | collective-permute-start | bytes 49160 | tf_op jit(solution)/shard_map/ppermute | solution.py:444
  6.0 4.1 %collective-permute-start.1 = (f32[4,8,128]{2,1,0:T(8,128)S(1)}, f32[4,8,128]{2,1,0:T(8,128)S(1)}, u32[]{:S(2)}, u32[]{:S(2)}) collective-permute-start(f32[4,8,128]{2,1,0:T(8,128)S(1)} %pad_maximum_fusion.own_pts), channel_id=1, source_target_pairs={{65,0},{64,1},{80,2},{81,3},{97,4},{96,5},{112,6},{113,7},{1,8},{0... | collective-permute-start | bytes 49160 | tf_op jit(solution)/shard_map/ppermute | solution.py:445
  10.2 1.3 pad_add_fusion
  11.5 0.7 collective-permute-done.1.far_pts
  12.8 9.9 %pair_rows.1 = f32[16,104,256]{2,1,0:T(8,128)} custom-call(s32[3,2]{1,0:T(4,128)} %get-tuple-element.75.meta, f32[4,8,128]{2,1,0:T(8,128)} %copy-done.7, f32[4,8,128]{2,1,0:T(8,128)} %copy-done.8, f32[4,8,128]{2,1,0:T(8,128)} %copy-done.9, f32[8,768,256]{2,1,0:T(8,128)} %src.2), custom_call_target="tpu_custom_call" | custom-call | flops 2000000000 | bytes 4000000 | tf_op jit(solution)/shard_map/pair_rows/pallas_call | solution.py:191
  22.8 5.9 %all-to-all-start = ((f32[16,104,256]{2,1,0:T(8,128)}), f32[16,104,256]{2,1,0:T(8,128)S(1)}, u32[]{:S(2)}, u32[]{:S(2)}) async-start(f32[16,104,256]{2,1,0:T(8,128)} %pair_rows.1), calls=%async_computation | async-start | bytes 3407872 | tf_op jit(solution)/shard_map/all_to_all | solution.py:428
  28.6 7.9 %pair_cols.1 = (f32[1,200,256]{2,1,0:T(8,128)}, f32[1,200,256]{2,1,0:T(8,128)}, f32[1,200,256]{2,1,0:T(8,128)}, f32[1,200,256]{2,1,0:T(8,128)}, f32[1,200,256]{2...) custom-call(s32[3,2]{1,0:T(4,128)} %get-tuple-element.74.meta, ...), custom_call_target="tpu_custom_call" | custom-call | flops 2000000000 | bytes 4000000 | tf_op jit(solution)/shard_map/pair_cols/pallas_call | solution.py:191
  36.7 1.2 dynamic-slice_bitcast_fusion
  37.9 0.7 collective-permute-start.6
  38.6 0.7 dynamic-slice_reduce_fusion
  39.4 7.4 %collective-permute-start.11 = (f32[1,200,256]{2,1,0:T(8,128)}, f32[1,200,256]{2,1,0:T(8,128)S(1)}, u32[]{:S(2)}, u32[]{:S(2)}) collective-permute-start(f32[1,200,256]{2,1,0:T(8,128)} %get-tuple-element.32), channel_id=1, source_target_pairs={{0,80},{16,64},{32,112},{48,96},{64,16},{80,0},{96,48},{112,32},{1... | collective-permute-start | bytes 614408 | tf_op jit(solution)/shard_map/ppermute | solution.py:434
  46.8 4.4 %collective-permute-start.12 = (f32[1,200,256]{2,1,0:T(8,128)}, f32[1,200,256]{2,1,0:T(8,128)S(1)}, u32[]{:S(2)}, u32[]{:S(2)}) collective-permute-start(f32[1,200,256]{2,1,0:T(8,128)} %get-tuple-element.33), channel_id=1, source_target_pairs={{0,96},{16,112},{32,64},{48,80},{64,32},{80,48},{96,0},{112,16},{1... | collective-permute-start | bytes 614408 | tf_op jit(solution)/shard_map/ppermute | solution.py:434
  51.3 2.2 %bitcast_multiply_fusion = (f32[384,256]{1,0:T(8,128)}, f32[384,256]{1,0:T(8,128)}) fusion(f32[8,768,256]{2,1,0:T(8,128)} %src.2, s32[]{:T(128)S(6)} %select_n.91, f32[384]{0:T(512)S(1)} %get-tuple-element.70, f32[384]{0:T(512)S(1)} %get-tuple-element.71, s32[]{:T(128)S(6)} %select_n.90), kind=kLoop, calls=%fused_computation.1 | loop fusion | flops 196608 | bytes 1575944 | tf_op jit(solution)/shard_map/mul | solution.py:456
  53.4 4.5 %collective-permute-start.2 = (f32[384,256]{1,0:T(8,128)}, f32[384,256]{1,0:T(8,128)}, u32[]{:S(2)}, u32[]{:S(2)}) collective-permute-start(f32[384,256]{1,0:T(8,128)} %get-tuple-element.73), channel_id=1, source_target_pairs={{0,0},{16,17},{64,66},{80,83},{32,36},{48,53},{96,102},{112,119},{... | collective-permute-start | bytes 1179656 | tf_op jit(solution)/shard_map/ppermute | solution.py:457
  57.9 11.9 %collective-permute-done.12.refs_6_ = f32[1,200,256]{2,1,0:T(8,128)S(1)} collective-permute-done((f32[1,200,256]{2,1,0:T(8,128)}, f32[1,200,256]{2,1,0:T(8,128)S(1)}, u32[]{:S(2)}, u32[]{:S(2)}) %collective-permute-start.12) | collective-permute-done | bytes 204832 | tf_op jit(solution)/shard_map/ppermute | solution.py:434
  70.4 2.3 %collective-permute-start.4 = (f32[384,256]{1,0:T(8,128)}, f32[384,256]{1,0:T(8,128)}, u32[]{:S(2)}, u32[]{:S(2)}) collective-permute-start(f32[384,256]{1,0:T(8,128)} %get-tuple-element.72), channel_id=1, source_target_pairs={{64,64},{80,81},{0,2},{16,19},{96,100},{112,117},{32,38},{48,55},{... | collective-permute-start | bytes 1179656 | tf_op jit(solution)/shard_map/ppermute | solution.py:457
  72.9 0.9 copy.11.ids
  74.0 3.2 %add_rows.1 = f32[16,48,256]{2,1,0:T(8,128)} custom-call(s32[16,2]{1,0:T(8,128)} %copy.11.ids, f32[16,104,256]{2,1,0:T(8,128)} %copy-done), custom_call_target="tpu_custom_call" | custom-call | flops 1000000 | bytes 3000000 | tf_op jit(solution)/shard_map/add_rows/pallas_call | solution.py:238
  77.1 10.5 %all-to-all-start.1 = ((f32[16,48,256]{2,1,0:T(8,128)}), f32[16,48,256]{2,1,0:T(8,128)S(1)}, u32[]{:S(2)}, u32[]{:S(2)}) async-start(f32[16,48,256]{2,1,0:T(8,128)} %add_rows.1), calls=%async_computation.1 | async-start | bytes 1572864 | tf_op jit(solution)/shard_map/all_to_all | solution.py:428
  87.7 1.4 collective-permute-start.8
  89.0 2.6 %collective-permute-start.9 = (f32[1,200,256]{2,1,0:T(8,128)}, f32[1,200,256]{2,1,0:T(8,128)S(1)}, u32[]{:S(2)}, u32[]{:S(2)}) collective-permute-start(f32[1,200,256]{2,1,0:T(8,128)} %get-tuple-element.30), channel_id=1, source_target_pairs={{0,48},{16,32},{32,16},{48,0},{64,112},{80,96},{96,80},{112,64},{1... | collective-permute-start | bytes 614408 | tf_op jit(solution)/shard_map/ppermute | solution.py:434
  91.6 2.8 %collective-permute-done.8.refs_2_ = f32[1,200,256]{2,1,0:T(8,128)S(1)} collective-permute-done((f32[1,200,256]{2,1,0:T(8,128)}, f32[1,200,256]{2,1,0:T(8,128)S(1)}, u32[]{:S(2)}, u32[]{:S(2)}) %collective-permute-start.8) | collective-permute-done | bytes 204832 | tf_op jit(solution)/shard_map/ppermute | solution.py:434
  94.4 5.9 %collective-permute-done.9.refs_3_ = f32[1,200,256]{2,1,0:T(8,128)S(1)} collective-permute-done((f32[1,200,256]{2,1,0:T(8,128)}, f32[1,200,256]{2,1,0:T(8,128)S(1)}, u32[]{:S(2)}, u32[]{:S(2)}) %collective-permute-start.9) | collective-permute-done | bytes 204832 | tf_op jit(solution)/shard_map/ppermute | solution.py:434
  101.0 4.0 %add_arrived.1 = (f32[1,96,256]{2,1,0:T(8,128)}, f32[1,96,256]{2,1,0:T(8,128)}, f32[1,96,256]{2,1,0:T(8,128)}, f32[1,96,256]{2,1,0:T(8,128)}, f32[1,96,256]{2,1,...) custom-call(s32[1]{0:T(128)} %bitcast.turn, ...), custom_call_target="tpu_custom_call" | custom-call | flops 1000000 | bytes 3000000 | tf_op jit(solution)/shard_map/add_arrived/pallas_call | solution.py:285
  105.1 1.4 collective-permute-start.15
  106.5 4.5 %collective-permute-start.3 = (f32[384,256]{1,0:T(8,128)}, f32[384,256]{1,0:T(8,128)}, u32[]{:S(2)}, u32[]{:S(2)}) collective-permute-start(f32[384,256]{1,0:T(8,128)} %collective-permute-done.2), channel_id=1, source_target_pairs={{0,0},{17,1},{66,2},{83,3},{36,4},{53,5},{102,6},{119,7},{8,8},{25... | collective-permute-start | bytes 1179656 | tf_op jit(solution)/shard_map/ppermute | solution.py:458
  111.0 2.8 %collective-permute-start.5 = (f32[384,256]{1,0:T(8,128)}, f32[384,256]{1,0:T(8,128)}, u32[]{:S(2)}, u32[]{:S(2)}) collective-permute-start(f32[384,256]{1,0:T(8,128)} %collective-permute-done.4), channel_id=1, source_target_pairs={{64,0},{81,1},{2,2},{19,3},{100,4},{117,5},{38,6},{55,7},{72,8},{8... | collective-permute-start | bytes 1179656 | tf_op jit(solution)/shard_map/ppermute | solution.py:458
  114.2 3.1 %collective-permute-start.17 = (f32[1,96,256]{2,1,0:T(8,128)}, f32[1,96,256]{2,1,0:T(8,128)S(1)}, u32[]{:S(2)}, u32[]{:S(2)}) collective-permute-start(f32[1,96,256]{2,1,0:T(8,128)} %get-tuple-element.39), channel_id=1, source_target_pairs={{0,64},{16,80},{32,96},{48,112},{64,0},{80,16},{96,32},{112,48},{1... | collective-permute-start | bytes 294920 | tf_op jit(solution)/shard_map/ppermute | solution.py:434
  117.3 0.8 fusion
  118.1 7.6 %collective-permute-done.16 = f32[1,96,256]{2,1,0:T(8,128)S(1)} collective-permute-done((f32[1,96,256]{2,1,0:T(8,128)}, f32[1,96,256]{2,1,0:T(8,128)S(1)}, u32[]{:S(2)}, u32[]{:S(2)}) %collective-permute-start.16) | collective-permute-done | bytes 98336 | tf_op jit(solution)/shard_map/ppermute | solution.py:434
  125.6 4.1 %collective-permute-start.18 = (f32[1,96,256]{2,1,0:T(8,128)}, f32[1,96,256]{2,1,0:T(8,128)S(1)}, u32[]{:S(2)}, u32[]{:S(2)}) collective-permute-start(f32[1,96,256]{2,1,0:T(8,128)} %get-tuple-element.40), channel_id=1, source_target_pairs={{0,80},{16,64},{32,112},{48,96},{64,16},{80,0},{96,48},{112,32},{1... | collective-permute-start | bytes 294920 | tf_op jit(solution)/shard_map/ppermute | solution.py:434
  129.9 1.0 collective-permute-start.19
  130.9 0.9 collective-permute-start.20
  132.0 0.8 collective-permute-done.18
  132.8 3.8 %collective-permute-done.19 = f32[1,96,256]{2,1,0:T(8,128)S(1)} collective-permute-done((f32[1,96,256]{2,1,0:T(8,128)}, f32[1,96,256]{2,1,0:T(8,128)S(1)}, u32[]{:S(2)}, u32[]{:S(2)}) %collective-permute-start.19) | collective-permute-done | bytes 98336 | tf_op jit(solution)/shard_map/ppermute | solution.py:434
  136.6 0.8 collective-permute-done.20
  137.5 16.6 %bases.1 = (f32[8,96,256]{2,1,0:T(8,128)S(1)}, f32[768,256]{1,0:T(8,128)}, f32[1,96,256]{2,1,0:T(8,128)S(1)}, f32[1,96,256]{2,1,0:T(8,128)S(1)}, f32[1,96,256]{2...) fusion(f32[8,96,256]{2,1,0:T(8,128)S(1)} %broadcast_in_dim.12, ...), kind=kCustom, calls=%fused_computation.13 | custom fusion | bytes 4718600 | tf_op jit(solution)/shard_map/bases/pallas_call | solution.py:407
  154.6 1.4 collective-permute-start.23
  156.0 1.5 collective-permute-start.24
  157.5 2.1 %collective-permute-start.25 = (f32[1,96,256]{2,1,0:T(8,128)S(1)}, f32[1,96,256]{2,1,0:T(8,128)S(1)}, u32[]{:S(2)}, u32[]{:S(2)}) collective-permute-start(f32[1,96,256]{2,1,0:T(8,128)S(1)} %get-tuple-element.65), channel_id=1, source_target_pairs={{0,80},{16,64},{32,112},{48,96},{64,16},{80,0},{96,48},{112,32},{1... | collective-permute-start | bytes 294920 | tf_op jit(solution)/shard_map/ppermute | solution.py:434
  159.6 5.2 %all-to-all-start.2 = ((f32[16,48,256]{2,1,0:T(8,128)}), f32[16,48,256]{2,1,0:T(8,128)S(1)}, u32[]{:S(2)}, u32[]{:S(2)}) async-start(f32[16,48,256]{2,1,0:T(8,128)} %bitcast.11), calls=%async_computation.2 | async-start | bytes 1572864 | tf_op jit(solution)/shard_map/all_to_all | solution.py:428
  164.8 1.3 collective-permute-start.26
  166.2 1.1 collective-permute-start.27
  167.4 3.6 %collective-permute-done.26 = f32[1,96,256]{2,1,0:T(8,128)S(1)} collective-permute-done((f32[1,96,256]{2,1,0:T(8,128)S(1)}, f32[1,96,256]{2,1,0:T(8,128)S(1)}, u32[]{:S(2)}, u32[]{:S(2)}) %collective-permute-start.26) | collective-permute-done | bytes 98336 | tf_op jit(solution)/shard_map/ppermute | solution.py:434
  171.0 1.6 collective-permute-done.27
  172.6 6.8 %all-to-all-done.2 = f32[16,48,256]{2,1,0:T(8,128)S(1)} async-done(((f32[16,48,256]{2,1,0:T(8,128)}), f32[16,48,256]{2,1,0:T(8,128)S(1)}, u32[]{:S(2)}, u32[]{:S(2)}) %all-to-all-start.2) | async-done | bytes 786464 | tf_op jit(solution)/shard_map/all_to_all | solution.py:428
  179.5 0.9 copy.24
  (69 shorter events, 4.9 us)
Async XLA Ops:
  2.0 10.2 %copy-start.7 = (f32[4,8,128]{2,1,0:T(8,128)}, f32[4,8,128]{2,1,0:T(8,128)S(1)}, u32[]{:S(2)}) copy-start(f32[4,8,128]{2,1,0:T(8,128)S(1)} %pad_maximum_fusion.own_pts) | copy-start | bytes 49156
  2.0 9.5 %collective-permute-start = (f32[4,8,128]{2,1,0:T(8,128)S(1)}, f32[4,8,128]{2,1,0:T(8,128)S(1)}, u32[]{:S(2)}, u32[]{:S(2)}) collective-permute-start(f32[4,8,128]{2,1,0:T(8,128)S(1)} %pad_maximum_fusion.own_pts), channel_id=1, source_target_pairs={{64,0},{65,1},{81,2},{80,3},{96,4},{97,5},{113,6},{112,7},{0,8},{1... | collective-permute-start | bytes 49160 | tf_op jit(solution)/shard_map/ppermute | solution.py:444
  6.0 6.2 %collective-permute-start.1 = (f32[4,8,128]{2,1,0:T(8,128)S(1)}, f32[4,8,128]{2,1,0:T(8,128)S(1)}, u32[]{:S(2)}, u32[]{:S(2)}) collective-permute-start(f32[4,8,128]{2,1,0:T(8,128)S(1)} %pad_maximum_fusion.own_pts), channel_id=1, source_target_pairs={{65,0},{64,1},{80,2},{81,3},{97,4},{96,5},{112,6},{113,7},{1,8},{0... | collective-permute-start | bytes 49160 | tf_op jit(solution)/shard_map/ppermute | solution.py:445
  11.5 0.7 copy-start.8
  12.2 0.6 copy-start.9
  22.8 50.0 %all-to-all-start = ((f32[16,104,256]{2,1,0:T(8,128)}), f32[16,104,256]{2,1,0:T(8,128)S(1)}, u32[]{:S(2)}, u32[]{:S(2)}) async-start(f32[16,104,256]{2,1,0:T(8,128)} %pair_rows.1), calls=%async_computation | async-start | bytes 3407872 | tf_op jit(solution)/shard_map/all_to_all | solution.py:428
  36.5 14.6 %collective-permute-start.10 = (f32[1,200,256]{2,1,0:T(8,128)}, f32[1,200,256]{2,1,0:T(8,128)S(1)}, u32[]{:S(2)}, u32[]{:S(2)}) collective-permute-start(f32[1,200,256]{2,1,0:T(8,128)} %get-tuple-element.31), channel_id=1, source_target_pairs={{0,64},{16,80},{32,96},{48,112},{64,0},{80,16},{96,32},{112,48},{1... | collective-permute-start | bytes 614408 | tf_op jit(solution)/shard_map/ppermute | solution.py:434
  37.9 93.0 %collective-permute-start.6 = (f32[768,256]{1,0:T(8,128)S(1)}, f32[768,256]{1,0:T(8,128)S(1)}, u32[]{:S(2)}, u32[]{:S(2)}) collective-permute-start(f32[768,256]{1,0:T(8,128)S(1)} %dynamic-slice_bitcast_fusion), channel_id=1, source_target_pairs={{0,0},{1,1},{16,2},{17,3},{36,4},{37,5},{52,6},{53,7},{72,8},{73,9... | collective-permute-start | bytes 2359304 | tf_op jit(solution)/shard_map/ppermute | solution.py:460
  39.4 14.0 %collective-permute-start.11 = (f32[1,200,256]{2,1,0:T(8,128)}, f32[1,200,256]{2,1,0:T(8,128)S(1)}, u32[]{:S(2)}, u32[]{:S(2)}) collective-permute-start(f32[1,200,256]{2,1,0:T(8,128)} %get-tuple-element.32), channel_id=1, source_target_pairs={{0,80},{16,64},{32,112},{48,96},{64,16},{80,0},{96,48},{112,32},{1... | collective-permute-start | bytes 614408 | tf_op jit(solution)/shard_map/ppermute | solution.py:434
  46.8 23.0 %collective-permute-start.12 = (f32[1,200,256]{2,1,0:T(8,128)}, f32[1,200,256]{2,1,0:T(8,128)S(1)}, u32[]{:S(2)}, u32[]{:S(2)}) collective-permute-start(f32[1,200,256]{2,1,0:T(8,128)} %get-tuple-element.33), channel_id=1, source_target_pairs={{0,96},{16,112},{32,64},{48,80},{64,32},{80,48},{96,0},{112,16},{1... | collective-permute-start | bytes 614408 | tf_op jit(solution)/shard_map/ppermute | solution.py:434
  51.1 36.5 %collective-permute-start.13 = (f32[1,200,256]{2,1,0:T(8,128)}, f32[1,200,256]{2,1,0:T(8,128)}, u32[]{:S(2)}, u32[]{:S(2)}) collective-permute-start(f32[1,200,256]{2,1,0:T(8,128)} %get-tuple-element.34), channel_id=1, source_target_pairs={{0,112},{16,96},{32,80},{48,64},{64,48},{80,32},{96,16},{112,0},{1... | collective-permute-start | bytes 614408 | tf_op jit(solution)/shard_map/ppermute | solution.py:434
  51.1 49.2 %copy-start.2 = (f32[1,200,256]{2,1,0:T(8,128)}, f32[1,200,256]{2,1,0:T(8,128)S(1)}, u32[]{:S(2)}) copy-start(f32[1,200,256]{2,1,0:T(8,128)S(1)} %collective-permute-done.10.refs_4_) | copy-start | bytes 614404
  51.1 37.9 %collective-permute-start.7 = (f32[1,200,256]{2,1,0:T(8,128)}, f32[1,200,256]{2,1,0:T(8,128)}, u32[]{:S(2)}, u32[]{:S(2)}) collective-permute-start(f32[1,200,256]{2,1,0:T(8,128)} %get-tuple-element.28), channel_id=1, source_target_pairs={{0,16},{16,0},{32,48},{48,32},{64,80},{80,64},{96,112},{112,96},{1... | collective-permute-start | bytes 614408 | tf_op jit(solution)/shard_map/ppermute | solution.py:434
  53.4 16.4 %copy-start.3 = (f32[1,200,256]{2,1,0:T(8,128)}, f32[1,200,256]{2,1,0:T(8,128)S(1)}, u32[]{:S(2)}) copy-start(f32[1,200,256]{2,1,0:T(8,128)S(1)} %collective-permute-done.11.refs_5_) | copy-start | bytes 614404
  53.4 53.1 %collective-permute-start.2 = (f32[384,256]{1,0:T(8,128)}, f32[384,256]{1,0:T(8,128)}, u32[]{:S(2)}, u32[]{:S(2)}) collective-permute-start(f32[384,256]{1,0:T(8,128)} %get-tuple-element.73), channel_id=1, source_target_pairs={{0,0},{16,17},{64,66},{80,83},{32,36},{48,53},{96,102},{112,119},{... | collective-permute-start | bytes 1179656 | tf_op jit(solution)/shard_map/ppermute | solution.py:457
  69.8 0.7 copy-start.4
  70.4 40.5 %collective-permute-start.4 = (f32[384,256]{1,0:T(8,128)}, f32[384,256]{1,0:T(8,128)}, u32[]{:S(2)}, u32[]{:S(2)}) collective-permute-start(f32[384,256]{1,0:T(8,128)} %get-tuple-element.72), channel_id=1, source_target_pairs={{64,64},{80,81},{0,2},{16,19},{96,100},{112,117},{32,38},{48,55},{... | collective-permute-start | bytes 1179656 | tf_op jit(solution)/shard_map/ppermute | solution.py:457
  72.8 1.2 copy-start
  77.1 60.3 %all-to-all-start.1 = ((f32[16,48,256]{2,1,0:T(8,128)}), f32[16,48,256]{2,1,0:T(8,128)S(1)}, u32[]{:S(2)}, u32[]{:S(2)}) async-start(f32[16,48,256]{2,1,0:T(8,128)} %add_rows.1), calls=%async_computation.1 | async-start | bytes 1572864 | tf_op jit(solution)/shard_map/all_to_all | solution.py:428
  87.7 6.8 %collective-permute-start.8 = (f32[1,200,256]{2,1,0:T(8,128)}, f32[1,200,256]{2,1,0:T(8,128)S(1)}, u32[]{:S(2)}, u32[]{:S(2)}) collective-permute-start(f32[1,200,256]{2,1,0:T(8,128)} %get-tuple-element.29), channel_id=1, source_target_pairs={{0,32},{16,48},{32,0},{48,16},{64,96},{80,112},{96,64},{112,80},{1... | collective-permute-start | bytes 614408 | tf_op jit(solution)/shard_map/ppermute | solution.py:434
  89.0 11.3 %collective-permute-start.9 = (f32[1,200,256]{2,1,0:T(8,128)}, f32[1,200,256]{2,1,0:T(8,128)S(1)}, u32[]{:S(2)}, u32[]{:S(2)}) collective-permute-start(f32[1,200,256]{2,1,0:T(8,128)} %get-tuple-element.30), channel_id=1, source_target_pairs={{0,48},{16,32},{32,16},{48,0},{64,112},{80,96},{96,80},{112,64},{1... | collective-permute-start | bytes 614408 | tf_op jit(solution)/shard_map/ppermute | solution.py:434
  94.4 5.9 %copy-start.5 = (f32[1,200,256]{2,1,0:T(8,128)}, f32[1,200,256]{2,1,0:T(8,128)S(1)}, u32[]{:S(2)}) copy-start(f32[1,200,256]{2,1,0:T(8,128)S(1)} %collective-permute-done.8.refs_2_) | copy-start | bytes 614404
  100.3 0.7 copy-start.6
  105.0 8.7 %collective-permute-start.14 = (f32[1,96,256]{2,1,0:T(8,128)}, f32[1,96,256]{2,1,0:T(8,128)S(1)}, u32[]{:S(2)}, u32[]{:S(2)}) collective-permute-start(f32[1,96,256]{2,1,0:T(8,128)} %get-tuple-element.36), channel_id=1, source_target_pairs={{0,16},{16,0},{32,48},{48,32},{64,80},{80,64},{96,112},{112,96},{1... | collective-permute-start | bytes 294920 | tf_op jit(solution)/shard_map/ppermute | solution.py:434
  105.1 9.1 %collective-permute-start.15 = (f32[1,96,256]{2,1,0:T(8,128)}, f32[1,96,256]{2,1,0:T(8,128)S(1)}, u32[]{:S(2)}, u32[]{:S(2)}) collective-permute-start(f32[1,96,256]{2,1,0:T(8,128)} %get-tuple-element.37), channel_id=1, source_target_pairs={{0,32},{16,48},{32,0},{48,16},{64,96},{80,112},{96,64},{112,80},{1... | collective-permute-start | bytes 294920 | tf_op jit(solution)/shard_map/ppermute | solution.py:434
  106.5 30.9 %collective-permute-start.3 = (f32[384,256]{1,0:T(8,128)}, f32[384,256]{1,0:T(8,128)}, u32[]{:S(2)}, u32[]{:S(2)}) collective-permute-start(f32[384,256]{1,0:T(8,128)} %collective-permute-done.2), channel_id=1, source_target_pairs={{0,0},{17,1},{66,2},{83,3},{36,4},{53,5},{102,6},{119,7},{8,8},{25... | collective-permute-start | bytes 1179656 | tf_op jit(solution)/shard_map/ppermute | solution.py:458
  111.0 26.5 %collective-permute-start.5 = (f32[384,256]{1,0:T(8,128)}, f32[384,256]{1,0:T(8,128)}, u32[]{:S(2)}, u32[]{:S(2)}) collective-permute-start(f32[384,256]{1,0:T(8,128)} %collective-permute-done.4), channel_id=1, source_target_pairs={{64,0},{81,1},{2,2},{19,3},{100,4},{117,5},{38,6},{55,7},{72,8},{8... | collective-permute-start | bytes 1179656 | tf_op jit(solution)/shard_map/ppermute | solution.py:458
  113.7 11.9 %collective-permute-start.16 = (f32[1,96,256]{2,1,0:T(8,128)}, f32[1,96,256]{2,1,0:T(8,128)S(1)}, u32[]{:S(2)}, u32[]{:S(2)}) collective-permute-start(f32[1,96,256]{2,1,0:T(8,128)} %get-tuple-element.38), channel_id=1, source_target_pairs={{0,48},{16,32},{32,16},{48,0},{64,112},{80,96},{96,80},{112,64},{1... | collective-permute-start | bytes 294920 | tf_op jit(solution)/shard_map/ppermute | solution.py:434
  114.2 15.7 %collective-permute-start.17 = (f32[1,96,256]{2,1,0:T(8,128)}, f32[1,96,256]{2,1,0:T(8,128)S(1)}, u32[]{:S(2)}, u32[]{:S(2)}) collective-permute-start(f32[1,96,256]{2,1,0:T(8,128)} %get-tuple-element.39), channel_id=1, source_target_pairs={{0,64},{16,80},{32,96},{48,112},{64,0},{80,16},{96,32},{112,48},{1... | collective-permute-start | bytes 294920 | tf_op jit(solution)/shard_map/ppermute | solution.py:434
  125.6 11.8 %copy-start.10 = (f32[1,96,256]{2,1,0:T(8,128)}, f32[1,96,256]{2,1,0:T(8,128)S(1)}, u32[]{:S(2)}) copy-start(f32[1,96,256]{2,1,0:T(8,128)S(1)} %collective-permute-done.16) | copy-start | bytes 294916
  125.6 7.2 %collective-permute-start.18 = (f32[1,96,256]{2,1,0:T(8,128)}, f32[1,96,256]{2,1,0:T(8,128)S(1)}, u32[]{:S(2)}, u32[]{:S(2)}) collective-permute-start(f32[1,96,256]{2,1,0:T(8,128)} %get-tuple-element.40), channel_id=1, source_target_pairs={{0,80},{16,64},{32,112},{48,96},{64,16},{80,0},{96,48},{112,32},{1... | collective-permute-start | bytes 294920 | tf_op jit(solution)/shard_map/ppermute | solution.py:434
  129.9 1.0 copy-start.11
  129.9 6.7 %collective-permute-start.19 = (f32[1,96,256]{2,1,0:T(8,128)}, f32[1,96,256]{2,1,0:T(8,128)S(1)}, u32[]{:S(2)}, u32[]{:S(2)}) collective-permute-start(f32[1,96,256]{2,1,0:T(8,128)} %get-tuple-element.41), channel_id=1, source_target_pairs={{0,96},{16,112},{32,64},{48,80},{64,32},{80,48},{96,0},{112,16},{1... | collective-permute-start | bytes 294920 | tf_op jit(solution)/shard_map/ppermute | solution.py:434
  130.9 6.5 %collective-permute-start.20 = (f32[1,96,256]{2,1,0:T(8,128)}, f32[1,96,256]{2,1,0:T(8,128)S(1)}, u32[]{:S(2)}, u32[]{:S(2)}) collective-permute-start(f32[1,96,256]{2,1,0:T(8,128)} %get-tuple-element.42), channel_id=1, source_target_pairs={{0,112},{16,96},{32,80},{48,64},{64,48},{80,32},{96,16},{112,0},{1... | collective-permute-start | bytes 294920 | tf_op jit(solution)/shard_map/ppermute | solution.py:434
  132.8 4.6 %copy-start.12 = (f32[1,96,256]{2,1,0:T(8,128)}, f32[1,96,256]{2,1,0:T(8,128)S(1)}, u32[]{:S(2)}) copy-start(f32[1,96,256]{2,1,0:T(8,128)S(1)} %collective-permute-done.18) | copy-start | bytes 294916
  136.6 0.8 copy-start.13
  154.1 10.7 %collective-permute-start.21 = (f32[1,96,256]{2,1,0:T(8,128)S(1)}, f32[1,96,256]{2,1,0:T(8,128)S(1)}, u32[]{:S(2)}, u32[]{:S(2)}) collective-permute-start(f32[1,96,256]{2,1,0:T(8,128)S(1)} %get-tuple-element.57), channel_id=1, source_target_pairs={{0,16},{16,0},{32,48},{48,32},{64,80},{80,64},{96,112},{112,96},{1... | collective-permute-start | bytes 294920 | tf_op jit(solution)/shard_map/ppermute | solution.py:434
  154.6 11.6 %collective-permute-start.22 = (f32[1,96,256]{2,1,0:T(8,128)S(1)}, f32[1,96,256]{2,1,0:T(8,128)S(1)}, u32[]{:S(2)}, u32[]{:S(2)}) collective-permute-start(f32[1,96,256]{2,1,0:T(8,128)S(1)} %get-tuple-element.59), channel_id=1, source_target_pairs={{0,32},{16,48},{32,0},{48,16},{64,96},{80,112},{96,64},{112,80},{1... | collective-permute-start | bytes 294920 | tf_op jit(solution)/shard_map/ppermute | solution.py:434
  154.6 12.7 %collective-permute-start.23 = (f32[1,96,256]{2,1,0:T(8,128)S(1)}, f32[1,96,256]{2,1,0:T(8,128)S(1)}, u32[]{:S(2)}, u32[]{:S(2)}) collective-permute-start(f32[1,96,256]{2,1,0:T(8,128)S(1)} %get-tuple-element.61), channel_id=1, source_target_pairs={{0,48},{16,32},{32,16},{48,0},{64,112},{80,96},{96,80},{112,64},{1... | collective-permute-start | bytes 294920 | tf_op jit(solution)/shard_map/ppermute | solution.py:434
  156.0 11.4 %collective-permute-start.24 = (f32[1,96,256]{2,1,0:T(8,128)S(1)}, f32[1,96,256]{2,1,0:T(8,128)S(1)}, u32[]{:S(2)}, u32[]{:S(2)}) collective-permute-start(f32[1,96,256]{2,1,0:T(8,128)S(1)} %get-tuple-element.63), channel_id=1, source_target_pairs={{0,64},{16,80},{32,96},{48,112},{64,0},{80,16},{96,32},{112,48},{1... | collective-permute-start | bytes 294920 | tf_op jit(solution)/shard_map/ppermute | solution.py:434
  157.5 9.9 %collective-permute-start.25 = (f32[1,96,256]{2,1,0:T(8,128)S(1)}, f32[1,96,256]{2,1,0:T(8,128)S(1)}, u32[]{:S(2)}, u32[]{:S(2)}) collective-permute-start(f32[1,96,256]{2,1,0:T(8,128)S(1)} %get-tuple-element.65), channel_id=1, source_target_pairs={{0,80},{16,64},{32,112},{48,96},{64,16},{80,0},{96,48},{112,32},{1... | collective-permute-start | bytes 294920 | tf_op jit(solution)/shard_map/ppermute | solution.py:434
  159.6 19.9 %all-to-all-start.2 = ((f32[16,48,256]{2,1,0:T(8,128)}), f32[16,48,256]{2,1,0:T(8,128)S(1)}, u32[]{:S(2)}, u32[]{:S(2)}) async-start(f32[16,48,256]{2,1,0:T(8,128)} %bitcast.11), calls=%async_computation.2 | async-start | bytes 1572864 | tf_op jit(solution)/shard_map/all_to_all | solution.py:428
  164.8 6.2 %collective-permute-start.26 = (f32[1,96,256]{2,1,0:T(8,128)S(1)}, f32[1,96,256]{2,1,0:T(8,128)S(1)}, u32[]{:S(2)}, u32[]{:S(2)}) collective-permute-start(f32[1,96,256]{2,1,0:T(8,128)S(1)} %get-tuple-element.67), channel_id=1, source_target_pairs={{0,96},{16,112},{32,64},{48,80},{64,32},{80,48},{96,0},{112,16},{1... | collective-permute-start | bytes 294920 | tf_op jit(solution)/shard_map/ppermute | solution.py:434
  166.2 6.4 %collective-permute-start.27 = (f32[1,96,256]{2,1,0:T(8,128)S(1)}, f32[1,96,256]{2,1,0:T(8,128)S(1)}, u32[]{:S(2)}, u32[]{:S(2)}) collective-permute-start(f32[1,96,256]{2,1,0:T(8,128)S(1)} %get-tuple-element.69), channel_id=1, source_target_pairs={{0,112},{16,96},{32,80},{48,64},{64,48},{80,32},{96,16},{112,0},{1... | collective-permute-start | bytes 294920 | tf_op jit(solution)/shard_map/ppermute | solution.py:434
  172.6 7.7 %copy-start.1 = (f32[8,96,256]{2,1,0:T(8,128)}, f32[8,96,256]{2,1,0:T(8,128)S(1)}, u32[]{:S(2)}) copy-start(f32[8,96,256]{2,1,0:T(8,128)S(1)} %constant_dynamic-update-slice_fusion) | copy-start | bytes 2359300

commit v6 on v5

--- a/solution.py
+++ b/solution.py
@@ -20,6 +20,7 @@
 ROW_CUT = HEIGHT // NC
 COL_CUT = HEIGHT // NR
 TAG = 8
+ORDER = (4, 5, 6, 7, 2, 3, 1)
 BOTH = ("row", "col")
 F32 = jnp.float32
 BF16 = jnp.bfloat16
@@ -329,7 +330,7 @@
         m = {}
         for t in range(8):
             root = lax.rsqrt(e[t][t])
-            inv = 1.0 / e[t][t]
+            inv = root * root
             final = jnp.where(sub == t, rows[t] * root, final)
             scaled.append(rows[t] * inv)
             for r in range(t + 1, 8):
@@ -429,10 +430,10 @@
 
 
 def swap_rows(value):
-    got = [value[0]]
-    for k in range(1, NR):
-        got.append(lax.ppermute(value[k], "row", [(i, i ^ k) for i in range(NR)]))
-    return got
+    got = {0: value[0]}
+    for k in ORDER:
+        got[k] = lax.ppermute(value[k], "row", [(i, i ^ k) for i in range(NR)])
+    return [got[k] for k in range(NR)]
 
 
 def level(positions, modulus, self_weight, omega, psi, blocks):

time: 182 us -> 182 us (level)
  no operation moved by 1% of the time
where the time goes in v6:
time: 182 us; the launch traced here: 180 us
  starting transfers between devices  79.3 us (44%)
  waiting for transfers between devices  46.5 us (26%)
  Pallas kernels  25 us (14%)
  local copies, waits for them, and re-layouts  23.8 us (13%)
  other arithmetic  4.38 us (2%)
    ppermute x21, waiting for transfers between devices, swap_rows(): got[k] = lax.ppermute(value[k], 'row', [(i, i ^ k) for i in range(NR)])  38.9 us
    ppermute x21, starting transfers between devices, swap_rows(): got[k] = lax.ppermute(value[k], 'row', [(i, i ^ k) for i in range(NR)])  34.8 us
    all_to_all x3, starting transfers between devices, trade(): return lax.all_to_all(value, axis, split_axis=0, concat_axis=0, tiled=True)  21.6 us
    pallas_call x2, Pallas kernels, pair_terms(): pl.pallas_call(functools.partial(pair_kernel, cut=cut, turned=turned), ou...  17.8 us
    pallas_call x1, local copies, waits for them, and re-layouts, bases(): pl.pallas_call(basis_kernel, out_shape=(shape,) + (shape_c,) * NR, in_spe...  16.2 us
    ppermute x2, starting transfers between devices, level(): self_rows.append(lax.ppermute(part, BOTH, along))  7.23 us
    all_to_all x3, waiting for transfers between devices, trade(): return lax.all_to_all(value, axis, split_axis=0, concat_axis=0, tiled=True)  6.84 us
    ppermute x2, starting transfers between devices, level(): part = lax.ppermute(part, BOTH, inside)  6.81 us
  transfers between devices with their start and end apart: 31, of which 12 were waited for; matrix products, arithmetic and copies ran while one was open for 4% of the time, Pallas kernels for 8%

profile of v6, /device:TPU:0, one launch (start us, length us, event | category | flops | bytes accessed | tf_op | source)
XLA Modules:
  0.0 180.0 jit_solution(5402415322508487358)
XLA Ops:
  0.6 0.7 copy.14
  2.0 4.0 %collective-permute-start = (f32[4,8,128]{2,1,0:T(8,128)S(1)}, f32[4,8,128]{2,1,0:T(8,128)S(1)}, u32[]{:S(2)}, u32[]{:S(2)}) collective-permute-start(f32[4,8,128]{2,1,0:T(8,128)S(1)} %pad_maximum_fusion.own_pts), channel_id=1, source_target_pairs={{64,0},{65,1},{81,2},{80,3},{96,4},{97,5},{113,6},{112,7},{0,8},{1... | collective-permute-start | bytes 49160 | tf_op jit(solution)/shard_map/ppermute | solution.py:445
  6.0 4.1 %collective-permute-start.1 = (f32[4,8,128]{2,1,0:T(8,128)S(1)}, f32[4,8,128]{2,1,0:T(8,128)S(1)}, u32[]{:S(2)}, u32[]{:S(2)}) collective-permute-start(f32[4,8,128]{2,1,0:T(8,128)S(1)} %pad_maximum_fusion.own_pts), channel_id=1, source_target_pairs={{65,0},{64,1},{80,2},{81,3},{97,4},{96,5},{112,6},{113,7},{1,8},{0... | collective-permute-start | bytes 49160 | tf_op jit(solution)/shard_map/ppermute | solution.py:446
  10.2 1.3 pad_add_fusion
  11.5 0.7 collective-permute-done.1.far_pts
  12.8 9.9 %pair_rows.1 = f32[16,104,256]{2,1,0:T(8,128)} custom-call(s32[3,2]{1,0:T(4,128)} %get-tuple-element.75.meta, f32[4,8,128]{2,1,0:T(8,128)} %copy-done.7, f32[4,8,128]{2,1,0:T(8,128)} %copy-done.8, f32[4,8,128]{2,1,0:T(8,128)} %copy-done.9, f32[8,768,256]{2,1,0:T(8,128)} %src.2), custom_call_target="tpu_custom_call" | custom-call | flops 2000000000 | bytes 4000000 | tf_op jit(solution)/shard_map/pair_rows/pallas_call | solution.py:192
  22.8 5.9 %all-to-all-start = ((f32[16,104,256]{2,1,0:T(8,128)}), f32[16,104,256]{2,1,0:T(8,128)S(1)}, u32[]{:S(2)}, u32[]{:S(2)}) async-start(f32[16,104,256]{2,1,0:T(8,128)} %pair_rows.1), calls=%async_computation | async-start | bytes 3407872 | tf_op jit(solution)/shard_map/all_to_all | solution.py:429
  28.6 7.9 %pair_cols.1 = (f32[1,200,256]{2,1,0:T(8,128)}, f32[1,200,256]{2,1,0:T(8,128)}, f32[1,200,256]{2,1,0:T(8,128)}, f32[1,200,256]{2,1,0:T(8,128)}, f32[1,200,256]{2...) custom-call(s32[3,2]{1,0:T(4,128)} %get-tuple-element.74.meta, ...), custom_call_target="tpu_custom_call" | custom-call | flops 2000000000 | bytes 4000000 | tf_op jit(solution)/shard_map/pair_cols/pallas_call | solution.py:192
  36.7 1.2 dynamic-slice_bitcast_fusion
  37.9 0.7 collective-permute-start.6
  38.6 0.7 dynamic-slice_reduce_fusion
  39.4 7.4 %collective-permute-start.11 = (f32[1,200,256]{2,1,0:T(8,128)}, f32[1,200,256]{2,1,0:T(8,128)S(1)}, u32[]{:S(2)}, u32[]{:S(2)}) collective-permute-start(f32[1,200,256]{2,1,0:T(8,128)} %get-tuple-element.32), channel_id=1, source_target_pairs={{0,80},{16,64},{32,112},{48,96},{64,16},{80,0},{96,48},{112,32},{1... | collective-permute-start | bytes 614408 | tf_op jit(solution)/shard_map/ppermute | solution.py:435
  46.8 4.4 %collective-permute-start.12 = (f32[1,200,256]{2,1,0:T(8,128)}, f32[1,200,256]{2,1,0:T(8,128)S(1)}, u32[]{:S(2)}, u32[]{:S(2)}) collective-permute-start(f32[1,200,256]{2,1,0:T(8,128)} %get-tuple-element.33), channel_id=1, source_target_pairs={{0,96},{16,112},{32,64},{48,80},{64,32},{80,48},{96,0},{112,16},{1... | collective-permute-start | bytes 614408 | tf_op jit(solution)/shard_map/ppermute | solution.py:435
  51.3 2.2 %bitcast_multiply_fusion = (f32[384,256]{1,0:T(8,128)}, f32[384,256]{1,0:T(8,128)}) fusion(f32[8,768,256]{2,1,0:T(8,128)} %src.2, s32[]{:T(128)S(6)} %select_n.91, f32[384]{0:T(512)S(1)} %get-tuple-element.70, f32[384]{0:T(512)S(1)} %get-tuple-element.71, s32[]{:T(128)S(6)} %select_n.90), kind=kLoop, calls=%fused_computation.1 | loop fusion | flops 196608 | bytes 1575944 | tf_op jit(solution)/shard_map/mul | solution.py:457
  53.4 4.5 %collective-permute-start.2 = (f32[384,256]{1,0:T(8,128)}, f32[384,256]{1,0:T(8,128)}, u32[]{:S(2)}, u32[]{:S(2)}) collective-permute-start(f32[384,256]{1,0:T(8,128)} %get-tuple-element.73), channel_id=1, source_target_pairs={{0,0},{16,17},{64,66},{80,83},{32,36},{48,53},{96,102},{112,119},{... | collective-permute-start | bytes 1179656 | tf_op jit(solution)/shard_map/ppermute | solution.py:458
  57.9 11.9 %collective-permute-done.12.refs_6_ = f32[1,200,256]{2,1,0:T(8,128)S(1)} collective-permute-done((f32[1,200,256]{2,1,0:T(8,128)}, f32[1,200,256]{2,1,0:T(8,128)S(1)}, u32[]{:S(2)}, u32[]{:S(2)}) %collective-permute-start.12) | collective-permute-done | bytes 204832 | tf_op jit(solution)/shard_map/ppermute | solution.py:435
  70.4 2.3 %collective-permute-start.4 = (f32[384,256]{1,0:T(8,128)}, f32[384,256]{1,0:T(8,128)}, u32[]{:S(2)}, u32[]{:S(2)}) collective-permute-start(f32[384,256]{1,0:T(8,128)} %get-tuple-element.72), channel_id=1, source_target_pairs={{64,64},{80,81},{0,2},{16,19},{96,100},{112,117},{32,38},{48,55},{... | collective-permute-start | bytes 1179656 | tf_op jit(solution)/shard_map/ppermute | solution.py:458
  72.9 0.9 copy.11.ids
  74.0 3.2 %add_rows.1 = f32[16,48,256]{2,1,0:T(8,128)} custom-call(s32[16,2]{1,0:T(8,128)} %copy.11.ids, f32[16,104,256]{2,1,0:T(8,128)} %copy-done), custom_call_target="tpu_custom_call" | custom-call | flops 1000000 | bytes 3000000 | tf_op jit(solution)/shard_map/add_rows/pallas_call | solution.py:239
  77.1 10.5 %all-to-all-start.1 = ((f32[16,48,256]{2,1,0:T(8,128)}), f32[16,48,256]{2,1,0:T(8,128)S(1)}, u32[]{:S(2)}, u32[]{:S(2)}) async-start(f32[16,48,256]{2,1,0:T(8,128)} %add_rows.1), calls=%async_computation.1 | async-start | bytes 1572864 | tf_op jit(solution)/shard_map/all_to_all | solution.py:429
  87.7 1.4 collective-permute-start.8
  89.0 2.6 %collective-permute-start.9 = (f32[1,200,256]{2,1,0:T(8,128)}, f32[1,200,256]{2,1,0:T(8,128)S(1)}, u32[]{:S(2)}, u32[]{:S(2)}) collective-permute-start(f32[1,200,256]{2,1,0:T(8,128)} %get-tuple-element.30), channel_id=1, source_target_pairs={{0,48},{16,32},{32,16},{48,0},{64,112},{80,96},{96,80},{112,64},{1... | collective-permute-start | bytes 614408 | tf_op jit(solution)/shard_map/ppermute | solution.py:435
  91.6 2.8 %collective-permute-done.8.refs_2_ = f32[1,200,256]{2,1,0:T(8,128)S(1)} collective-permute-done((f32[1,200,256]{2,1,0:T(8,128)}, f32[1,200,256]{2,1,0:T(8,128)S(1)}, u32[]{:S(2)}, u32[]{:S(2)}) %collective-permute-start.8) | collective-permute-done | bytes 204832 | tf_op jit(solution)/shard_map/ppermute | solution.py:435
  94.4 5.9 %collective-permute-done.9.refs_3_ = f32[1,200,256]{2,1,0:T(8,128)S(1)} collective-permute-done((f32[1,200,256]{2,1,0:T(8,128)}, f32[1,200,256]{2,1,0:T(8,128)S(1)}, u32[]{:S(2)}, u32[]{:S(2)}) %collective-permute-start.9) | collective-permute-done | bytes 204832 | tf_op jit(solution)/shard_map/ppermute | solution.py:435
  101.0 4.0 %add_arrived.1 = (f32[1,96,256]{2,1,0:T(8,128)}, f32[1,96,256]{2,1,0:T(8,128)}, f32[1,96,256]{2,1,0:T(8,128)}, f32[1,96,256]{2,1,0:T(8,128)}, f32[1,96,256]{2,1,...) custom-call(s32[1]{0:T(128)} %bitcast.turn, ...), custom_call_target="tpu_custom_call" | custom-call | flops 1000000 | bytes 3000000 | tf_op jit(solution)/shard_map/add_arrived/pallas_call | solution.py:286
  105.1 1.4 collective-permute-start.15
  106.5 4.5 %collective-permute-start.3 = (f32[384,256]{1,0:T(8,128)}, f32[384,256]{1,0:T(8,128)}, u32[]{:S(2)}, u32[]{:S(2)}) collective-permute-start(f32[384,256]{1,0:T(8,128)} %collective-permute-done.2), channel_id=1, source_target_pairs={{0,0},{17,1},{66,2},{83,3},{36,4},{53,5},{102,6},{119,7},{8,8},{25... | collective-permute-start | bytes 1179656 | tf_op jit(solution)/shard_map/ppermute | solution.py:459
  111.0 2.8 %collective-permute-start.5 = (f32[384,256]{1,0:T(8,128)}, f32[384,256]{1,0:T(8,128)}, u32[]{:S(2)}, u32[]{:S(2)}) collective-permute-start(f32[384,256]{1,0:T(8,128)} %collective-permute-done.4), channel_id=1, source_target_pairs={{64,0},{81,1},{2,2},{19,3},{100,4},{117,5},{38,6},{55,7},{72,8},{8... | collective-permute-start | bytes 1179656 | tf_op jit(solution)/shard_map/ppermute | solution.py:459
  114.2 3.1 %collective-permute-start.17 = (f32[1,96,256]{2,1,0:T(8,128)}, f32[1,96,256]{2,1,0:T(8,128)S(1)}, u32[]{:S(2)}, u32[]{:S(2)}) collective-permute-start(f32[1,96,256]{2,1,0:T(8,128)} %get-tuple-element.39), channel_id=1, source_target_pairs={{0,64},{16,80},{32,96},{48,112},{64,0},{80,16},{96,32},{112,48},{1... | collective-permute-start | bytes 294920 | tf_op jit(solution)/shard_map/ppermute | solution.py:435
  117.3 0.8 fusion
  118.1 7.6 %collective-permute-done.16 = f32[1,96,256]{2,1,0:T(8,128)S(1)} collective-permute-done((f32[1,96,256]{2,1,0:T(8,128)}, f32[1,96,256]{2,1,0:T(8,128)S(1)}, u32[]{:S(2)}, u32[]{:S(2)}) %collective-permute-start.16) | collective-permute-done | bytes 98336 | tf_op jit(solution)/shard_map/ppermute | solution.py:435
  125.6 4.1 %collective-permute-start.18 = (f32[1,96,256]{2,1,0:T(8,128)}, f32[1,96,256]{2,1,0:T(8,128)S(1)}, u32[]{:S(2)}, u32[]{:S(2)}) collective-permute-start(f32[1,96,256]{2,1,0:T(8,128)} %get-tuple-element.40), channel_id=1, source_target_pairs={{0,80},{16,64},{32,112},{48,96},{64,16},{80,0},{96,48},{112,32},{1... | collective-permute-start | bytes 294920 | tf_op jit(solution)/shard_map/ppermute | solution.py:435
  129.9 1.0 collective-permute-start.19
  130.9 0.9 collective-permute-start.20
  132.0 0.8 collective-permute-done.18
  132.8 3.8 %collective-permute-done.19 = f32[1,96,256]{2,1,0:T(8,128)S(1)} collective-permute-done((f32[1,96,256]{2,1,0:T(8,128)}, f32[1,96,256]{2,1,0:T(8,128)S(1)}, u32[]{:S(2)}, u32[]{:S(2)}) %collective-permute-start.19) | collective-permute-done | bytes 98336 | tf_op jit(solution)/shard_map/ppermute | solution.py:435
  136.6 0.8 collective-permute-done.20
  137.5 16.2 %bases.1 = (f32[8,96,256]{2,1,0:T(8,128)S(1)}, f32[768,256]{1,0:T(8,128)}, f32[1,96,256]{2,1,0:T(8,128)S(1)}, f32[1,96,256]{2,1,0:T(8,128)S(1)}, f32[1,96,256]{2...) fusion(f32[8,96,256]{2,1,0:T(8,128)S(1)} %broadcast_in_dim.12, ...), kind=kCustom, calls=%fused_computation.13 | custom fusion | bytes 4718600 | tf_op jit(solution)/shard_map/bases/pallas_call | solution.py:408
  154.2 1.4 collective-permute-start.23
  155.6 1.5 collective-permute-start.24
  157.1 2.1 %collective-permute-start.25 = (f32[1,96,256]{2,1,0:T(8,128)S(1)}, f32[1,96,256]{2,1,0:T(8,128)S(1)}, u32[]{:S(2)}, u32[]{:S(2)}) collective-permute-start(f32[1,96,256]{2,1,0:T(8,128)S(1)} %get-tuple-element.65), channel_id=1, source_target_pairs={{0,80},{16,64},{32,112},{48,96},{64,16},{80,0},{96,48},{112,32},{1... | collective-permute-start | bytes 294920 | tf_op jit(solution)/shard_map/ppermute | solution.py:435
  159.2 5.2 %all-to-all-start.2 = ((f32[16,48,256]{2,1,0:T(8,128)}), f32[16,48,256]{2,1,0:T(8,128)S(1)}, u32[]{:S(2)}, u32[]{:S(2)}) async-start(f32[16,48,256]{2,1,0:T(8,128)} %bitcast.11), calls=%async_computation.2 | async-start | bytes 1572864 | tf_op jit(solution)/shard_map/all_to_all | solution.py:429
  164.5 1.3 collective-permute-start.26
  165.9 1.1 collective-permute-start.27
  167.1 3.6 %collective-permute-done.26 = f32[1,96,256]{2,1,0:T(8,128)S(1)} collective-permute-done((f32[1,96,256]{2,1,0:T(8,128)S(1)}, f32[1,96,256]{2,1,0:T(8,128)S(1)}, u32[]{:S(2)}, u32[]{:S(2)}) %collective-permute-start.26) | collective-permute-done | bytes 98336 | tf_op jit(solution)/shard_map/ppermute | solution.py:435
  170.7 1.6 collective-permute-done.27
  172.3 6.8 %all-to-all-done.2 = f32[16,48,256]{2,1,0:T(8,128)S(1)} async-done(((f32[16,48,256]{2,1,0:T(8,128)}), f32[16,48,256]{2,1,0:T(8,128)S(1)}, u32[]{:S(2)}, u32[]{:S(2)}) %all-to-all-start.2) | async-done | bytes 786464 | tf_op jit(solution)/shard_map/all_to_all | solution.py:429
  179.1 0.9 copy.24
  (69 shorter events, 4.9 us)
Async XLA Ops:
  2.0 10.2 %copy-start.7 = (f32[4,8,128]{2,1,0:T(8,128)}, f32[4,8,128]{2,1,0:T(8,128)S(1)}, u32[]{:S(2)}) copy-start(f32[4,8,128]{2,1,0:T(8,128)S(1)} %pad_maximum_fusion.own_pts) | copy-start | bytes 49156
  2.0 9.5 %collective-permute-start = (f32[4,8,128]{2,1,0:T(8,128)S(1)}, f32[4,8,128]{2,1,0:T(8,128)S(1)}, u32[]{:S(2)}, u32[]{:S(2)}) collective-permute-start(f32[4,8,128]{2,1,0:T(8,128)S(1)} %pad_maximum_fusion.own_pts), channel_id=1, source_target_pairs={{64,0},{65,1},{81,2},{80,3},{96,4},{97,5},{113,6},{112,7},{0,8},{1... | collective-permute-start | bytes 49160 | tf_op jit(solution)/shard_map/ppermute | solution.py:445
  6.0 6.2 %collective-permute-start.1 = (f32[4,8,128]{2,1,0:T(8,128)S(1)}, f32[4,8,128]{2,1,0:T(8,128)S(1)}, u32[]{:S(2)}, u32[]{:S(2)}) collective-permute-start(f32[4,8,128]{2,1,0:T(8,128)S(1)} %pad_maximum_fusion.own_pts), channel_id=1, source_target_pairs={{65,0},{64,1},{80,2},{81,3},{97,4},{96,5},{112,6},{113,7},{1,8},{0... | collective-permute-start | bytes 49160 | tf_op jit(solution)/shard_map/ppermute | solution.py:446
  11.5 0.7 copy-start.8
  12.2 0.6 copy-start.9
  22.8 50.0 %all-to-all-start = ((f32[16,104,256]{2,1,0:T(8,128)}), f32[16,104,256]{2,1,0:T(8,128)S(1)}, u32[]{:S(2)}, u32[]{:S(2)}) async-start(f32[16,104,256]{2,1,0:T(8,128)} %pair_rows.1), calls=%async_computation | async-start | bytes 3407872 | tf_op jit(solution)/shard_map/all_to_all | solution.py:429
  36.5 14.6 %collective-permute-start.10 = (f32[1,200,256]{2,1,0:T(8,128)}, f32[1,200,256]{2,1,0:T(8,128)S(1)}, u32[]{:S(2)}, u32[]{:S(2)}) collective-permute-start(f32[1,200,256]{2,1,0:T(8,128)} %get-tuple-element.31), channel_id=1, source_target_pairs={{0,64},{16,80},{32,96},{48,112},{64,0},{80,16},{96,32},{112,48},{1... | collective-permute-start | bytes 614408 | tf_op jit(solution)/shard_map/ppermute | solution.py:435
  37.9 93.0 %collective-permute-start.6 = (f32[768,256]{1,0:T(8,128)S(1)}, f32[768,256]{1,0:T(8,128)S(1)}, u32[]{:S(2)}, u32[]{:S(2)}) collective-permute-start(f32[768,256]{1,0:T(8,128)S(1)} %dynamic-slice_bitcast_fusion), channel_id=1, source_target_pairs={{0,0},{1,1},{16,2},{17,3},{36,4},{37,5},{52,6},{53,7},{72,8},{73,9... | collective-permute-start | bytes 2359304 | tf_op jit(solution)/shard_map/ppermute | solution.py:461
  39.4 14.0 %collective-permute-start.11 = (f32[1,200,256]{2,1,0:T(8,128)}, f32[1,200,256]{2,1,0:T(8,128)S(1)}, u32[]{:S(2)}, u32[]{:S(2)}) collective-permute-start(f32[1,200,256]{2,1,0:T(8,128)} %get-tuple-element.32), channel_id=1, source_target_pairs={{0,80},{16,64},{32,112},{48,96},{64,16},{80,0},{96,48},{112,32},{1... | collective-permute-start | bytes 614408 | tf_op jit(solution)/shard_map/ppermute | solution.py:435
  46.8 23.0 %collective-permute-start.12 = (f32[1,200,256]{2,1,0:T(8,128)}, f32[1,200,256]{2,1,0:T(8,128)S(1)}, u32[]{:S(2)}, u32[]{:S(2)}) collective-permute-start(f32[1,200,256]{2,1,0:T(8,128)} %get-tuple-element.33), channel_id=1, source_target_pairs={{0,96},{16,112},{32,64},{48,80},{64,32},{80,48},{96,0},{112,16},{1... | collective-permute-start | bytes 614408 | tf_op jit(solution)/shard_map/ppermute | solution.py:435
  51.1 36.5 %collective-permute-start.13 = (f32[1,200,256]{2,1,0:T(8,128)}, f32[1,200,256]{2,1,0:T(8,128)}, u32[]{:S(2)}, u32[]{:S(2)}) collective-permute-start(f32[1,200,256]{2,1,0:T(8,128)} %get-tuple-element.34), channel_id=1, source_target_pairs={{0,112},{16,96},{32,80},{48,64},{64,48},{80,32},{96,16},{112,0},{1... | collective-permute-start | bytes 614408 | tf_op jit(solution)/shard_map/ppermute | solution.py:435
  51.1 49.2 %copy-start.2 = (f32[1,200,256]{2,1,0:T(8,128)}, f32[1,200,256]{2,1,0:T(8,128)S(1)}, u32[]{:S(2)}) copy-start(f32[1,200,256]{2,1,0:T(8,128)S(1)} %collective-permute-done.10.refs_4_) | copy-start | bytes 614404
  51.1 37.9 %collective-permute-start.7 = (f32[1,200,256]{2,1,0:T(8,128)}, f32[1,200,256]{2,1,0:T(8,128)}, u32[]{:S(2)}, u32[]{:S(2)}) collective-permute-start(f32[1,200,256]{2,1,0:T(8,128)} %get-tuple-element.28), channel_id=1, source_target_pairs={{0,16},{16,0},{32,48},{48,32},{64,80},{80,64},{96,112},{112,96},{1... | collective-permute-start | bytes 614408 | tf_op jit(solution)/shard_map/ppermute | solution.py:435
  53.4 16.4 %copy-start.3 = (f32[1,200,256]{2,1,0:T(8,128)}, f32[1,200,256]{2,1,0:T(8,128)S(1)}, u32[]{:S(2)}) copy-start(f32[1,200,256]{2,1,0:T(8,128)S(1)} %collective-permute-done.11.refs_5_) | copy-start | bytes 614404
  53.4 53.1 %collective-permute-start.2 = (f32[384,256]{1,0:T(8,128)}, f32[384,256]{1,0:T(8,128)}, u32[]{:S(2)}, u32[]{:S(2)}) collective-permute-start(f32[384,256]{1,0:T(8,128)} %get-tuple-element.73), channel_id=1, source_target_pairs={{0,0},{16,17},{64,66},{80,83},{32,36},{48,53},{96,102},{112,119},{... | collective-permute-start | bytes 1179656 | tf_op jit(solution)/shard_map/ppermute | solution.py:458
  69.8 0.7 copy-start.4
  70.4 40.5 %collective-permute-start.4 = (f32[384,256]{1,0:T(8,128)}, f32[384,256]{1,0:T(8,128)}, u32[]{:S(2)}, u32[]{:S(2)}) collective-permute-start(f32[384,256]{1,0:T(8,128)} %get-tuple-element.72), channel_id=1, source_target_pairs={{64,64},{80,81},{0,2},{16,19},{96,100},{112,117},{32,38},{48,55},{... | collective-permute-start | bytes 1179656 | tf_op jit(solution)/shard_map/ppermute | solution.py:458
  72.8 1.2 copy-start
  77.1 60.3 %all-to-all-start.1 = ((f32[16,48,256]{2,1,0:T(8,128)}), f32[16,48,256]{2,1,0:T(8,128)S(1)}, u32[]{:S(2)}, u32[]{:S(2)}) async-start(f32[16,48,256]{2,1,0:T(8,128)} %add_rows.1), calls=%async_computation.1 | async-start | bytes 1572864 | tf_op jit(solution)/shard_map/all_to_all | solution.py:429
  87.7 6.8 %collective-permute-start.8 = (f32[1,200,256]{2,1,0:T(8,128)}, f32[1,200,256]{2,1,0:T(8,128)S(1)}, u32[]{:S(2)}, u32[]{:S(2)}) collective-permute-start(f32[1,200,256]{2,1,0:T(8,128)} %get-tuple-element.29), channel_id=1, source_target_pairs={{0,32},{16,48},{32,0},{48,16},{64,96},{80,112},{96,64},{112,80},{1... | collective-permute-start | bytes 614408 | tf_op jit(solution)/shard_map/ppermute | solution.py:435
  89.0 11.3 %collective-permute-start.9 = (f32[1,200,256]{2,1,0:T(8,128)}, f32[1,200,256]{2,1,0:T(8,128)S(1)}, u32[]{:S(2)}, u32[]{:S(2)}) collective-permute-start(f32[1,200,256]{2,1,0:T(8,128)} %get-tuple-element.30), channel_id=1, source_target_pairs={{0,48},{16,32},{32,16},{48,0},{64,112},{80,96},{96,80},{112,64},{1... | collective-permute-start | bytes 614408 | tf_op jit(solution)/shard_map/ppermute | solution.py:435
  94.4 5.9 %copy-start.5 = (f32[1,200,256]{2,1,0:T(8,128)}, f32[1,200,256]{2,1,0:T(8,128)S(1)}, u32[]{:S(2)}) copy-start(f32[1,200,256]{2,1,0:T(8,128)S(1)} %collective-permute-done.8.refs_2_) | copy-start | bytes 614404
  100.3 0.7 copy-start.6
  105.0 8.7 %collective-permute-start.14 = (f32[1,96,256]{2,1,0:T(8,128)}, f32[1,96,256]{2,1,0:T(8,128)S(1)}, u32[]{:S(2)}, u32[]{:S(2)}) collective-permute-start(f32[1,96,256]{2,1,0:T(8,128)} %get-tuple-element.36), channel_id=1, source_target_pairs={{0,16},{16,0},{32,48},{48,32},{64,80},{80,64},{96,112},{112,96},{1... | collective-permute-start | bytes 294920 | tf_op jit(solution)/shard_map/ppermute | solution.py:435
  105.1 9.1 %collective-permute-start.15 = (f32[1,96,256]{2,1,0:T(8,128)}, f32[1,96,256]{2,1,0:T(8,128)S(1)}, u32[]{:S(2)}, u32[]{:S(2)}) collective-permute-start(f32[1,96,256]{2,1,0:T(8,128)} %get-tuple-element.37), channel_id=1, source_target_pairs={{0,32},{16,48},{32,0},{48,16},{64,96},{80,112},{96,64},{112,80},{1... | collective-permute-start | bytes 294920 | tf_op jit(solution)/shard_map/ppermute | solution.py:435
  106.5 30.9 %collective-permute-start.3 = (f32[384,256]{1,0:T(8,128)}, f32[384,256]{1,0:T(8,128)}, u32[]{:S(2)}, u32[]{:S(2)}) collective-permute-start(f32[384,256]{1,0:T(8,128)} %collective-permute-done.2), channel_id=1, source_target_pairs={{0,0},{17,1},{66,2},{83,3},{36,4},{53,5},{102,6},{119,7},{8,8},{25... | collective-permute-start | bytes 1179656 | tf_op jit(solution)/shard_map/ppermute | solution.py:459
  111.0 26.5 %collective-permute-start.5 = (f32[384,256]{1,0:T(8,128)}, f32[384,256]{1,0:T(8,128)}, u32[]{:S(2)}, u32[]{:S(2)}) collective-permute-start(f32[384,256]{1,0:T(8,128)} %collective-permute-done.4), channel_id=1, source_target_pairs={{64,0},{81,1},{2,2},{19,3},{100,4},{117,5},{38,6},{55,7},{72,8},{8... | collective-permute-start | bytes 1179656 | tf_op jit(solution)/shard_map/ppermute | solution.py:459
  113.7 11.9 %collective-permute-start.16 = (f32[1,96,256]{2,1,0:T(8,128)}, f32[1,96,256]{2,1,0:T(8,128)S(1)}, u32[]{:S(2)}, u32[]{:S(2)}) collective-permute-start(f32[1,96,256]{2,1,0:T(8,128)} %get-tuple-element.38), channel_id=1, source_target_pairs={{0,48},{16,32},{32,16},{48,0},{64,112},{80,96},{96,80},{112,64},{1... | collective-permute-start | bytes 294920 | tf_op jit(solution)/shard_map/ppermute | solution.py:435
  114.2 15.7 %collective-permute-start.17 = (f32[1,96,256]{2,1,0:T(8,128)}, f32[1,96,256]{2,1,0:T(8,128)S(1)}, u32[]{:S(2)}, u32[]{:S(2)}) collective-permute-start(f32[1,96,256]{2,1,0:T(8,128)} %get-tuple-element.39), channel_id=1, source_target_pairs={{0,64},{16,80},{32,96},{48,112},{64,0},{80,16},{96,32},{112,48},{1... | collective-permute-start | bytes 294920 | tf_op jit(solution)/shard_map/ppermute | solution.py:435
  125.6 11.8 %copy-start.10 = (f32[1,96,256]{2,1,0:T(8,128)}, f32[1,96,256]{2,1,0:T(8,128)S(1)}, u32[]{:S(2)}) copy-start(f32[1,96,256]{2,1,0:T(8,128)S(1)} %collective-permute-done.16) | copy-start | bytes 294916
  125.6 7.2 %collective-permute-start.18 = (f32[1,96,256]{2,1,0:T(8,128)}, f32[1,96,256]{2,1,0:T(8,128)S(1)}, u32[]{:S(2)}, u32[]{:S(2)}) collective-permute-start(f32[1,96,256]{2,1,0:T(8,128)} %get-tuple-element.40), channel_id=1, source_target_pairs={{0,80},{16,64},{32,112},{48,96},{64,16},{80,0},{96,48},{112,32},{1... | collective-permute-start | bytes 294920 | tf_op jit(solution)/shard_map/ppermute | solution.py:435
  129.9 1.0 copy-start.11
  129.9 6.7 %collective-permute-start.19 = (f32[1,96,256]{2,1,0:T(8,128)}, f32[1,96,256]{2,1,0:T(8,128)S(1)}, u32[]{:S(2)}, u32[]{:S(2)}) collective-permute-start(f32[1,96,256]{2,1,0:T(8,128)} %get-tuple-element.41), channel_id=1, source_target_pairs={{0,96},{16,112},{32,64},{48,80},{64,32},{80,48},{96,0},{112,16},{1... | collective-permute-start | bytes 294920 | tf_op jit(solution)/shard_map/ppermute | solution.py:435
  130.9 6.5 %collective-permute-start.20 = (f32[1,96,256]{2,1,0:T(8,128)}, f32[1,96,256]{2,1,0:T(8,128)S(1)}, u32[]{:S(2)}, u32[]{:S(2)}) collective-permute-start(f32[1,96,256]{2,1,0:T(8,128)} %get-tuple-element.42), channel_id=1, source_target_pairs={{0,112},{16,96},{32,80},{48,64},{64,48},{80,32},{96,16},{112,0},{1... | collective-permute-start | bytes 294920 | tf_op jit(solution)/shard_map/ppermute | solution.py:435
  132.8 4.6 %copy-start.12 = (f32[1,96,256]{2,1,0:T(8,128)}, f32[1,96,256]{2,1,0:T(8,128)S(1)}, u32[]{:S(2)}) copy-start(f32[1,96,256]{2,1,0:T(8,128)S(1)} %collective-permute-done.18) | copy-start | bytes 294916
  136.6 0.8 copy-start.13
  153.8 10.7 %collective-permute-start.21 = (f32[1,96,256]{2,1,0:T(8,128)S(1)}, f32[1,96,256]{2,1,0:T(8,128)S(1)}, u32[]{:S(2)}, u32[]{:S(2)}) collective-permute-start(f32[1,96,256]{2,1,0:T(8,128)S(1)} %get-tuple-element.57), channel_id=1, source_target_pairs={{0,16},{16,0},{32,48},{48,32},{64,80},{80,64},{96,112},{112,96},{1... | collective-permute-start | bytes 294920 | tf_op jit(solution)/shard_map/ppermute | solution.py:435
  154.2 11.6 %collective-permute-start.22 = (f32[1,96,256]{2,1,0:T(8,128)S(1)}, f32[1,96,256]{2,1,0:T(8,128)S(1)}, u32[]{:S(2)}, u32[]{:S(2)}) collective-permute-start(f32[1,96,256]{2,1,0:T(8,128)S(1)} %get-tuple-element.59), channel_id=1, source_target_pairs={{0,32},{16,48},{32,0},{48,16},{64,96},{80,112},{96,64},{112,80},{1... | collective-permute-start | bytes 294920 | tf_op jit(solution)/shard_map/ppermute | solution.py:435
  154.2 12.7 %collective-permute-start.23 = (f32[1,96,256]{2,1,0:T(8,128)S(1)}, f32[1,96,256]{2,1,0:T(8,128)S(1)}, u32[]{:S(2)}, u32[]{:S(2)}) collective-permute-start(f32[1,96,256]{2,1,0:T(8,128)S(1)} %get-tuple-element.61), channel_id=1, source_target_pairs={{0,48},{16,32},{32,16},{48,0},{64,112},{80,96},{96,80},{112,64},{1... | collective-permute-start | bytes 294920 | tf_op jit(solution)/shard_map/ppermute | solution.py:435
  155.6 11.4 %collective-permute-start.24 = (f32[1,96,256]{2,1,0:T(8,128)S(1)}, f32[1,96,256]{2,1,0:T(8,128)S(1)}, u32[]{:S(2)}, u32[]{:S(2)}) collective-permute-start(f32[1,96,256]{2,1,0:T(8,128)S(1)} %get-tuple-element.63), channel_id=1, source_target_pairs={{0,64},{16,80},{32,96},{48,112},{64,0},{80,16},{96,32},{112,48},{1... | collective-permute-start | bytes 294920 | tf_op jit(solution)/shard_map/ppermute | solution.py:435
  157.1 9.9 %collective-permute-start.25 = (f32[1,96,256]{2,1,0:T(8,128)S(1)}, f32[1,96,256]{2,1,0:T(8,128)S(1)}, u32[]{:S(2)}, u32[]{:S(2)}) collective-permute-start(f32[1,96,256]{2,1,0:T(8,128)S(1)} %get-tuple-element.65), channel_id=1, source_target_pairs={{0,80},{16,64},{32,112},{48,96},{64,16},{80,0},{96,48},{112,32},{1... | collective-permute-start | bytes 294920 | tf_op jit(solution)/shard_map/ppermute | solution.py:435
  159.2 19.9 %all-to-all-start.2 = ((f32[16,48,256]{2,1,0:T(8,128)}), f32[16,48,256]{2,1,0:T(8,128)S(1)}, u32[]{:S(2)}, u32[]{:S(2)}) async-start(f32[16,48,256]{2,1,0:T(8,128)} %bitcast.11), calls=%async_computation.2 | async-start | bytes 1572864 | tf_op jit(solution)/shard_map/all_to_all | solution.py:429
  164.5 6.2 %collective-permute-start.26 = (f32[1,96,256]{2,1,0:T(8,128)S(1)}, f32[1,96,256]{2,1,0:T(8,128)S(1)}, u32[]{:S(2)}, u32[]{:S(2)}) collective-permute-start(f32[1,96,256]{2,1,0:T(8,128)S(1)} %get-tuple-element.67), channel_id=1, source_target_pairs={{0,96},{16,112},{32,64},{48,80},{64,32},{80,48},{96,0},{112,16},{1... | collective-permute-start | bytes 294920 | tf_op jit(solution)/shard_map/ppermute | solution.py:435
  165.9 6.4 %collective-permute-start.27 = (f32[1,96,256]{2,1,0:T(8,128)S(1)}, f32[1,96,256]{2,1,0:T(8,128)S(1)}, u32[]{:S(2)}, u32[]{:S(2)}) collective-permute-start(f32[1,96,256]{2,1,0:T(8,128)S(1)} %get-tuple-element.69), channel_id=1, source_target_pairs={{0,112},{16,96},{32,80},{48,64},{64,48},{80,32},{96,16},{112,0},{1... | collective-permute-start | bytes 294920 | tf_op jit(solution)/shard_map/ppermute | solution.py:435
  172.3 7.7 %copy-start.1 = (f32[8,96,256]{2,1,0:T(8,128)}, f32[8,96,256]{2,1,0:T(8,128)S(1)}, u32[]{:S(2)}) copy-start(f32[8,96,256]{2,1,0:T(8,128)S(1)} %constant_dynamic-update-slice_fusion) | copy-start | bytes 2359300
